TPU v7x, 32 devices: a whole 2x2x4 slice. The times are simulated.
32 devices in a mesh: fsdp: 2 (over x), seq: 16 (over z, y, core).
Axes of the slice: x: 2, y: 2, z: 4, core: 2. Of those that a mesh axis runs over, the one named last changes fastest.
Arguments:
- tokens: bfloat16 [16384, 1152], P(('fsdp', 'seq')), may hold values from -16 to 16
- qkv_weight: bfloat16 [2, 1152, 3456], P(None, ('fsdp', 'seq')), may hold values from -0.1875 to 0.1875
- out_weight: bfloat16 [2, 1152, 1152], P(None, ('fsdp', 'seq')), may hold values from -1 to 1
- up_weight: bfloat16 [2, 1152, 4608], P(None, ('fsdp', 'seq')), may hold values from -0.1875 to 0.1875
- down_weight: bfloat16 [2, 4608, 1152], P(None, ('fsdp', 'seq')), may hold values from -0.09375 to 0.09375
- mod_weight: bfloat16 [2, 1152, 6912], P(None, ('fsdp', 'seq')), may hold values from -0.375 to 0.375
- qv_bias: bfloat16 [2, 2304], P(None, ('fsdp', 'seq')), may hold values from -3 to 3
- out_bias: bfloat16 [2, 1152], P(None, ('fsdp', 'seq')), may hold values from -3 to 3
- up_bias: bfloat16 [2, 4608], P(None, ('fsdp', 'seq')), may hold values from -3 to 3
- down_bias: bfloat16 [2, 1152], P(None, ('fsdp', 'seq')), may hold values from -3 to 3
- mod_bias: bfloat16 [2, 6912], P(None, ('fsdp', 'seq')), may hold values from -3 to 3
- row_items: int32 [16], P('seq'), may hold values from 1 to 4, as said below
- timesteps: int32 [16, 4], P('seq'), may hold values from 0 to 999
- head_mask: int32 [16, 2, 4, 16], P('seq'), may hold values 0 or 1
- channel_mask: int32 [16, 2, 4, 4608], P('seq'), may hold values 0 or 1
- token_keep: int32 [16384, 2], P(('fsdp', 'seq')), may hold values 0 or 1
- cotangent: float32 [16384, 1152], P(('fsdp', 'seq')), may hold values from -6 to 6
Outputs:
- output: bfloat16 [16384, 1152], P(('fsdp', 'seq'))
- grad_tokens: float32 [16384, 1152], P(('fsdp', 'seq'))
- grad_qkv_weight: float32 [2, 1152, 3456], P(None, ('fsdp', 'seq'))
- grad_out_weight: float32 [2, 1152, 1152], P(None, ('fsdp', 'seq'))
- grad_up_weight: float32 [2, 1152, 4608], P(None, ('fsdp', 'seq'))
- grad_down_weight: float32 [2, 4608, 1152], P(None, ('fsdp', 'seq'))
- grad_mod_weight: float32 [2, 1152, 6912], P(None, ('fsdp', 'seq'))
- grad_qv_bias: float32 [2, 2304], P(None, ('fsdp', 'seq'))
- grad_out_bias: float32 [2, 1152], P(None, ('fsdp', 'seq'))
- grad_up_bias: float32 [2, 4608], P(None, ('fsdp', 'seq'))
- grad_down_bias: float32 [2, 1152], P(None, ('fsdp', 'seq'))
- grad_mod_bias: float32 [2, 6912], P(None, ('fsdp', 'seq'))
Inputs may be any that keep to these rules, and one draw needn't show every extreme that they name: `row_items`: each row holds 1 or 4 items, exactly half of the rows each. A row of one item uses only the first slot of timesteps, head_mask and channel_mask.
All inputs are finite; a program needn't handle non-finite values. No bound on the sum of `head_mask` or of `channel_mask` or of `token_keep` on one device may be relied on, other than what follows from the above.
Results may differ from a plain program's by a relative error of at most 0.018.
The roundings to bfloat16 on the way count: a program that leaves them out, or rounds other values in their place, can miss the bound.
Values may be sent and summed in bfloat16 or wider, within the bound.
No kernel may reach another device: no remote copies, remote signals or barrier semaphores. Data moves between devices by JAX's collectives and lax.ppermute only.
A program may use at most 448 MiB of HBM per device.

v0:
```python
import math

import jax
import jax.numpy as jnp
from jax import lax
from jax.sharding import PartitionSpec as P

highest = lax.Precision.HIGHEST


def swapped(block, axis, bit):
    count = lax.axis_size(axis)
    route = []
    for low in range(count):
        high = low | 1 << bit
        if high != low and high < count:
            route += [(low, high), (high, low)]
    return lax.ppermute(block, axis, route)


def embed_steps(step_values, model_width):
    half_width = model_width // 2
    frequency = jnp.exp(-math.log(10000.0) * jnp.arange(half_width, dtype=jnp.float32) / half_width)
    angles = step_values.astype(jnp.float32)[:, None] * frequency[None, :]
    return jnp.concatenate([jnp.cos(angles), jnp.sin(angles)], axis=1)


def modulate(values, shift_part, scale_part):
    centered = values - jnp.mean(values, axis=1, keepdims=True)
    spread = jnp.mean(centered * centered, axis=1, keepdims=True)
    return centered * lax.rsqrt(spread + 1e-06) * (1.0 + scale_part) + shift_part


def contract_rows(left_side, right_side):
    return lax.dot_general(
        left_side, right_side, (((0,), (0,)), ((), ())), preferred_element_type=jnp.float32
    )


def contract_cols(left_side, right_side):
    return lax.dot_general(
        left_side, right_side, (((1,), (1,)), ((), ())), preferred_element_type=jnp.float32
    )


def gelu_tanh(inner_value):
    return jax.nn.gelu(inner_value, approximate=True)


def body(
    tokens,
    qkv_weight,
    out_weight,
    up_weight,
    down_weight,
    mod_weight,
    qv_bias,
    out_bias,
    up_bias,
    down_bias,
    mod_bias,
    row_items,
    timesteps,
    head_mask,
    channel_mask,
    token_keep,
    cotangent,
):
    layer_count = qkv_weight.shape[0]
    model_width = out_weight.shape[2]
    head_count = head_mask.shape[3]
    head_size = model_width // head_count
    group_heads = math.gcd(head_count, 4)
    group_count = head_count // group_heads
    item_count = timesteps.shape[1]
    local_rows = tokens.shape[0]
    row_len = 2 * local_rows
    half_index = lax.axis_index("fsdp")
    flat_index = lax.axis_index(("fsdp", "seq"))
    lower_half = half_index == 0
    scale_factor = 1.0 / math.sqrt(head_size)
    shard_rows = mod_weight.shape[1]
    mod_cols = mod_bias.shape[1]
    items_here = row_items[0]
    query_pos = half_index * local_rows + jnp.arange(local_rows, dtype=jnp.int32)
    key_pos = jnp.arange(row_len, dtype=jnp.int32)
    query_item = query_pos * items_here // row_len
    key_item = key_pos * items_here // row_len
    same_item = query_item[:, None] == key_item[None, :]
    pick_item = (query_item[:, None] == jnp.arange(item_count, dtype=jnp.int32)[None, :]).astype(
        jnp.float32
    )
    every_step = lax.all_gather(timesteps, "seq", axis=0, tiled=True)
    cond_every = jax.nn.silu(embed_steps(every_step.reshape(-1), model_width)).astype(jnp.bfloat16)
    cond_cols = lax.dynamic_slice_in_dim(cond_every, flat_index * shard_rows, shard_rows, 1)
    cond_twice = jnp.concatenate([cond_cols, cond_cols], axis=0).astype(jnp.float32)

    def to_groups(matrix, count):
        return jnp.moveaxis(matrix.reshape(count, group_count, group_heads, head_size), 1, 0)

    def from_groups(grouped, count):
        return jnp.moveaxis(grouped, 0, 1).reshape(count, model_width)

    def group_scores(query_group, key_group):
        raw = (
            jnp.einsum("qhd,khd->hqk", query_group, key_group, preferred_element_type=jnp.float32)
            * scale_factor
        )
        return jnp.where(same_item[None], raw, -1e30)

    def attend_group(packed):
        query_group, key_group, value_group = packed
        scores = group_scores(query_group, key_group)
        largest = jnp.max(scores, axis=2, keepdims=True)
        log_total = largest + jnp.log(jnp.sum(jnp.exp(scores - largest), axis=2, keepdims=True))
        probs_low = jnp.exp(scores - log_total).astype(jnp.bfloat16)
        attended = jnp.einsum(
            "hqk,khd->qhd", probs_low, value_group, preferred_element_type=jnp.float32
        )
        return (attended, log_total)

    def attend_back(packed):
        query_group, key_group, value_group, mixed_group, log_total = packed
        probs_again = jnp.exp(group_scores(query_group, key_group) - log_total)
        grad_probs = jnp.einsum(
            "qhd,khd->hqk", mixed_group, value_group, preferred_element_type=jnp.float32
        )
        grad_value = jnp.einsum(
            "hqk,qhd->khd",
            probs_again.astype(jnp.bfloat16),
            mixed_group,
            preferred_element_type=jnp.float32,
        )
        grad_scores = (
            probs_again * (grad_probs - jnp.sum(probs_again * grad_probs, axis=2, keepdims=True))
        ).astype(jnp.bfloat16)
        grad_query = (
            jnp.einsum("hqk,khd->qhd", grad_scores, key_group, preferred_element_type=jnp.float32)
            * scale_factor
        )
        grad_key = (
            jnp.einsum("hqk,qhd->khd", grad_scores, query_group, preferred_element_type=jnp.float32)
            * scale_factor
        )
        return (grad_query, grad_key, grad_value)

    current = tokens.astype(jnp.float32)
    saved_layers = []
    kept_weights = []
    for layer in range(layer_count):
        full = (
            lax.all_gather(qkv_weight[layer], ("fsdp", "seq"), axis=0, tiled=True),
            lax.all_gather(out_weight[layer], ("fsdp", "seq"), axis=0, tiled=True),
            lax.all_gather(up_weight[layer], ("fsdp", "seq"), axis=0, tiled=True),
            lax.all_gather(down_weight[layer], ("fsdp", "seq"), axis=0, tiled=True),
            lax.all_gather(qv_bias[layer], ("fsdp", "seq"), axis=0, tiled=True),
            lax.all_gather(out_bias[layer], ("fsdp", "seq"), axis=0, tiled=True),
            lax.all_gather(up_bias[layer], ("fsdp", "seq"), axis=0, tiled=True),
            lax.all_gather(down_bias[layer], ("fsdp", "seq"), axis=0, tiled=True),
            lax.all_gather(mod_bias[layer], ("fsdp", "seq"), axis=0, tiled=True),
        )
        (
            full_qkv,
            full_out,
            full_up,
            full_down,
            full_pair_bias,
            full_out_bias,
            full_up_bias,
            full_down_bias,
            full_mod_bias,
        ) = full
        heads_on = head_mask[0, layer].astype(jnp.float32)
        channel_on = channel_mask[0, layer].astype(jnp.float32)
        forward_keep_tok = token_keep[:, layer].astype(jnp.float32)[:, None]
        partial_mod = jnp.dot(cond_cols, mod_weight[layer], preferred_element_type=jnp.float32)
        row_mod = lax.psum_scatter(partial_mod, "seq", scatter_dimension=0, tiled=True)
        modulation = lax.psum(row_mod, "fsdp") + full_mod_bias.astype(jnp.float32)
        forward_token_mod = jnp.dot(
            pick_item, modulation, precision=highest, preferred_element_type=jnp.float32
        )
        (
            forward_shift_one,
            forward_scale_one,
            forward_gate_one,
            forward_shift_two,
            forward_scale_two,
            forward_gate_two,
        ) = jnp.split(forward_token_mod, 6, axis=1)
        forward_head_on_tok = jnp.dot(
            pick_item, heads_on, precision=highest, preferred_element_type=jnp.float32
        )
        forward_channel_tok = jnp.dot(
            pick_item, channel_on, precision=highest, preferred_element_type=jnp.float32
        )
        forward_low_one = modulate(current, forward_shift_one, forward_scale_one).astype(
            jnp.bfloat16
        )
        bias_three = jnp.concatenate(
            [
                full_pair_bias[:model_width],
                jnp.zeros((model_width,), jnp.bfloat16),
                full_pair_bias[model_width:],
            ]
        ).astype(jnp.float32)
        qkv_low = (
            jnp.dot(forward_low_one, full_qkv, preferred_element_type=jnp.float32) + bias_three
        ).astype(jnp.bfloat16)
        queries = qkv_low[:, :model_width]
        keys_here = qkv_low[:, model_width : 2 * model_width]
        values_here = qkv_low[:, 2 * model_width :]
        other_keys, other_values = swapped((keys_here, values_here), "fsdp", 0)
        keys_row = jnp.concatenate(
            [
                jnp.where(lower_half, keys_here, other_keys),
                jnp.where(lower_half, other_keys, keys_here),
            ],
            axis=0,
        )
        values_row = jnp.concatenate(
            [
                jnp.where(lower_half, values_here, other_values),
                jnp.where(lower_half, other_values, values_here),
            ],
            axis=0,
        )
        forward_query_groups = to_groups(queries, local_rows)
        forward_key_groups = to_groups(keys_row, row_len)
        forward_value_groups = to_groups(values_row, row_len)
        attended_groups, forward_log_totals = lax.map(
            attend_group, (forward_query_groups, forward_key_groups, forward_value_groups)
        )
        forward_attended = from_groups(attended_groups, local_rows).reshape(
            local_rows, head_count, head_size
        )
        forward_mixed_low = (
            (forward_attended * forward_head_on_tok[:, :, None])
            .reshape(local_rows, model_width)
            .astype(jnp.bfloat16)
        )
        forward_branch_one = jnp.dot(
            forward_mixed_low, full_out, preferred_element_type=jnp.float32
        ) + full_out_bias.astype(jnp.float32)
        forward_after_attn = current + forward_gate_one * forward_branch_one
        forward_low_two = modulate(forward_after_attn, forward_shift_two, forward_scale_two).astype(
            jnp.bfloat16
        )
        forward_hidden_pre = jnp.dot(
            forward_low_two, full_up, preferred_element_type=jnp.float32
        ) + full_up_bias.astype(jnp.float32)
        forward_hidden_low = (gelu_tanh(forward_hidden_pre) * forward_channel_tok).astype(
            jnp.bfloat16
        )
        forward_branch_two = jnp.dot(
            forward_hidden_low, full_down, preferred_element_type=jnp.float32
        ) + full_down_bias.astype(jnp.float32)
        forward_result = (
            forward_after_attn + forward_keep_tok * forward_gate_two * forward_branch_two
        )
        forward_saved = (
            current,
            forward_token_mod,
            forward_head_on_tok,
            forward_channel_tok,
            forward_keep_tok,
            forward_low_one,
            forward_query_groups,
            forward_key_groups,
            forward_value_groups,
            forward_log_totals,
            forward_mixed_low,
            forward_branch_one,
            forward_after_attn,
            forward_low_two,
            forward_hidden_pre,
            forward_hidden_low,
            forward_branch_two,
        )
        current = forward_result
        saved_layers.append(forward_saved)
        kept_weights.append((full[0], full[1], full[2], full[3]))
    grad_current = cotangent
    layer_totals = [None] * layer_count
    for layer in reversed(range(layer_count)):
        back_weights = kept_weights[layer]
        back_qkv, back_out, back_up, back_down = back_weights
        (
            inputs,
            token_mod,
            head_on_tok,
            channel_tok,
            keep_tok,
            low_one,
            query_groups,
            key_groups,
            value_groups,
            log_totals,
            mixed_low,
            branch_one,
            after_attn,
            low_two,
            hidden_pre,
            hidden_low,
            branch_two,
        ) = saved_layers[layer]
        shift_one, scale_one, gate_one, shift_two, scale_two, gate_two = jnp.split(
            token_mod, 6, axis=1
        )
        down_grad = (grad_current * keep_tok * gate_two).astype(jnp.bfloat16)
        grad_gate_two = grad_current * keep_tok * branch_two
        grad_down_bias = jnp.sum(down_grad.astype(jnp.float32), axis=0)
        grad_hidden = contract_cols(down_grad, back_down) * channel_tok
        _, gelu_back = jax.vjp(gelu_tanh, hidden_pre)
        up_grad = gelu_back(grad_hidden)[0].astype(jnp.bfloat16)
        grad_up_bias = jnp.sum(up_grad.astype(jnp.float32), axis=0)
        grad_normed_two = contract_cols(up_grad, back_up)
        _, norm_back_two = jax.vjp(modulate, after_attn, shift_two, scale_two)
        grad_after, grad_shift_two, grad_scale_two = norm_back_two(grad_normed_two)
        grad_after = grad_after + grad_current
        out_grad = (grad_after * gate_one).astype(jnp.bfloat16)
        grad_gate_one = grad_after * branch_one
        grad_out_bias = jnp.sum(out_grad.astype(jnp.float32), axis=0)
        grad_mixed = (
            contract_cols(out_grad, back_out).reshape(local_rows, head_count, head_size)
            * head_on_tok[:, :, None]
        ).astype(jnp.bfloat16)
        mixed_groups = to_groups(grad_mixed.reshape(local_rows, model_width), local_rows)
        query_parts, key_parts, value_parts = lax.map(
            attend_back, (query_groups, key_groups, value_groups, mixed_groups, log_totals)
        )
        backward_grad_query = from_groups(query_parts, local_rows)
        grad_key_row = from_groups(key_parts, row_len)
        grad_value_row = from_groups(value_parts, row_len)
        own_key = jnp.where(lower_half, grad_key_row[:local_rows], grad_key_row[local_rows:])
        sent_key = jnp.where(lower_half, grad_key_row[local_rows:], grad_key_row[:local_rows])
        own_value = jnp.where(lower_half, grad_value_row[:local_rows], grad_value_row[local_rows:])
        sent_value = jnp.where(lower_half, grad_value_row[local_rows:], grad_value_row[:local_rows])
        back_key = swapped(sent_key.astype(jnp.bfloat16), "fsdp", 0).astype(sent_key.dtype)
        back_value = swapped(sent_value.astype(jnp.bfloat16), "fsdp", 0).astype(sent_value.dtype)
        grad_qkv = jnp.concatenate(
            [backward_grad_query, own_key + back_key, own_value + back_value], axis=1
        ).astype(jnp.bfloat16)
        grad_qkv_wide = grad_qkv.astype(jnp.float32)
        grad_pair_bias = jnp.concatenate(
            [
                jnp.sum(grad_qkv_wide[:, :model_width], axis=0),
                jnp.sum(grad_qkv_wide[:, 2 * model_width :], axis=0),
            ]
        )
        grad_normed_one = contract_cols(grad_qkv, back_qkv)
        _, norm_back_one = jax.vjp(modulate, inputs, shift_one, scale_one)
        grad_inputs, grad_shift_one, grad_scale_one = norm_back_one(grad_normed_one)
        grad_inputs = grad_inputs + grad_after
        grad_token_mod = jnp.concatenate(
            [
                grad_shift_one,
                grad_scale_one,
                grad_gate_one,
                grad_shift_two,
                grad_scale_two,
                grad_gate_two,
            ],
            axis=1,
        )
        grad_modulation = lax.dot_general(
            pick_item,
            grad_token_mod,
            (((0,), (0,)), ((), ())),
            precision=highest,
            preferred_element_type=jnp.float32,
        )
        every_mod_grad = lax.all_gather(
            grad_modulation.astype(jnp.bfloat16), ("fsdp", "seq"), axis=0, tiled=True
        ).astype(grad_modulation.dtype)
        grad_mod_weight = lax.dot_general(
            cond_twice,
            every_mod_grad,
            (((0,), (0,)), ((), ())),
            precision=highest,
            preferred_element_type=jnp.float32,
        )
        grad_mod_bias = lax.dynamic_slice_in_dim(
            jnp.sum(every_mod_grad, axis=0), flat_index * mod_cols, mod_cols, 0
        )
        main_rows = lax.psum_scatter(
            jnp.concatenate(
                [
                    contract_rows(low_one, grad_qkv),
                    contract_rows(mixed_low, out_grad),
                    contract_rows(low_two, up_grad),
                ],
                axis=1,
            ),
            ("fsdp", "seq"),
            scatter_dimension=0,
            tiled=True,
        )
        down_rows = lax.psum_scatter(
            contract_rows(hidden_low, down_grad), ("fsdp", "seq"), scatter_dimension=0, tiled=True
        )
        pair_part = lax.psum_scatter(
            grad_pair_bias, ("fsdp", "seq"), scatter_dimension=0, tiled=True
        )
        out_part = lax.psum_scatter(grad_out_bias, ("fsdp", "seq"), scatter_dimension=0, tiled=True)
        up_part = lax.psum_scatter(grad_up_bias, ("fsdp", "seq"), scatter_dimension=0, tiled=True)
        down_part = lax.psum_scatter(
            grad_down_bias, ("fsdp", "seq"), scatter_dimension=0, tiled=True
        )
        grad_qkv_weight = main_rows[:, : 3 * model_width]
        grad_out_weight = main_rows[:, 3 * model_width : 4 * model_width]
        grad_up_weight = main_rows[:, 4 * model_width :]
        grads = (
            grad_qkv_weight,
            grad_out_weight,
            grad_up_weight,
            down_rows,
            grad_mod_weight,
            pair_part,
            out_part,
            up_part,
            down_part,
            grad_mod_bias,
        )
        grad_current, grads = (grad_inputs, grads)
        layer_totals[layer] = grads
    stacked = tuple(
        (
            jnp.stack([layer_totals[layer][index] for layer in range(layer_count)])
            for index in range(10)
        )
    )
    return (
        current.astype(jnp.bfloat16),
        grad_current,
        stacked[0],
        stacked[1],
        stacked[2],
        stacked[3],
        stacked[4],
        stacked[5],
        stacked[6],
        stacked[7],
        stacked[8],
        stacked[9],
    )


def solution(mesh):
    return jax.shard_map(
        body,
        mesh=mesh,
        in_specs=(
            P(("fsdp", "seq"), None),
            P(None, ("fsdp", "seq"), None),
            P(None, ("fsdp", "seq"), None),
            P(None, ("fsdp", "seq"), None),
            P(None, ("fsdp", "seq"), None),
            P(None, ("fsdp", "seq"), None),
            P(None, ("fsdp", "seq")),
            P(None, ("fsdp", "seq")),
            P(None, ("fsdp", "seq")),
            P(None, ("fsdp", "seq")),
            P(None, ("fsdp", "seq")),
            P("seq"),
            P("seq", None),
            P("seq", None, None, None),
            P("seq", None, None, None),
            P(("fsdp", "seq"), None),
            P(("fsdp", "seq"), None),
        ),
        out_specs=(
            P(("fsdp", "seq"), None),
            P(("fsdp", "seq"), None),
            P(None, ("fsdp", "seq"), None),
            P(None, ("fsdp", "seq"), None),
            P(None, ("fsdp", "seq"), None),
            P(None, ("fsdp", "seq"), None),
            P(None, ("fsdp", "seq"), None),
            P(None, ("fsdp", "seq")),
            P(None, ("fsdp", "seq")),
            P(None, ("fsdp", "seq")),
            P(None, ("fsdp", "seq")),
            P(None, ("fsdp", "seq")),
        ),
        check_vma=False,
    )
```

profile of v0, /device:TPU:0, one launch (start us, length us, event | category | flops | bytes accessed | tf_op | source)
XLA Modules:
  0.0 3294.5 jit_solution(3040853195872729568)
XLA Ops:
  8.1 23.2 all-gather.18
  40.9 101.6 %all-reduce.36.cloned.1.call-done = (f32[64,6912]{1,0:T(8,128)}, f32[64,6912]{1,0:T(8,128)}) async-done(((f32[64,6912]{1,0:T(8,128)}, f32[64,6912]{1,0:T(8,128)}), (f32[64,6912]{1,0:T(8,128)}, f32[64,6912]{1,0:T(8,128)})) %all-reduce.36.cloned.1.call-update) | async-done | bytes 3538960
  154.8 42.9 %all-reduce.26 = (bf16[6912]{0:T(1024)(128)(2,1)S(1)}, bf16[2304]{0:T(1024)(128)(2,1)S(1)}, bf16[1152]{0:T(1024)(128)(2,1)}, bf16[4608]{0:T(1024)(128)(2,1)}, bf...) all-reduce(bf16[6912]{0:T(1024)(128)(2,1)S(1)} %dynamic-update-slic, ...), channel_id=2, replica_groups=mesh['fsdp'=2,'seq'=16] {'fsdp','seq'}, use_global_device_ids=true, to_apply=%add | all-reduce | flops 32256 | bytes 129024
  214.5 44.1 %all-gather.32.cloned.1.call-done = bf16[1,1152,3456]{2,0,1:T(2,128)(2,1)} async-done(((bf16[1,36,3456]{2,0,1:T(2,128)(2,1)}), bf16[1,1152,3456]{2,0,1:T(2,128)(2,1)}) %all-gather.32.cloned.1.call-update) | async-done | bytes 7962640 | tf_op jit(solution)/shard_map/all_gather | solution.py:152
  273.6 30.5 collective-permute-done.1
  354.5 42.1 %while.56 = (s32[]{:T(128)}, f32[4,512,4,72]{1,3,2,0:T(8,128)}, f32[4,4,512,1]{2,1,3,0:T(4,128)}, bf16[4,1024,4,72]{1,3,2,0:T(8,128)(2,1)}, bf16[4,512,4,72]{1,3...) while((s32[]{:T(128)}, f32[4,512,4,72]{1,3,2,0:T(8,128)}, ...), condition=%wide.region_7.8_spmd.clone, body=%wide.region_4.7_spmd.clone.sunk | while | flops 627570688 | bytes 29401692 | solution.py:230
  413.6 61.9 %all-gather.36.cloned.1.call-done = bf16[1,1152,4608]{2,0,1:T(2,128)(2,1)} async-done(((bf16[1,36,4608]{2,0,1:T(2,128)(2,1)}), bf16[1,1152,4608]{2,0,1:T(2,128)(2,1)}) %all-gather.36.cloned.1.call-update) | async-done | bytes 10616848 | tf_op jit(solution)/shard_map/all_gather | solution.py:154
  500.7 62.6 %all-gather.38.cloned.1.call-done = bf16[1,4608,1152]{2,1,0:T(8,128)(2,1)} async-done(((bf16[1,144,1152]{2,1,0:T(8,128)(2,1)}), bf16[1,4608,1152]{2,1,0:T(8,128)(2,1)}) %all-gather.38.cloned.1.call-update) | async-done | bytes 10616848 | tf_op jit(solution)/shard_map/all_gather | solution.py:155
  580.7 95.0 %all-gather.40.cloned.1.call-done = bf16[1,1152,3456]{2,0,1:T(2,128)(2,1)} async-done(((bf16[1,36,3456]{2,0,1:T(2,128)(2,1)}), bf16[1,1152,3456]{2,0,1:T(2,128)(2,1)}) %all-gather.40.cloned.1.call-update) | async-done | bytes 7962640 | tf_op jit(solution)/shard_map/all_gather | solution.py:152
  687.9 31.5 collective-permute-done.3
  735.7 22.7 collective-permute-done.2
  768.5 38.6 %while.57 = (s32[]{:T(128)}, f32[4,512,4,72]{1,3,2,0:T(8,128)}, f32[4,4,512,1]{2,1,3,0:T(4,128)}, bf16[4,1024,4,72]{1,3,2,0:T(8,128)(2,1)}, bf16[4,512,4,72]{1,3...) while((s32[]{:T(128)}, f32[4,512,4,72]{1,3,2,0:T(8,128)}, ...), condition=%wide.region_17.18_spmd.clone, body=%wide.region_14.17_spmd.clone.sunk | while | flops 627570688 | bytes 29401692 | solution.py:230
  825.9 67.9 %all-gather.44.cloned.1.call-done = bf16[1,1152,4608]{2,0,1:T(2,128)(2,1)} async-done(((bf16[1,36,4608]{2,0,1:T(2,128)(2,1)}), bf16[1,1152,4608]{2,0,1:T(2,128)(2,1)}) %all-gather.44.cloned.1.call-update) | async-done | bytes 10616848 | tf_op jit(solution)/shard_map/all_gather | solution.py:154
  919.5 62.7 %all-gather.46.cloned.1.call-done = bf16[1,4608,1152]{2,1,0:T(8,128)(2,1)} async-done(((bf16[1,144,1152]{2,1,0:T(8,128)(2,1)}), bf16[1,4608,1152]{2,1,0:T(8,128)(2,1)}) %all-gather.46.cloned.1.call-update) | async-done | bytes 10616848 | tf_op jit(solution)/shard_map/all_gather | solution.py:155
  982.2 19.4 convert_reduce_fusion
  1001.6 17.2 multiply_reduce_fusion.4
  1019.5 14.5 fusion.268
  1049.6 68.2 %while.58 = (s32[]{:T(128)}, bf16[4,512,4,72]{1,3,2,0:T(8,128)(2,1)}, f32[4,1024,4,72]{1,3,2,0:T(8,128)}, f32[4,1024,4,72]{1,3,2,0:T(8,128)}, bf16[4,1024,4,72]{...) while((s32[]{:T(128)}, ...), condition=%wide.region_24.25_spmd.clone, body=%wide.region_22.24_spmd.clone.sunk | while | flops 1542371328 | bytes 85134544 | solution.py:328
  1129.6 19.8 collective-permute-done.4
  1149.9 24.1 collective-permute-done.5
  1178.8 14.8 constant_dynamic-update-slice_fusion.3
  1204.3 22.8 convert_reduce_fusion.1
  1227.1 16.1 multiply_reduce_fusion.2
  1259.9 68.9 %while.59 = (s32[]{:T(128)}, bf16[4,512,4,72]{1,3,2,0:T(8,128)(2,1)}, f32[4,1024,4,72]{1,3,2,0:T(8,128)}, f32[4,1024,4,72]{1,3,2,0:T(8,128)}, bf16[4,1024,4,72]{...) while((s32[]{:T(128)}, ...), condition=%wide.region_31.32_spmd.clone, body=%wide.region_29.31_spmd.clone.sunk | while | flops 1542371328 | bytes 85134544 | solution.py:328
  1345.1 15.4 collective-permute-done.6
  1360.9 23.2 collective-permute-done.7
  1507.5 29.4 pad_maximum_fusion.1
  1549.1 29.6 pad_maximum_fusion
  1591.0 37.5 %all-gather.48.cloned.1.call-done = bf16[32,4,6912]{2,1,0:T(4,128)(2,1)} async-done(((bf16[1,4,6912]{2,1,0:T(4,128)(2,1)}), bf16[32,4,6912]{2,1,0:T(4,128)(2,1)}) %all-gather.48.cloned.1.call-update) | async-done | bytes 1769488 | tf_op jit(solution)/shard_map/all_gather | solution.py:372
  1635.2 219.6 %reduce-scatter.5.cloned.1.call-done = f32[144,1152]{1,0:T(8,128)} async-done(((f32[4608,1152]{1,0:T(8,128)}), f32[144,1152]{1,0:T(8,128)}) %reduce-scatter.5.cloned.1.call-update) | async-done | bytes 663568 | tf_op jit(solution)/shard_map/reduce_scatter | solution.py:398
  1854.8 225.6 %reduce-scatter.3.cloned.1.call-done = f32[144,1152]{1,0:T(8,128)} async-done(((f32[4608,1152]{1,0:T(8,128)}), f32[144,1152]{1,0:T(8,128)}) %reduce-scatter.3.cloned.1.call-update) | async-done | bytes 663568 | tf_op jit(solution)/shard_map/reduce_scatter | solution.py:398
  2082.9 1191.8 %all-reduce.34.cloned.1.call-done = (f32[1152,9216]{1,0:T(8,128)}, f32[1152,9216]{1,0:T(8,128)}) async-done(((f32[1152,9216]{1,0:T(8,128)}, f32[1152,9216]{1,0:T(8,128)}), (f32[1152,9216]{1,0:T(8,128)}, f32[1152,9216]{1,0:T(8,128)})) %all-reduce.34.cloned.1.call-update) | async-done | bytes 84934672
  (647 shorter events, 706.3 us)
Async XLA Ops:
  8.0 134.5 %all-reduce.36.cloned.1.call-start = ((), (), s32[]{:S(2)}) async-start(), calls=%async_computation.16 | async-start | bytes 7077888
  39.0 105.3 %copy-start.52 = (bf16[2,36,3456]{2,0,1:T(2,128)(2,1)S(1)}, bf16[2,36,3456]{2,0,1:T(2,128)(2,1)}, u32[]{:S(2)}) copy-start(bf16[2,36,3456]{2,0,1:T(2,128)(2,1)} %param.26) | copy-start | bytes 1492996
  39.0 107.0 %copy-start.63 = (bf16[2,36,1152]{2,0,1:T(2,128)(2,1)S(1)}, bf16[2,36,1152]{2,0,1:T(2,128)(2,1)}, u32[]{:S(2)}) copy-start(bf16[2,36,1152]{2,0,1:T(2,128)(2,1)} %param.27) | copy-start | bytes 497668
  39.0 108.1 %copy-start.49 = (bf16[2,36,4608]{2,0,1:T(2,128)(2,1)S(1)}, bf16[2,36,4608]{2,0,1:T(2,128)(2,1)}, u32[]{:S(2)}) copy-start(bf16[2,36,4608]{2,0,1:T(2,128)(2,1)} %param.28) | copy-start | bytes 1990660
  39.0 160.8 %all-reduce.38.cloned.1.call-start = ((), (), s32[]{:S(2)}) async-start(), calls=%async_computation.17 | async-start | bytes 442368 | tf_op jit(solution)/shard_map/psum | solution.py:178
  144.3 114.3 %all-gather.32.cloned.1.call-start = ((), (), s32[]{:S(2)}) async-start(), calls=%async_computation.4 | async-start | bytes 16422912 | tf_op jit(solution)/shard_map/all_gather | solution.py:152
  146.0 254.4 %all-gather.34.cloned.1.call-start = ((), (), s32[]{:S(2)}) async-start(), calls=%async_computation.5 | async-start | bytes 5474304 | tf_op jit(solution)/shard_map/all_gather | solution.py:153
  147.0 328.5 %all-gather.36.cloned.1.call-start = ((), (), s32[]{:S(2)}) async-start(), calls=%async_computation.6 | async-start | bytes 21897216 | tf_op jit(solution)/shard_map/all_gather | solution.py:154
  149.1 414.2 %all-gather.38.cloned.1.call-start = ((), (), s32[]{:S(2)}) async-start(), calls=%async_computation.7 | async-start | bytes 10948608 | tf_op jit(solution)/shard_map/all_gather | solution.py:155
  150.1 525.6 %all-gather.40.cloned.1.call-start = ((), (), s32[]{:S(2)}) async-start(), calls=%async_computation.8 | async-start | bytes 16422912 | tf_op jit(solution)/shard_map/all_gather | solution.py:152
  150.9 659.3 %all-gather.42.cloned.1.call-start = ((), (), s32[]{:S(2)}) async-start(), calls=%async_computation.9 | async-start | bytes 5474304 | tf_op jit(solution)/shard_map/all_gather | solution.py:153
  151.6 742.2 %all-gather.44.cloned.1.call-start = ((), (), s32[]{:S(2)}) async-start(), calls=%async_computation.10 | async-start | bytes 21897216 | tf_op jit(solution)/shard_map/all_gather | solution.py:154
  152.2 830.0 %all-gather.46.cloned.1.call-start = ((), (), s32[]{:S(2)}) async-start(), calls=%async_computation.11 | async-start | bytes 10948608 | tf_op jit(solution)/shard_map/all_gather | solution.py:155
  271.0 33.0 %collective-permute-start.1 = (bf16[512,1152]{1,0:T(8,128)(2,1)S(1)}, bf16[512,1152]{1,0:T(8,128)(2,1)}, u32[]{:S(2)}, u32[]{:S(2)}) collective-permute-start(bf16[512,1152]{1,0:T(8,128)(2,1)S(1)} %slice.240), channel_id=1, source_target_pairs={{0,16},{16,0},{1,17},{17,1},{2,18},{18,2},{3,19},{19,3},{4,20},{20... | collective-permute-start | bytes 3538952 | tf_op jit(solution)/shard_map/ppermute | solution.py:18
  272.6 1306.2 %all-reduce.32.cloned.1.call-start = ((), (), s32[]{:S(2)}) async-start(), calls=%async_computation.14 | async-start | bytes 196608
  308.2 36.1 %collective-permute-start = (bf16[512,1152]{1,0:T(8,128)(2,1)}, bf16[512,1152]{1,0:T(8,128)(2,1)}, u32[]{:S(2)}, u32[]{:S(2)}) collective-permute-start(bf16[512,1152]{1,0:T(8,128)(2,1)} %get-tuple-element.498), channel_id=1, source_target_pairs={{0,16},{16,0},{1,17},{17,1},{2,18},{18,2},{3,19},{19,3},{4,20},{20... | collective-permute-start | bytes 3538952 | tf_op jit(solution)/shard_map/ppermute | solution.py:18
  407.4 155.9 %copy-start.1 = (f32[512,1152]{1,0:T(8,128)}, f32[512,1152]{1,0:T(8,128)S(1)}, u32[]{:S(2)}) copy-start(f32[512,1152]{1,0:T(8,128)S(1)} %get-tuple-element.474) | copy-start | bytes 7077892
  577.7 98.0 %copy-start.101 = (f32[3456]{0:T(1024)S(1)}, f32[3456]{0:T(1024)}, u32[]{:S(2)}) copy-start(f32[3456]{0:T(1024)} %get-tuple-element.522) | copy-start | bytes 41476
  580.7 105.6 %copy-start.53 = (bf16[512,1152]{1,0:T(8,128)(2,1)}, bf16[512,1152]{1,0:T(8,128)(2,1)S(1)}, u32[]{:S(2)}) copy-start(bf16[512,1152]{1,0:T(8,128)(2,1)S(1)} %fusion.194) | copy-start | bytes 3538948
  686.5 32.9 collective-permute-start.3
  721.2 37.2 %collective-permute-start.2 = (bf16[512,1152]{1,0:T(8,128)(2,1)}, bf16[512,1152]{1,0:T(8,128)(2,1)}, u32[]{:S(2)}, u32[]{:S(2)}) collective-permute-start(bf16[512,1152]{1,0:T(8,128)(2,1)} %get-tuple-element.496), channel_id=1, source_target_pairs={{0,16},{16,0},{1,17},{17,1},{2,18},{18,2},{3,19},{19,3},{4,20},{20... | collective-permute-start | bytes 3538952 | tf_op jit(solution)/shard_map/ppermute | solution.py:18
  818.2 201.3 %copy-start.80 = (f32[512]{0:T(512)}, f32[512]{0:T(512)S(1)}, u32[]{:S(2)}) copy-start(f32[512]{0:T(512)S(1)} %broadcast_multiply_fusion) | copy-start | bytes 6148
  1120.5 28.9 collective-permute-start.4
  1125.4 48.6 %collective-permute-start.5 = (bf16[512,1152]{0,1:T(8,128)(2,1)S(1)}, bf16[512,1152]{0,1:T(8,128)(2,1)S(1)}, u32[]{:S(2)}, u32[]{:S(2)}) collective-permute-start(bf16[512,1152]{0,1:T(8,128)(2,1)S(1)} %bitcast.498), channel_id=1, source_target_pairs={{0,16},{16,0},{1,17},{17,1},{2,18},{18,2},{3,19},{19,3},{4,20},{20... | collective-permute-start | bytes 3538952 | tf_op jit(solution)/shard_map/ppermute | solution.py:18
  1259.9 74.7 %copy-start.95 = (f32[512]{0:T(512)S(1)}, f32[512]{0:T(512)}, u32[]{:S(2)}) copy-start(f32[512]{0:T(512)} %copy-done.94) | copy-start | bytes 6148
  1331.5 29.0 collective-permute-start.6
  1341.1 43.1 %collective-permute-start.7 = (bf16[512,1152]{0,1:T(8,128)(2,1)S(1)}, bf16[512,1152]{0,1:T(8,128)(2,1)S(1)}, u32[]{:S(2)}, u32[]{:S(2)}) collective-permute-start(bf16[512,1152]{0,1:T(8,128)(2,1)S(1)} %bitcast.496), channel_id=1, source_target_pairs={{0,16},{16,0},{1,17},{17,1},{2,18},{18,2},{3,19},{19,3},{4,20},{20... | collective-permute-start | bytes 3538952 | tf_op jit(solution)/shard_map/ppermute | solution.py:18
  1387.1 200.1 %all-gather.50.cloned.1.call-start = ((), (), s32[]{:S(2)}) async-start(), calls=%async_computation.13 | async-start | bytes 1824768 | tf_op jit(solution)/shard_map/all_gather | solution.py:372
  1395.9 232.6 %all-gather.48.cloned.1.call-start = ((), (), s32[]{:S(2)}) async-start(), calls=%async_computation.12 | async-start | bytes 1824768 | tf_op jit(solution)/shard_map/all_gather | solution.py:372
  1433.9 420.9 %reduce-scatter.5.cloned.1.call-start = ((), (), s32[]{:S(2)}) async-start(), calls=%async_computation.3 | async-start | bytes 21897216 | tf_op jit(solution)/shard_map/reduce_scatter | solution.py:398
  1448.1 632.4 %reduce-scatter.3.cloned.1.call-start = ((), (), s32[]{:S(2)}) async-start(), calls=%async_computation.2 | async-start | bytes 21897216 | tf_op jit(solution)/shard_map/reduce_scatter | solution.py:398
  1463.1 1811.6 %all-reduce.34.cloned.1.call-start = ((), (), s32[]{:S(2)}) async-start(), calls=%async_computation.15 | async-start | bytes 169869312
  (135 other events, 1147.7 us)
Sparse Core Ops, SparseCore 0:
  39.1 103.2 all-reduce.35
  145.5 21.8 all-reduce.37
Sparse Core Ops, SparseCore 1:
  148.2 110.4 all-gather.31
  261.3 76.2 all-gather.33
  340.9 134.6 all-gather.35
  478.4 84.8 all-gather.37
  566.2 109.5 all-gather.39
  678.6 77.7 all-gather.41
  759.7 134.1 all-gather.43
  897.2 85.0 all-gather.45
  1387.2 122.2 all-reduce.31
  1513.3 56.7 all-gather.49
  1573.7 54.7 all-gather.47
  1636.1 218.7 reduce-scatter.4
  1861.1 219.3 reduce-scatter.2
  2088.1 1186.6 all-reduce.33
where the time goes:
time: 3300 us; the launch traced here: 3290 us
  waiting for transfers between devices  2350 us (71%)
  matrix products  493 us (15%)
  other arithmetic  223 us (7%)
  local copies, waits for them, and re-layouts  127 us (4%)
  blocking collectives  66.1 us (2%)
    unnamed x19, waiting for transfers between devices  1300 us
    reduce_scatter x2, waiting for transfers between devices, body(): lax.psum_scatter(contract_rows(hidden_low, down_grad), ('fsdp', 'seq'), s...  445 us
    ppermute x8, waiting for transfers between devices, swapped(): return lax.ppermute(block, axis, route)  180 us
    all_gather x2, waiting for transfers between devices, body(): lax.all_gather(qkv_weight[layer], ('fsdp', 'seq'), axis=0, tiled=True)  139 us
    all_gather x2, waiting for transfers between devices, body(): lax.all_gather(up_weight[layer], ('fsdp', 'seq'), axis=0, tiled=True)  130 us
    all_gather x2, waiting for transfers between devices, body(): lax.all_gather(down_weight[layer], ('fsdp', 'seq'), axis=0, tiled=True)  125 us
    dot_general x8, matrix products, contract_cols(): lax.dot_general(left_side, right_side, (((1,), (1,)), ((), ())), preferre...  111 us
    dot_general x8, matrix products, contract_rows(): lax.dot_general(left_side, right_side, (((0,), (0,)), ((), ())), preferre...  82.7 us
  transfers between devices with their start and end apart: 24, of which 19 were waited for; matrix products, arithmetic and copies ran while one was open for 15% of the time, Pallas kernels for 0%

commit v1 on v0

v1 whole, which is shorter than its diff:
```python
import math

import jax
import jax.numpy as jnp
from jax import lax
from jax.experimental import pallas as pl
from jax.experimental.pallas import tpu as pltpu
from jax.sharding import PartitionSpec as P

BF = jnp.bfloat16
F32 = jnp.float32
AXES = ("fsdp", "seq")


def swap_bit(block, stage):
    axis, bit = stage
    count = lax.axis_size(axis)
    return lax.ppermute(block, axis, [(low, low ^ (1 << bit)) for low in range(count)])


def stage_bit(stage):
    axis, bit = stage
    return (lax.axis_index(axis) >> bit) & 1


def contract(left, right, left_dim, right_dim):
    return lax.dot_general(
        left, right, (((left_dim,), (right_dim,)), ((), ())), preferred_element_type=F32
    )


def relative_masks(stages, mask_of):
    masks = [0]
    for stage in reversed(stages):
        masks = masks + [mask ^ mask_of(stage) for mask in masks]
    return masks


class Feed:
    def __init__(self):
        self.flights = []
        self.ticks = 0
        self.later = {}

    def start(self, flight):
        wait, parts = next(flight)
        self.flights.append((flight, self.ticks + wait - 1, parts))

    def at(self, tick, flight):
        self.later.setdefault(tick, []).append(flight)

    def tick(self, value):
        for flight in self.later.pop(self.ticks, []):
            self.start(flight)
        due = [entry for entry in self.flights if entry[1] <= self.ticks]
        flying = [entry for entry in self.flights if entry[1] > self.ticks]
        self.ticks += 1
        value, arrived = lax.optimization_barrier((value, [parts for _, _, parts in due]))
        for (flight, _, _), parts in zip(due, arrived):
            try:
                wait, sent = flight.send(parts)
                flying.append((flight, self.ticks + wait - 1, sent))
            except StopIteration:
                pass
        self.flights = flying
        return value

    def until(self, result, value):
        while not result:
            value = self.tick(value)
        return value

    def finish(self, value):
        while self.flights or self.later:
            value = self.tick(value)
        return value


def reduce_flight(away, stay, right, side, routes, cuts, rows, waits, result):
    core_stage, first_route, second_route, far_stages = routes
    first, second = cuts
    arrived = yield waits[0], swap_bit(contract(away, right, side, 0).astype(BF), core_stage)
    kept, first_sent, second_sent = keep_grad(stay, right, side, arrived, first, second)
    first_arrived, second_arrived = yield waits[1], (
        swap_bit(first_sent, first_route[0]),
        swap_bit(second_sent, second_route[0]),
    )

    def add(left, other, low, high):
        return left[low:high].astype(F32) + other[low:high].astype(F32)

    first_kept, second_kept = kept[:first], kept[first:]
    half_first, half_second = first // 2, second // 2
    first_sent = add(first_kept, first_arrived, half_first, first).astype(BF)
    second_sent = add(second_kept, second_arrived, half_second, second).astype(BF)
    first_kept = add(first_kept, first_arrived, 0, half_first).astype(BF)
    second_kept = add(second_kept, second_arrived, 0, half_second).astype(BF)
    first_arrived, second_arrived = yield waits[2], (
        swap_bit(first_sent, first_route[1]),
        swap_bit(second_sent, second_route[1]),
    )
    for index, stage in enumerate(far_stages):
        first, second = half_first, half_second
        half_first, half_second = first // 2, second // 2
        sent = jnp.concatenate(
            [
                add(first_kept, first_arrived, half_first, first),
                add(second_kept, second_arrived, half_second, second),
            ],
            axis=0,
        ).astype(BF)
        first_kept = add(first_kept, first_arrived, 0, half_first).astype(BF)
        second_kept = add(second_kept, second_arrived, 0, half_second).astype(BF)
        arrived = yield 1, swap_bit(sent, stage)
        first_arrived, second_arrived = arrived[:half_first], arrived[half_first:]
    block = jnp.concatenate(
        [
            add(first_kept, first_arrived, 0, half_first),
            add(second_kept, second_arrived, 0, half_second),
        ],
        axis=0,
    )
    result.append(block[:rows])


def wide_tile(columns):
    return next(tile for tile in (1536, 1152, 768, 512, 384, 256, 128) if columns % tile == 0)


def keep_grad(left, right, side, arrived, first, second):
    half = first + second
    tokens, columns = right.shape
    tile = wide_tile(columns)

    def kernel(left_ref, right_ref, arrived_ref, kept_ref, first_ref, second_ref, *scratch):
        if side == 0:
            turned_ref = scratch[0]

            @pl.when(pl.program_id(0) == 0)
            def _():
                turned_ref[...] = left_ref[...].astype(F32).T.astype(BF)

        else:
            turned_ref = left_ref
        total = jnp.dot(turned_ref[...], right_ref[...], preferred_element_type=F32)
        total = (total + arrived_ref[...].astype(F32)).astype(BF)
        kept_ref[...] = total[:half]
        first_ref[...] = total[half : half + first]
        second_ref[...] = total[half + first :]

    outs = [jax.ShapeDtypeStruct((count, columns), BF) for count in (half, first, second)]
    return pl.pallas_call(
        kernel,
        out_shape=outs,
        grid=(columns // tile,),
        in_specs=[
            pl.BlockSpec(left.shape, lambda j: (0, 0)),
            pl.BlockSpec((tokens, tile), lambda j: (0, j)),
            pl.BlockSpec((2 * half, tile), lambda j: (0, j)),
        ],
        out_specs=[
            pl.BlockSpec((count, tile), lambda j: (0, j)) for count in (half, first, second)
        ],
        scratch_shapes=[pltpu.VMEM((2 * half, tokens), BF)] if side == 0 else [],
        cost_estimate=cost(4 * half * tokens * columns, [left, right, arrived, *outs]),
        name="keep_grad",
    )(left, right, arrived)


def modulation_flight(block, bias, stages, result):
    for stage in stages[:-1]:
        half = block.shape[0] // 2
        arrived = yield 1, swap_bit(block[half:], stage)
        block = block[:half] + arrived
    arrived = yield 1, swap_bit(block, stages[-1])
    result.append(block + arrived + bias[None])


def gather_flight(shard, cut, routes, waits, result):
    core_stage, first_route, second_route, far_stages = routes
    waits = [1] * (len(far_stages) - 2) + list(waits)
    shard = yield 1, shard
    blocks = [shard]
    for stage in reversed(far_stages):
        sent = jnp.concatenate(blocks, axis=0) if len(blocks) > 1 else blocks[0]
        arrived = yield waits.pop(0), swap_bit(sent, stage)
        rows = shard.shape[0]
        blocks = blocks + [
            arrived[start : start + rows] for start in range(0, arrived.shape[0], rows)
        ]
    owned = [
        jnp.concatenate([block[:cut] for block in blocks], axis=0),
        jnp.concatenate([block[cut:] for block in blocks], axis=0),
    ]
    routes = (second_route, first_route)
    arrived = yield (
        waits.pop(0),
        [swap_bit(part, route[0]) for part, route in zip(owned, routes)],
    )
    pairs = [jnp.concatenate([part, more], axis=0) for part, more in zip(owned, arrived)]
    fars = yield waits.pop(0), [swap_bit(pair, route[1]) for pair, route in zip(pairs, routes)]
    others = yield (
        waits.pop(0),
        [[swap_bit(pair, core_stage), swap_bit(far, core_stage)] for pair, far in zip(pairs, fars)],
    )
    for pair, far, other in zip(pairs, fars, others):
        result.append((pair, far, other[0], other[1]))


def take_chunks(left, places, chunk_rows):
    far_count = places.shape[0] - 3
    columns = left.shape[1]
    part_rows = chunk_rows // 2

    def take(places_ref, in_ref, stay_ref, away_ref):
        x_here, y_here, core_here = places_ref[0], places_ref[1], places_ref[2]
        for half in range(2):
            for one in range(2):
                for two in range(2):
                    x_place = jnp.bitwise_xor(x_here, two if half else one)
                    y_place = jnp.bitwise_xor(y_here, one if half else two)
                    stay_ref[two, half, one, 0] = in_ref[x_place, 0, y_place, core_here, half]
                    away_ref[two, half, one, 0] = in_ref[x_place, 0, y_place, 1 - core_here, half]

    shape = (2, 2, 2, far_count, part_rows, columns)
    out_spec = pl.BlockSpec(
        (2, 2, 2, 1, part_rows, columns), lambda i, places: (0, 0, 0, i, 0, 0)
    )
    parts = pl.pallas_call(
        take,
        out_shape=[jax.ShapeDtypeStruct(shape, left.dtype)] * 2,
        grid_spec=pltpu.PrefetchScalarGridSpec(
            num_scalar_prefetch=1,
            grid=(far_count,),
            in_specs=[
                pl.BlockSpec(
                    (2, 1, 2, 2, 2, part_rows, columns),
                    lambda i, places: (0, places[3 + i], 0, 0, 0, 0, 0),
                )
            ],
            out_specs=[out_spec, out_spec],
        ),
        cost_estimate=pl.CostEstimate(
            flops=0, bytes_accessed=4 * left.size, transcendentals=0
        ),
        name="take_chunks",
    )(places, left.reshape(2, far_count, 2, 2, 2, part_rows, columns))
    return [part.reshape(left.shape[0] // 2, columns) for part in parts]


def place_chunks(first, second, places, out_shape):
    far_count = places.shape[0] - 3
    columns = out_shape[1]
    rows = first[0].shape[0] // (2 * far_count)
    pieces = [piece.reshape(2, far_count, rows, columns) for piece in (*first, *second)]

    def place(places_ref, *refs):
        out_ref = refs[-1]
        x_here, y_here, core_here = places_ref[0], places_ref[1], places_ref[2]
        for half in range(2):
            for core in range(2):
                for two in range(2):
                    ref = refs[4 * half + 2 * core + two]
                    for one in range(2):
                        x_place = jnp.bitwise_xor(x_here, two if half else one)
                        y_place = jnp.bitwise_xor(y_here, one if half else two)
                        core_place = jnp.bitwise_xor(core_here, core)
                        out_ref[x_place, 0, y_place, core_place, half] = ref[one, 0]

    in_spec = pl.BlockSpec((2, 1, rows, columns), lambda i, places: (0, i, 0, 0))
    view = (2, far_count, 2, 2, 2, rows, columns)
    return pl.pallas_call(
        place,
        out_shape=jax.ShapeDtypeStruct(view, BF),
        grid_spec=pltpu.PrefetchScalarGridSpec(
            num_scalar_prefetch=1,
            grid=(far_count,),
            in_specs=[in_spec] * 8,
            out_specs=pl.BlockSpec(
                (2, 1, 2, 2, 2, rows, columns), lambda i, places: (0, places[3 + i], 0, 0, 0, 0, 0)
            ),
        ),
        cost_estimate=pl.CostEstimate(
            flops=0, bytes_accessed=4 * out_shape[0] * columns, transcendentals=0
        ),
        name="place_chunks",
    )(places, *pieces).reshape(out_shape)


class Tiles:
    def __init__(self, parts, tile, start, count):
        first, second = parts
        self.pieces = [piece for pair in zip(first, second) for piece in pair]
        self.tile, self.start, self.count = tile, start, count
        self.rows = sum(piece.shape[0] for piece in self.pieces)

    def operands(self):
        return list(self.pieces)

    def specs(self):
        return [
            pl.BlockSpec((piece.shape[0], self.tile), lambda j: (0, self.start + j))
            for piece in self.pieces
        ]

    def weight(self, refs):
        return jnp.concatenate([ref[...] for ref in refs[:8]], axis=0)

    def columns(self):
        return self.count * self.tile


def cost(flops, arrays, transcendentals=0):
    return pl.CostEstimate(
        flops=int(flops),
        bytes_accessed=int(sum(array.size * array.dtype.itemsize for array in arrays)),
        transcendentals=int(transcendentals),
    )


def project(left, tiles, bias, out_dtype, name):
    rows = left.shape[0]
    operands = tiles.operands()

    def kernel(left_ref, bias_ref, *refs):
        out_ref = refs[-1]

        total = jnp.dot(left_ref[...], tiles.weight(refs), preferred_element_type=F32)
        out_ref[...] = (total + bias_ref[...]).astype(out_dtype)

    out = jax.ShapeDtypeStruct((rows, tiles.columns()), out_dtype)
    return pl.pallas_call(
        kernel,
        out_shape=out,
        grid=(tiles.count,),
        in_specs=[
            pl.BlockSpec(left.shape, lambda j: (0, 0)),
            pl.BlockSpec((1, tiles.tile), lambda j: (0, j)),
            *tiles.specs(),
        ],
        out_specs=pl.BlockSpec((rows, tiles.tile), lambda j: (0, j)),
        cost_estimate=cost(2 * rows * left.shape[1] * tiles.columns(), [left, out, *operands]),
        name=name,
    )(left, bias.reshape(1, -1), *operands)


def gelu_parts(value):
    inner = math.sqrt(2.0 / math.pi) * (value + 0.044715 * (value * value * value))
    return jnp.tanh(inner)


def project_up(left, tiles, bias, channel_on):
    rows = left.shape[0]
    groups = channel_on.shape[0]
    operands = tiles.operands()

    def kernel(left_ref, bias_ref, channel_ref, *refs):
        pre_ref, turned_ref = refs[-2:]

        pre = jnp.dot(left_ref[...], tiles.weight(refs), preferred_element_type=F32)
        pre = pre + bias_ref[...]
        pre_ref[...] = pre
        hidden = 0.5 * pre * (1.0 + gelu_parts(pre))
        span = rows // groups
        for group in range(groups):
            part = hidden[group * span : (group + 1) * span] * channel_ref[group : group + 1]
            turned_ref[:, group * span : (group + 1) * span] = part.T.astype(BF)

    pre = jax.ShapeDtypeStruct((rows, tiles.columns()), F32)
    turned = jax.ShapeDtypeStruct((tiles.columns(), rows), BF)
    return pl.pallas_call(
        kernel,
        out_shape=[pre, turned],
        grid=(tiles.count,),
        in_specs=[
            pl.BlockSpec(left.shape, lambda j: (0, 0)),
            pl.BlockSpec((1, tiles.tile), lambda j: (0, j)),
            pl.BlockSpec((groups, tiles.tile), lambda j: (0, j)),
            *tiles.specs(),
        ],
        out_specs=[
            pl.BlockSpec((rows, tiles.tile), lambda j: (0, j)),
            pl.BlockSpec((tiles.tile, rows), lambda j: (j, 0)),
        ],
        cost_estimate=cost(
            2 * rows * left.shape[1] * tiles.columns(), [left, pre, turned, *operands], pre.size
        ),
        name="project_up",
    )(left, bias.reshape(1, -1), channel_on, *operands)


def project_back(right, tiles, order, parts, name):
    rows = right.shape[0]
    operands = tiles.operands()
    width = order.shape[1]

    def kernel(right_ref, order_ref, *refs):
        out_ref, total_ref = refs[-2:]
        index = pl.program_id(0)

        @pl.when(index == 0)
        def _():
            total_ref[...] = jnp.zeros_like(total_ref)

        total_ref[...] += contract(right_ref[...], tiles.weight(refs), 1, 1)

        @pl.when(index == tiles.count - 1)
        def _():
            rest = total_ref[...]
            out = None
            for part in range(parts):
                high = rest.astype(BF)
                placed = jnp.dot(high, order_ref[...], preferred_element_type=F32)
                out = placed if out is None else out + placed
                if part < parts - 1:
                    rest = rest - high.astype(F32)
            out_ref[...] = out

    out = jax.ShapeDtypeStruct((rows, width), F32)
    return pl.pallas_call(
        kernel,
        out_shape=out,
        grid=(tiles.count,),
        in_specs=[
            pl.BlockSpec((rows, tiles.tile), lambda j: (0, j)),
            pl.BlockSpec(order.shape, lambda j: (0, 0)),
            *tiles.specs(),
        ],
        out_specs=pl.BlockSpec(out.shape, lambda j: (0, 0)),
        scratch_shapes=[pltpu.VMEM((rows, tiles.rows), F32)],
        cost_estimate=cost(
            2 * rows * tiles.rows * (tiles.columns() + parts * width), [right, out, order, *operands]
        ),
        name=name,
    )(right, order, *operands)


def hidden_back(down_grad, full_down, pre, channel_on, tile):
    rows, width = down_grad.shape
    groups = channel_on.shape[0]
    columns = pre.shape[1]

    def kernel(grad_ref, weight_ref, pre_ref, channel_ref, out_ref, sum_ref):
        value = pre_ref[...]
        tanh = gelu_parts(value)
        slope = 0.5 * (1.0 + tanh) + 0.5 * value * (1.0 - tanh * tanh) * math.sqrt(
            2.0 / math.pi
        ) * (1.0 + 3.0 * 0.044715 * value * value)
        grad = contract(grad_ref[...], weight_ref[...], 1, 1) * slope
        span = rows // groups
        total = None
        for group in range(groups):
            part = (
                grad[group * span : (group + 1) * span] * channel_ref[group : group + 1]
            ).astype(BF)
            out_ref[group * span : (group + 1) * span] = part
            along = jnp.sum(part.astype(F32), axis=0, keepdims=True)
            total = along if total is None else total + along
        sum_ref[...] = total

    out = jax.ShapeDtypeStruct((rows, columns), BF)
    sums = jax.ShapeDtypeStruct((1, columns), F32)
    return pl.pallas_call(
        kernel,
        out_shape=[out, sums],
        grid=(columns // tile,),
        in_specs=[
            pl.BlockSpec(down_grad.shape, lambda j: (0, 0)),
            pl.BlockSpec((tile, width), lambda j: (j, 0)),
            pl.BlockSpec((rows, tile), lambda j: (0, j)),
            pl.BlockSpec((groups, tile), lambda j: (0, j)),
        ],
        out_specs=[
            pl.BlockSpec((rows, tile), lambda j: (0, j)),
            pl.BlockSpec((1, tile), lambda j: (0, j)),
        ],
        cost_estimate=cost(
            2 * rows * width * columns, [down_grad, full_down, pre, out], rows * columns
        ),
        name="hidden_back",
    )(down_grad, full_down, pre, channel_on)


def head_window(head, head_size, width):
    start = jnp.minimum(head * head_size // 128, width // 128 - 2) * 128
    lane = lax.broadcasted_iota(jnp.int32, (1, 256), 1) + start
    inside = (lane >= head * head_size) & (lane < (head + 1) * head_size)
    return pl.multiple_of(start, 128), inside


def attend(qkv, other, head_on, block_mask, head_count):
    rows = qkv.shape[0]
    width = qkv.shape[1] // 3
    head_size = width // head_count
    groups = head_on.shape[0]
    span = rows // groups
    factor = 1.0 / math.sqrt(head_size) / math.log(2.0)

    def kernel(qkv_ref, other_ref, head_ref, mask_ref, mixed_ref, total_ref):
        head = pl.program_id(0)
        start, inside = head_window(head, head_size, width)
        window = pl.ds(start, 256)
        key_window = pl.ds(start + width, 256)
        value_window = pl.ds(start + 2 * width, 256)
        keys = (qkv_ref[:, key_window], other_ref[:, window])
        values = (qkv_ref[:, value_window], other_ref[:, key_window])
        for group in range(groups):
            at = pl.ds(group * span, span)
            query = qkv_ref[at, window]
            query = jnp.where(inside, query, jnp.zeros_like(query))
            scores = [
                contract(query, key, 1, 1) * factor
                + mask_ref[group : group + 1, side * rows : (side + 1) * rows]
                for side, key in enumerate(keys)
            ]
            largest = jnp.maximum(
                jnp.max(scores[0], axis=1, keepdims=True), jnp.max(scores[1], axis=1, keepdims=True)
            )
            powers = [jnp.exp2(score - largest) for score in scores]
            total = jnp.sum(powers[0], axis=1, keepdims=True) + jnp.sum(
                powers[1], axis=1, keepdims=True
            )
            inverse = 1.0 / total
            out = None
            for power, value in zip(powers, values):
                part = jnp.dot((power * inverse).astype(BF), value, preferred_element_type=F32)
                out = part if out is None else out + part
            out = (out * head_ref[group : group + 1, window]).astype(BF)
            mixed_ref[at, window] = jnp.where(inside, out, mixed_ref[at, window])
            lane = lax.broadcasted_iota(jnp.int32, (1, 128), 1)
            total_ref[at, :] = jnp.where(
                lane == head, largest + jnp.log2(total), total_ref[at, :]
            )

    mixed = jax.ShapeDtypeStruct((rows, width), BF)
    totals = jax.ShapeDtypeStruct((rows, 128), F32)
    return pl.pallas_call(
        kernel,
        out_shape=[mixed, totals],
        grid=(head_count,),
        in_specs=[
            pl.BlockSpec(array.shape, lambda h: (0, 0)) for array in (qkv, other, head_on, block_mask)
        ],
        out_specs=[pl.BlockSpec(array.shape, lambda h: (0, 0)) for array in (mixed, totals)],
        cost_estimate=cost(
            4 * head_count * rows * 2 * rows * 256, [qkv, other, mixed], head_count * rows * 2 * rows
        ),
        name="attend",
    )(qkv, other, head_on, block_mask)


def attend_back(qkv, other, grad_mixed, totals, block_mask, head_count):
    rows = qkv.shape[0]
    width = qkv.shape[1] // 3
    head_size = width // head_count
    blocks = block_mask.shape[0]
    span = 2 * rows // blocks
    scale = 1.0 / math.sqrt(head_size)
    factor = scale / math.log(2.0)

    def kernel(qkv_ref, other_ref, grad_ref, totals_ref, mask_ref, query_out, own_out, other_out):
        head = pl.program_id(0)
        start, inside = head_window(head, head_size, width)
        window = pl.ds(start, 256)
        key_window = pl.ds(start + width, 256)
        value_window = pl.ds(start + 2 * width, 256)
        query = qkv_ref[:, window]
        query = jnp.where(inside, query, jnp.zeros_like(query))
        grad = grad_ref[:, window]
        grad = jnp.where(inside, grad, jnp.zeros_like(grad))
        total = totals_ref[pl.ds(head, 1), :]
        kept = []
        along = None
        for block in range(blocks):
            own = block < blocks // 2
            at = pl.ds((block if own else block - blocks // 2) * span, span)
            key = qkv_ref[at, key_window] if own else other_ref[at, window]
            value = qkv_ref[at, value_window] if own else other_ref[at, key_window]
            scores = contract(key, query, 1, 1)
            probs = jnp.exp2(scores * factor + (mask_ref[block : block + 1, :] - total))
            grad_probs = contract(value, grad, 1, 1)
            part = jnp.sum(probs * grad_probs, axis=0, keepdims=True)
            along = part if along is None else along + part
            kept.append((own, at, key, probs, grad_probs))
        query_grad = None
        for own, at, key, probs, grad_probs in kept:
            grad_scores = (probs * (grad_probs - along)).astype(BF)
            key_part = jnp.dot(grad_scores, query, preferred_element_type=F32) * scale
            value_part = jnp.dot(probs.astype(BF), grad, preferred_element_type=F32)
            out_ref = own_out if own else other_out
            out_ref[at, window] = jnp.where(
                inside, key_part.astype(out_ref.dtype), out_ref[at, window]
            )
            out_ref[at, key_window] = jnp.where(
                inside, value_part.astype(out_ref.dtype), out_ref[at, key_window]
            )
            part = contract(grad_scores, key, 0, 0)
            query_grad = part if query_grad is None else query_grad + part
        query_out[:, window] = jnp.where(
            inside, (query_grad * scale).astype(BF), query_out[:, window]
        )

    outs = [
        jax.ShapeDtypeStruct((rows, width), BF),
        jax.ShapeDtypeStruct((rows, 2 * width), F32),
        jax.ShapeDtypeStruct((rows, 2 * width), BF),
    ]
    operands = (qkv, other, grad_mixed, totals, block_mask)
    return pl.pallas_call(
        kernel,
        out_shape=outs,
        grid=(head_count,),
        in_specs=[pl.BlockSpec(array.shape, lambda h: (0, 0)) for array in operands],
        out_specs=[pl.BlockSpec(array.shape, lambda h: (0, 0)) for array in outs],
        cost_estimate=cost(
            10 * head_count * rows * 2 * rows * 256, [*operands, *outs], head_count * rows * 2 * rows
        ),
        name="attend_back",
    )(*operands)


def cond_columns(steps, first, count, model_width):
    half_width = model_width // 2
    index = first + jnp.arange(count, dtype=jnp.int32)
    is_sine = index >= half_width
    place = jnp.where(is_sine, index - half_width, index).astype(F32)
    frequency = jnp.exp(-math.log(10000.0) * place / half_width)
    angles = steps.astype(F32)[:, None] * frequency[None, :]
    values = jnp.where(is_sine[None, :], jnp.sin(angles), jnp.cos(angles))
    return jax.nn.silu(values).astype(BF)


def normalize(values):
    centered = values - jnp.mean(values, axis=-1, keepdims=True)
    spread = jnp.mean(centered * centered, axis=-1, keepdims=True)
    inverse = lax.rsqrt(spread + 1e-06)
    return centered * inverse, inverse


def normalize_back(grad_normed, normed, inverse):
    along = jnp.mean(grad_normed * normed, axis=-1, keepdims=True)
    level = jnp.mean(grad_normed, axis=-1, keepdims=True)
    return inverse * (grad_normed - level - normed * along)


def body(
    tokens,
    qkv_weight,
    out_weight,
    up_weight,
    down_weight,
    mod_weight,
    qv_bias,
    out_bias,
    up_bias,
    down_bias,
    mod_bias,
    row_items,
    timesteps,
    head_mask,
    channel_mask,
    token_keep,
    cotangent,
):
    layer_count = qkv_weight.shape[0]
    width = out_weight.shape[2]
    hidden_width = up_weight.shape[2]
    head_count = head_mask.shape[3]
    head_size = width // head_count
    item_count = timesteps.shape[1]
    local_rows = tokens.shape[0]
    row_len = 2 * local_rows
    group_rows = row_len // item_count
    group_count = local_rows // group_rows
    scale_factor = 1.0 / math.sqrt(head_size)
    seq_count = lax.axis_size("seq")
    seq_bits = seq_count.bit_length() - 1
    device_count = 2 * seq_count
    half_index = lax.axis_index("fsdp")
    seq_index = lax.axis_index("seq")
    flat_index = half_index * seq_count + seq_index
    shard_rows = mod_weight.shape[1]
    items_here = row_items[0]
    far_stages = [("seq", bit) for bit in range(2, seq_bits)]
    core_stage = ("seq", 0)

    padded_rows = -(-shard_rows // 8) * 8
    row_cut = (padded_rows + 8) // 16 * 8
    x_stage, y_stage = ("fsdp", 0), ("seq", 1)
    routes = (core_stage, (y_stage, x_stage), (x_stage, y_stage), far_stages)
    far_count = 1 << len(far_stages)

    def flat_mask(stage):
        return seq_count if stage[0] == "fsdp" else 1 << stage[1]

    chunk_masks, chunk_places = [], []
    for core_mask in (0, 1):
        for two in range(2):
            for part, route in enumerate(routes[1:3]):
                part_rows = padded_rows - row_cut if part else row_cut
                first_mask = flat_mask(route[0]) if two else 0
                for mask in relative_masks([route[1], *far_stages], flat_mask):
                    chunk_masks += [core_mask ^ first_mask ^ mask] * part_rows
                    chunk_places += list(range(row_cut * part, row_cut * part + part_rows))
    chunk_masks = jnp.array(chunk_masks, jnp.int32)
    chunk_places = jnp.array(chunk_places, jnp.int32)
    source = jnp.where(
        chunk_places < shard_rows, (flat_index ^ chunk_masks) * shard_rows + chunk_places, -1
    )
    order = (source[:, None] == jnp.arange(width, dtype=jnp.int32)[None, :]).astype(BF)

    def ordered(left):
        return contract(left, order, 1, 1).astype(BF)

    feed = Feed()
    place_table = jnp.stack(
        [half_index, (seq_index >> 1) & 1, seq_index & 1]
        + [
            (seq_index >> 2) ^ (mask >> 2)
            for mask in relative_masks(far_stages, lambda stage: 1 << stage[1])
        ]
    ).astype(jnp.int32)

    def scatter_ordered(left, right, waits, result):
        half = left.shape[1] // 2
        cuts = (2 * far_count * row_cut, 2 * far_count * (padded_rows - row_cut))
        feed.start(
            reduce_flight(
                left[:, half:], left[:, :half], right, 0, routes, cuts, shard_rows, waits, result
            )
        )

    def scatter_chunks(turned, right, waits, result):
        rows = turned.shape[0] // device_count
        stay, away = take_chunks(turned, place_table, rows)
        cuts = (far_count * rows, far_count * rows)
        feed.start(reduce_flight(away, stay, right, 1, routes, cuts, rows, waits, result))

    gathered = []

    def unit_ticks(unit):
        early = ((0, 1, 2, 3, 5, 6), (1, 3, 4, 6, 8, 9), (4, 6, 7, 8, 11, 12))
        late = ((7, 8, 10, 11, 13, 14), (8, 10, 11, 13, 16, 17), (11, 13, 15, 16, 19, 20))
        if unit < 3:
            return early[unit]
        return tuple(tick + 8 * (unit // 3 - 1) for tick in late[unit % 3])

    def padded(shard):
        return jnp.pad(shard, ((0, padded_rows - shard_rows), (0, 0)))

    for layer in range(layer_count):
        up_out = jnp.concatenate([up_weight[layer], out_weight[layer]], axis=1)
        for index, (shard, cut) in enumerate(
            (
                (padded(qkv_weight[layer]), row_cut),
                (padded(up_out), row_cut),
                (down_weight[layer], down_weight.shape[1] // 2),
            )
        ):
            result = []
            gathered.append(result)
            start, *due = unit_ticks(3 * layer + index)
            waits = [after - before for before, after in zip([start] + due, due)]
            feed.at(start, gather_flight(shard, cut, routes, waits, result))

    def qkv_tiles(layer):
        return Tiles(gathered[3 * layer], width, 0, 3)

    def pair_tiles(layer):
        return Tiles(gathered[3 * layer], width, 1, 2)

    def up_tiles(layer):
        tile = wide_tile(hidden_width) // 2
        return Tiles(gathered[3 * layer + 1], tile, 0, hidden_width // tile)

    def out_tiles(layer):
        return Tiles(gathered[3 * layer + 1], width, hidden_width // width, 1)

    biases = (qv_bias, out_bias, up_bias, down_bias, mod_bias)
    steps_high = (timesteps // 32).astype(BF)
    steps_low = (timesteps % 32).astype(BF)
    small = jnp.concatenate(
        [bias.reshape(-1) for bias in biases] + [steps_high.reshape(-1), steps_low.reshape(-1)]
    )
    small = feed.tick(small[None])
    small_stages = [("seq", bit) for bit in reversed(range(seq_bits))] + [x_stage]
    for index, stage in enumerate(small_stages):
        small = jnp.concatenate([small, swap_bit(small, stage)], axis=0)
        if index == 1:
            small = feed.tick(small)
    small_masks = jnp.array(relative_masks(list(reversed(small_stages)), flat_mask), jnp.int32)
    put_back = (flat_index ^ small_masks)[None, :] == jnp.arange(device_count)[:, None]
    every_small = jnp.dot(put_back.astype(BF), small, preferred_element_type=F32)
    full_biases = []
    offset = 0
    for bias in biases:
        columns = bias.shape[1]
        full_biases.append(
            [
                every_small[:, offset + layer * columns : offset + (layer + 1) * columns]
                .reshape(-1)
                for layer in range(layer_count)
            ]
        )
        offset += layer_count * columns
    step_parts = every_small[:seq_count, offset:]
    every_step = step_parts[:, :item_count] * 32.0 + step_parts[:, item_count:]

    cond_every = cond_columns(every_step.reshape(-1), flat_index * shard_rows, shard_rows, width)
    seq_masks = jnp.array(
        relative_masks([("seq", bit) for bit in range(seq_bits)], lambda stage: 1 << stage[1]),
        jnp.int32,
    )
    pick_row = (seq_index ^ seq_masks)[:, None] == jnp.arange(seq_count)[None, :]
    cond_relative = (
        jnp.sum(
            jnp.where(
                pick_row[:, :, None, None],
                cond_every.astype(F32).reshape(1, seq_count, item_count, shard_rows),
                0.0,
            ),
            axis=1,
        )
        .astype(BF)
        .reshape(seq_count * item_count, shard_rows)
    )

    mod_stages = [("seq", bit) for bit in range(seq_bits)] + [("fsdp", 0)]
    modulations = [[] for _ in range(layer_count)]

    def modulation_part(layer):
        return jnp.dot(cond_relative, mod_weight[layer], preferred_element_type=F32)

    block = feed.tick(modulation_part(0))
    for index, stage in enumerate(mod_stages[:-1]):
        half = block.shape[0] // 2
        block = block[:half] + swap_bit(block[half:], stage)
        if index == 1:
            block = feed.tick(block)
    block = block + swap_bit(block, mod_stages[-1]) + full_biases[4][0][None]
    modulations[0].append(feed.tick(block))
    for layer in range(1, layer_count):
        feed.start(
            modulation_flight(
                modulation_part(layer), full_biases[4][layer], mod_stages, modulations[layer]
            )
        )

    group_item = (
        (half_index * local_rows + jnp.arange(group_count, dtype=jnp.int32) * group_rows)
        * items_here
        // row_len
    )
    other_item = (
        ((1 - half_index) * local_rows + jnp.arange(group_count, dtype=jnp.int32) * group_rows)
        * items_here
        // row_len
    )
    group_is = group_item[:, None] == jnp.arange(item_count, dtype=jnp.int32)[None, :]

    def of_groups(table):
        return jnp.sum(
            jnp.where(group_is[:, :, None], table.astype(F32)[None], 0.0), axis=1, keepdims=False
        )[:, None, :]

    block_item = jnp.concatenate([group_item, other_item])
    block_mask = jnp.where(group_item[:, None] == block_item[None, :], 0.0, -1e30).astype(F32)
    query_mask = jnp.repeat(block_mask, group_rows, axis=1)
    key_mask = jnp.repeat(block_mask.T, group_rows, axis=1)

    def grouped(values):
        return values.reshape(group_count, group_rows, values.shape[-1])

    def ungrouped(values):
        return values.reshape(local_rows, values.shape[-1])

    current = grouped(tokens.astype(F32))
    saved_layers = []
    full_downs = []
    for layer in range(layer_count):
        pair_bias, out_b, up_b, down_b = (full_biases[index][layer] for index in range(4))
        current = feed.until(modulations[layer], current)
        (modulation,) = modulations[layer]
        shift_one, scale_one, gate_one, shift_two, scale_two, gate_two = jnp.split(
            of_groups(modulation), 6, axis=2
        )
        head_on = jnp.repeat(of_groups(head_mask[0, layer]), head_size, axis=2)[:, 0]
        channel_on = of_groups(channel_mask[0, layer])[:, 0]
        keep_tok = grouped(token_keep[:, layer].astype(F32)[:, None])
        normed_one, inverse_one = normalize(current)
        low_one = ungrouped((normed_one * (1.0 + scale_one) + shift_one).astype(BF))
        other_one = swap_bit(low_one, x_stage)
        bias_three = jnp.concatenate(
            [pair_bias[:width], jnp.zeros((width,), F32), pair_bias[width:]]
        )
        low_one = feed.tick(low_one)
        low_one = feed.tick(ordered(low_one))
        low_one = feed.until(gathered[3 * layer], low_one)
        qkv_low = project(low_one, qkv_tiles(layer), bias_three, BF, "project_qkv")
        other_low = project(
            ordered(other_one), pair_tiles(layer), bias_three[width:], BF, "project_pair"
        )
        other_low = feed.tick(other_low)
        mixed_low, totals = attend(qkv_low, other_low, head_on, query_mask, head_count)
        totals = totals[:, :head_count].T
        mixed_low = feed.tick(mixed_low)
        mixed_low = feed.tick(ordered(mixed_low))
        mixed_low = feed.until(gathered[3 * layer + 1], mixed_low)
        branch_one = grouped(project(mixed_low, out_tiles(layer), out_b, F32, "project_out"))
        after_attn = current + gate_one * branch_one
        normed_two, inverse_two = normalize(after_attn)
        low_two = ungrouped((normed_two * (1.0 + scale_two) + shift_two).astype(BF))
        low_two = feed.tick(ordered(low_two))
        hidden_pre, hidden_turned = project_up(low_two, up_tiles(layer), up_b, channel_on)
        hidden_turned = feed.tick(hidden_turned)
        hidden_turned = feed.tick(hidden_turned)
        hidden_turned = feed.until(gathered[3 * layer + 2], hidden_turned)
        full_down = place_chunks(*gathered[3 * layer + 2], place_table, (hidden_width, width))
        full_downs.append(full_down)
        branch_two = grouped(contract(hidden_turned, full_down, 0, 0) + down_b)
        saved_layers.append(
            dict(
                inputs=current,
                scale_one=scale_one,
                gate_one=gate_one,
                scale_two=scale_two,
                gate_two=gate_two,
                head_on=head_on,
                channel_on=channel_on,
                keep_tok=keep_tok,
                low_one=low_one,
                qkv_low=qkv_low,
                other_low=other_low,
                totals=totals,
                mixed_low=mixed_low,
                branch_one=branch_one,
                after_attn=after_attn,
                low_two=low_two,
                hidden_pre=hidden_pre,
                hidden_turned=hidden_turned,
                branch_two=branch_two,
            )
        )
        current = after_attn + keep_tok * gate_two * branch_two
    output = ungrouped(current).astype(BF)
    output = feed.finish(output)

    cond_rows = jnp.concatenate(
        [
            cond_every.reshape(seq_count, item_count, shard_rows),
            jnp.zeros((seq_count, 8 - item_count, shard_rows), BF),
        ],
        axis=1,
    ).reshape(seq_count * 8, shard_rows)
    cond_twice = jnp.concatenate([cond_rows, cond_rows], axis=0)
    grad_current = grouped(cotangent)
    layer_totals = [None] * layer_count
    for layer in reversed(range(layer_count)):
        saved = saved_layers[layer]
        kept_grad = grad_current * saved["keep_tok"]
        down_grad = ungrouped((kept_grad * saved["gate_two"]).astype(BF))
        grad_gate_two = jnp.sum(kept_grad * saved["branch_two"], axis=1)
        grad_down_bias = jnp.sum(down_grad.astype(F32), axis=0)
        down_rows, up_rows, out_rows, qkv_rows = [], [], [], []
        scatter_chunks(saved["hidden_turned"], down_grad, (1, 2, 2), down_rows)
        up_grad, grad_up_bias = hidden_back(
            down_grad, full_downs[layer], saved["hidden_pre"], saved["channel_on"], wide_tile(hidden_width) // 2
        )
        grad_up_bias = grad_up_bias[0]
        up_grad = feed.tick(up_grad)
        scatter_ordered(saved["low_two"], up_grad, (1, 2, 2), up_rows)
        grad_h2 = grouped(project_back(up_grad, up_tiles(layer), order, 2, "back_up"))
        grad_h2 = feed.tick(grad_h2)
        normed_two, inverse_two = normalize(saved["after_attn"])
        grad_shift_two = jnp.sum(grad_h2, axis=1)
        grad_scale_two = jnp.sum(grad_h2 * normed_two, axis=1)
        grad_after = grad_current + normalize_back(
            grad_h2 * (1.0 + saved["scale_two"]), normed_two, inverse_two
        )
        out_grad = ungrouped((grad_after * saved["gate_one"]).astype(BF))
        grad_gate_one = jnp.sum(grad_after * saved["branch_one"], axis=1)
        grad_out_bias = jnp.sum(out_grad.astype(F32), axis=0)
        out_grad = feed.tick(out_grad)
        scatter_ordered(saved["mixed_low"], out_grad, (1, 1, 1), out_rows)
        grad_mixed = ungrouped(
            (
                grouped(project_back(out_grad, out_tiles(layer), order, 1, "back_out"))
                * saved["head_on"][:, None]
            ).astype(BF)
        )
        grad_mixed = feed.tick(grad_mixed)
        grad_query, own_pair, other_pair = attend_back(
            saved["qkv_low"], saved["other_low"], grad_mixed, saved["totals"], key_mask, head_count
        )
        other_pair = feed.tick(other_pair)
        back_pair = swap_bit(other_pair, x_stage)
        grad_qkv = jnp.concatenate(
            [grad_query, (own_pair + back_pair.astype(F32)).astype(BF)], axis=1
        )
        grad_qkv = feed.tick(grad_qkv)
        grad_qkv_bias = jnp.sum(grad_qkv.astype(F32), axis=0)
        scatter_ordered(saved["low_one"], grad_qkv, (1, 2, 2), qkv_rows)
        grad_h1 = grouped(project_back(grad_qkv, qkv_tiles(layer), order, 2, "back_qkv"))
        grad_h1 = feed.tick(grad_h1)
        normed_one, inverse_one = normalize(saved["inputs"])
        grad_shift_one = jnp.sum(grad_h1, axis=1)
        grad_scale_one = jnp.sum(grad_h1 * normed_one, axis=1)
        grad_inputs = grad_after + normalize_back(
            grad_h1 * (1.0 + saved["scale_one"]), normed_one, inverse_one
        )
        grad_groups = jnp.concatenate(
            [
                grad_shift_one,
                grad_scale_one,
                grad_gate_one,
                grad_shift_two,
                grad_scale_two,
                grad_gate_two,
            ],
            axis=1,
        )
        grad_slots = jnp.sum(jnp.where(group_is[:, :, None], grad_groups[:, None, :], 0.0), axis=0)
        mod_width = grad_slots.shape[1]
        bias_row = jnp.concatenate(
            [
                grad_qkv_bias[:width],
                grad_qkv_bias[2 * width :],
                grad_out_bias,
                grad_up_bias,
                grad_down_bias,
            ]
        )
        spare = jnp.zeros(((8 - item_count) * mod_width - bias_row.shape[0],), F32)
        packet = jnp.concatenate(
            [grad_slots, jnp.concatenate([bias_row, spare]).reshape(8 - item_count, mod_width)],
            axis=0,
        ).astype(BF)
        every_packet = lax.all_gather(packet, AXES, axis=0, tiled=True)
        grad_mod_weight = contract(cond_twice, every_packet, 0, 0)
        packet_sum = jnp.sum(
            every_packet.astype(F32).reshape(device_count, 8, mod_width), axis=0
        )
        mod_cols = mod_bias.shape[1]
        grad_mod_bias = lax.dynamic_slice_in_dim(
            jnp.sum(packet_sum[:item_count], axis=0), flat_index * mod_cols, mod_cols, 0
        )
        bias_sum = packet_sum[item_count:].reshape(-1)
        parts = []
        start = 0
        for bias in (qv_bias, out_bias, up_bias, down_bias):
            columns = bias.shape[1]
            parts.append(
                lax.dynamic_slice_in_dim(bias_sum, start + flat_index * columns, columns, 0)
            )
            start += device_count * columns
        grad_current = grad_inputs
        layer_totals[layer] = (
            qkv_rows,
            out_rows,
            up_rows,
            down_rows,
            grad_mod_weight,
            *parts,
            grad_mod_bias,
        )
    grad_current = feed.finish(grad_current)
    layer_totals = [
        [part[0] if isinstance(part, list) else part for part in totals] for totals in layer_totals
    ]
    stacked = tuple(
        jnp.stack([layer_totals[layer][index] for layer in range(layer_count)])
        for index in range(10)
    )
    return (output, ungrouped(grad_current), *stacked)


def solution(mesh):
    rows = P(AXES, None)
    matrix = P(None, AXES, None)
    vector = P(None, AXES)
    return jax.shard_map(
        body,
        mesh=mesh,
        in_specs=(
            rows,
            matrix,
            matrix,
            matrix,
            matrix,
            matrix,
            vector,
            vector,
            vector,
            vector,
            vector,
            P("seq"),
            P("seq", None),
            P("seq", None, None, None),
            P("seq", None, None, None),
            rows,
            rows,
        ),
        out_specs=(
            rows,
            rows,
            matrix,
            matrix,
            matrix,
            matrix,
            matrix,
            vector,
            vector,
            vector,
            vector,
            vector,
        ),
        check_vma=False,
    )
```

time: 3300 us -> 1440 us (0.44)
  waiting for transfers between devices: 2350 us -> 374 us
  Pallas kernels: 0 us -> 407 us
  matrix products: 493 us -> 105 us
  starting transfers between devices: 11.8 us -> 126 us
  local copies, waits for them, and re-layouts: 127 us -> 196 us
  blocking collectives: 66.1 us -> 0 us
    unnamed x19 -> x2, waiting for transfers between devices: 1300 us -> 0.03 us
    reduce_scatter x2 -> x0, waiting for transfers between devices: 445 us -> none  [body(): lax.psum_scatter(contract_rows(hidden_low, down_grad), ('fsdp', 'seq'), s...]
    pallas_call x0 -> x32, Pallas kernels: none -> 407 us  [the longest x6 79.5 us: project_back(): pl.pallas_call(kernel, out_shape=out, grid=(tiles.count,), in_specs=[pl.B...]
    all_gather x10 -> x2, waiting for transfers between devices: 432 us -> 30.3 us  [body(): every_packet = lax.all_gather(packet, AXES, axis=0, tiled=True)]
    dot_general x92 -> x23, matrix products: 493 us -> 105 us  [the longest x20 102 us: contract(): lax.dot_general(left, right, (((left_dim,), (right_dim,)), ((), ())), pre...]
    ppermute x8 -> x135, waiting for transfers between devices: 180 us -> 344 us  [swap_bit(): lax.ppermute(block, axis, [(low, low ^ 1 << bit) for low in range(count)])]
    ppermute x8 -> x135, starting transfers between devices: 10.1 us -> 126 us  [swap_bit(): lax.ppermute(block, axis, [(low, low ^ 1 << bit) for low in range(count)])]
    unnamed x272 -> x481, local copies, waits for them, and re-layouts: 56.3 us -> 102 us
  transfers between devices with their start and end apart: 24 -> 137, of which waited for: 19 -> 36; matrix products, arithmetic and copies ran while one was open for 15% -> 29% of each run, Pallas kernels for 0% -> 27%
where the time goes in v1:
time: 1440 us; the launch traced here: 1430 us
  Pallas kernels  407 us (28%)
  waiting for transfers between devices  374 us (26%)
  other arithmetic  204 us (14%)
  local copies, waits for them, and re-layouts  196 us (14%)
  starting transfers between devices  126 us (9%)
  matrix products  105 us (7%)
  between operations  18 us (1%)
    ppermute x135, waiting for transfers between devices, swap_bit(): lax.ppermute(block, axis, [(low, low ^ 1 << bit) for low in range(count)])  344 us
    ppermute x135, starting transfers between devices, swap_bit(): lax.ppermute(block, axis, [(low, low ^ 1 << bit) for low in range(count)])  126 us
    unnamed x481, local copies, waits for them, and re-layouts  102 us
    dot_general x20, matrix products, contract(): lax.dot_general(left, right, (((left_dim,), (right_dim,)), ((), ())), pre...  102 us
    pallas_call x6, Pallas kernels, project_back(): pl.pallas_call(kernel, out_shape=out, grid=(tiles.count,), in_specs=[pl.B...  79.5 us
    pallas_call x2, Pallas kernels, attend_back(): pl.pallas_call(kernel, out_shape=outs, grid=(head_count,), in_specs=[pl.B...  76.8 us
    pallas_call x8, Pallas kernels, keep_grad(): pl.pallas_call(kernel, out_shape=outs, grid=(columns // tile,), in_specs=...  60.8 us
    pallas_call x2, Pallas kernels, attend(): pl.pallas_call(kernel, out_shape=[mixed, totals], grid=(head_count,), in_...  52.4 us
  transfers between devices with their start and end apart: 137, of which 36 were waited for; matrix products, arithmetic and copies ran while one was open for 29% of the time, Pallas kernels for 27%

profile of v1, /device:TPU:0, one launch (start us, length us, event | category | flops | bytes accessed | tf_op | source)
XLA Modules:
  0.0 1429.7 jit_solution(15460714092831651351)
XLA Ops:
  94.3 10.9 collective-permute-done.8
  124.7 18.7 %collective-permute-done.13 = f32[4,6912]{1,0:T(4,128)S(1)} collective-permute-done((f32[4,6912]{1,0:T(4,128)S(1)}, f32[4,6912]{1,0:T(4,128)S(1)}, u32[]{:S(2)}, u32[]{:S(2)}) %collective-permute-start.13) | collective-permute-done | bytes 110624 | tf_op jit(solution)/shard_map/ppermute | solution.py:18
  158.0 19.9 %collective-permute-done.16.refs_2_ = bf16[192,3456]{1,0:T(8,128)(2,1)S(1)} collective-permute-done((bf16[192,3456]{1,0:T(8,128)(2,1)S(1)}, bf16[192,3456]{1,0:T(8,128)(2,1)S(1)}, u32[]{:S(2)}, u32[]{:S(2)}) %collective-permute-start.16) | collective-permute-done | bytes 1327136 | tf_op jit(solution)/shard_map/ppermute | solution.py:18
  182.8 25.7 %collective-permute-done.27 = bf16[512,1152]{1,0:T(8,128)(2,1)S(1)} collective-permute-done((bf16[512,1152]{1,0:T(8,128)(2,1)S(1)}, bf16[512,1152]{1,0:T(8,128)(2,1)S(1)}, u32[]{:S(2)}, u32[]{:S(2)}) %collective-permute-start.27) | collective-permute-done | bytes 1179680 | tf_op jit(solution)/shard_map/ppermute | solution.py:18
  229.5 9.8 project_qkv.2.qkv_ref
  258.6 26.1 %attend.2 = (bf16[512,1152]{1,0:T(8,128)(2,1)}, f32[512,128]{1,0:T(8,128)}) custom-call(bf16[512,3456]{1,0:T(8,128)(2,1)} %project_qkv.2.qkv_ref, bf16[512,2304]{1,0:T(8,128)(2,1)} %project_pair.2.other_ref, f32[2,1152]{1,0:T(2,128)} %broadcast_in_dim.251.head_ref, f32[2,1024]{1,0:T(2,128)} %bitcast.330), custom_call_target="tpu_custom_call" | custom-call | flops 8589934592 | bytes 7077888 | tf_op jit(solution)/shard_map/attend/pallas_call | solution.py:537
  358.3 14.5 %project_up.2 = (f32[512,4608]{1,0:T(8,128)}, bf16[4608,512]{1,0:T(8,128)(2,1)}) custom-call(bf16[512,1280]{1,0:T(8,128)(2,1)} %fusion.12.left_ref, f32[1,4608]{1,0:T(1,128)} %reshape_reshape.13.bias_ref, f32[2,4608]{1,0:T(2,128)} %get-tuple-element.529.channel_ref, bf16[192,5760]{1,0:T(8,128)(2,1)} %copy-done.17, ...), custom_call_target="tpu_custom_call" | custom-call | flops 6039797760 | bytes 30212096 | tf_op jit(solution)/shard_map/project_up/pallas_call | solution.py:371
  405.4 12.9 fusion.101
  426.5 9.1 collective-permute-done.54
  447.4 12.1 collective-permute-done.61
  484.3 9.8 project_qkv.3.qkv_ref
  494.1 26.3 %attend.3 = (bf16[512,1152]{1,0:T(8,128)(2,1)}, f32[512,128]{1,0:T(8,128)}) custom-call(bf16[512,3456]{1,0:T(8,128)(2,1)} %project_qkv.3.qkv_ref, bf16[512,2304]{1,0:T(8,128)(2,1)} %project_pair.3.other_ref, f32[2,1152]{1,0:T(2,128)} %broadcast_in_dim.262.head_ref, f32[2,1024]{1,0:T(2,128)} %bitcast.331), custom_call_target="tpu_custom_call" | custom-call | flops 8589934592 | bytes 7077888 | tf_op jit(solution)/shard_map/attend/pallas_call | solution.py:537
  556.3 14.5 %project_up.3 = (f32[512,4608]{1,0:T(8,128)}, bf16[4608,512]{1,0:T(8,128)(2,1)}) custom-call(bf16[512,1280]{1,0:T(8,128)(2,1)} %fusion.16.left_ref, f32[1,4608]{1,0:T(1,128)} %reshape_reshape.15.bias_ref, f32[2,4608]{1,0:T(2,128)} %get-tuple-element.528.channel_ref, bf16[192,5760]{1,0:T(8,128)(2,1)} %constant_dynamic-update-slice_fusion.40.refs_0_, ...), custom_call_target="tpu_custom_call" | custom-call | flops 6039797760 | bytes 30212096 | tf_op jit(solution)/shard_map/project_up/pallas_call | solution.py:371
  601.6 16.2 %hidden_back.2 = (bf16[512,4608]{1,0:T(8,128)(2,1)}, f32[1,4608]{1,0:T(1,128)}) custom-call(bf16[512,1152]{1,0:T(8,128)(2,1)} %get-tuple-element.541.grad_ref.right_ref, bf16[4608,1152]{1,0:T(8,128)(2,1)} %bitcast.291, f32[512,4608]{1,0:T(8,128)} %get-tuple-element.319.pre_ref, f32[2,4608]{1,0:T(2,128)} %get-tuple-element.528.channel_ref), custom_call_target="tpu_custom_call" | custom-call | flops 5435817984 | bytes 25952256 | tf_op jit(solution)/shard_map/hidden_back/pallas_call | solution.py:463
  680.6 16.4 %back_up.2 = f32[512,1152]{1,0:T(8,128)} custom-call(bf16[512,4608]{1,0:T(8,128)(2,1)} %get-tuple-element.322.right_ref, bf16[1280,1152]{1,0:T(8,128)(2,1)} %fusion.order_ref, bf16[192,5760]{1,0:T(8,128)(2,1)} %constant_dynamic-update-slice_fusion.40.refs_0_, bf16[128,5760]{1,0:T(8,128)(2,1)} %constant_dynamic-update-slice_fusion.45.refs_1_, ...), custom_call_target="tpu_custom_call" | custom-call | flops 9059696640 | bytes 24772608 | tf_op jit(solution)/shard_map/back_up/pallas_call | solution.py:420
  710.3 9.4 keep_grad.9
  727.4 12.6 fusion.27
  758.9 10.8 collective-permute-done.82
  779.8 38.5 %attend_back.2 = (bf16[512,1152]{1,0:T(8,128)(2,1)}, f32[512,2304]{1,0:T(8,128)}, bf16[512,2304]{1,0:T(8,128)(2,1)}) custom-call(bf16[512,3456]{1,0:T(8,128)(2,1)} %project_qkv.3.qkv_ref, bf16[512,2304]{1,0:T(8,128)(2,1)} %project_pair.3.other_ref, bf16[512,1152]{1,0:T(8,128)(2,1)} %fusion.30.grad_ref, f32[16,512]{1,0:T(8,128)} %slice_bitcast_fusion.3.totals_ref, ...), custom_call_target="tpu_custom_call" | custom-call | flops 21474836480 | bytes 15376384 | tf_op jit(solution)/shard_map/attend_back/pallas_call | solution.py:609
  832.7 40.1 %collective-permute-done.88 = bf16[512,2304]{1,0:T(8,128)(2,1)S(1)} collective-permute-done((bf16[512,2304]{1,0:T(8,128)(2,1)}, bf16[512,2304]{1,0:T(8,128)(2,1)S(1)}, u32[]{:S(2)}, u32[]{:S(2)}) %collective-permute-start.88) | collective-permute-done | bytes 2359328 | tf_op jit(solution)/shard_map/ppermute | solution.py:18
  904.9 15.1 %back_qkv.2 = f32[512,1152]{1,0:T(8,128)} custom-call(bf16[512,3456]{1,0:T(8,128)(2,1)} %copy-done.3, bf16[1280,1152]{1,0:T(8,128)(2,1)} %fusion.order_ref, bf16[192,3456]{1,0:T(8,128)(2,1)} %constant_dynamic-update-slice_fusion.30.refs_0_, bf16[128,3456]{1,0:T(8,128)(2,1)} %constant_dynamic-update-slice_fusion.35.refs_1_, ...), custom_call_target="tpu_custom_call" | custom-call | flops 7549747200 | bytes 17694720 | tf_op jit(solution)/shard_map/back_qkv/pallas_call | solution.py:420
  960.7 16.3 %hidden_back.3 = (bf16[512,4608]{1,0:T(8,128)(2,1)}, f32[1,4608]{1,0:T(1,128)}) custom-call(bf16[512,1152]{1,0:T(8,128)(2,1)} %bitcast.312, bf16[4608,1152]{1,0:T(8,128)(2,1)} %bitcast.290, f32[512,4608]{1,0:T(8,128)} %get-tuple-element.359.pre_ref, f32[2,4608]{1,0:T(2,128)} %get-tuple-element.529.channel_ref), custom_call_target="tpu_custom_call" | custom-call | flops 5435817984 | bytes 25952256 | tf_op jit(solution)/shard_map/hidden_back/pallas_call | solution.py:463
  1006.8 16.7 %back_up.3 = f32[512,1152]{1,0:T(8,128)} custom-call(bf16[512,4608]{1,0:T(8,128)(2,1)} %get-tuple-element.364.right_ref, bf16[1280,1152]{1,0:T(8,128)(2,1)} %fusion.order_ref, bf16[192,5760]{1,0:T(8,128)(2,1)} %copy-done.17, bf16[128,5760]{1,0:T(8,128)(2,1)} %constant_dynamic-update-slice_fusion.15.refs_1_, ...), custom_call_target="tpu_custom_call" | custom-call | flops 9059696640 | bytes 24772608 | tf_op jit(solution)/shard_map/back_up/pallas_call | solution.py:420
  1035.3 9.8 keep_grad.13
  1069.7 24.9 %collective-permute-done.107 = bf16[64,3456]{1,0:T(8,128)(2,1)S(1)} collective-permute-done((bf16[64,3456]{1,0:T(8,128)(2,1)S(1)}, bf16[64,3456]{1,0:T(8,128)(2,1)S(1)}, u32[]{:S(2)}, u32[]{:S(2)}) %collective-permute-start.107) | collective-permute-done | bytes 442400 | tf_op jit(solution)/shard_map/ppermute | solution.py:18
  1108.1 38.3 %attend_back.3 = (bf16[512,1152]{1,0:T(8,128)(2,1)}, f32[512,2304]{1,0:T(8,128)}, bf16[512,2304]{1,0:T(8,128)(2,1)}) custom-call(bf16[512,3456]{1,0:T(8,128)(2,1)} %project_qkv.2.qkv_ref, bf16[512,2304]{1,0:T(8,128)(2,1)} %project_pair.2.other_ref, bf16[512,1152]{1,0:T(8,128)(2,1)} %fusion.29.grad_ref, f32[16,512]{1,0:T(8,128)} %slice_bitcast_fusion.2.totals_ref, ...), custom_call_target="tpu_custom_call" | custom-call | flops 21474836480 | bytes 15376384 | tf_op jit(solution)/shard_map/attend_back/pallas_call | solution.py:609
  1164.8 56.6 %collective-permute-done.116 = bf16[512,2304]{1,0:T(8,128)(2,1)S(1)} collective-permute-done((bf16[512,2304]{1,0:T(8,128)(2,1)S(1)}, bf16[512,2304]{1,0:T(8,128)(2,1)S(1)}, u32[]{:S(2)}, u32[]{:S(2)}) %collective-permute-start.116) | collective-permute-done | bytes 2359328 | tf_op jit(solution)/shard_map/ppermute | solution.py:18
  1245.7 15.1 %back_qkv.3 = f32[512,1152]{1,0:T(8,128)} custom-call(bf16[512,3456]{1,0:T(8,128)(2,1)} %copy-done.2, bf16[1280,1152]{1,0:T(8,128)(2,1)} %fusion.order_ref, bf16[192,3456]{1,0:T(8,128)(2,1)} %copy-done.53, bf16[128,3456]{1,0:T(8,128)(2,1)} %copy-done.75, bf16[192,3456]{1,0:T(8,128)(2,1)} %copy-done.64, bf16[128,3456]{1,0:T(8,128)(2,1)} %copy-done.79, ...), custom_call_target="tpu_custom_call" | custom-call | flops 7549747200 | bytes 17694720 | tf_op jit(solution)/shard_map/back_qkv/pallas_call | solution.py:420
  1314.8 10.0 collective-permute-done.130
  1324.8 12.0 collective-permute-done.129
  1353.1 11.9 collective-permute-done.133
  1380.0 30.3 %all-gather.3.cloned.1.call-done = bf16[256,6912]{1,0:T(8,128)(2,1)} async-done(((bf16[8,6912]{1,0:T(8,128)(2,1)}), bf16[256,6912]{1,0:T(8,128)(2,1)}) %all-gather.3.cloned.1.call-update) | async-done | bytes 3538960 | tf_op jit(solution)/shard_map/all_gather | solution.py:1038
  (1096 shorter events, 800.4 us)
Async XLA Ops:
  7.2 1370.1 %all-gather.5.cloned.1.call-start = ((), (), s32[]{:S(2)}) async-start(), calls=%async_computation.1 | async-start | bytes 3649536 | tf_op jit(solution)/shard_map/all_gather | solution.py:1038
  41.3 63.9 %collective-permute-start.9 = (bf16[40,5760]{1,0:T(8,128)(2,1)}, bf16[40,5760]{1,0:T(8,128)(2,1)}, u32[]{:S(2)}, u32[]{:S(2)}) collective-permute-start(bf16[40,5760]{1,0:T(8,128)(2,1)} %fusion.55), channel_id=1, source_target_pairs={{0,8},{1,9},{2,10},{3,11},{4,12},{5,13},{6,14},{7,15},{8,0},{9,1},... | collective-permute-start | bytes 1382408 | tf_op jit(solution)/shard_map/ppermute | solution.py:18
  68.2 88.2 %collective-permute-start.18 = (f32[32,6912]{1,0:T(8,128)}, f32[32,6912]{1,0:T(8,128)}, u32[]{:S(2)}, u32[]{:S(2)}) collective-permute-start(f32[32,6912]{1,0:T(8,128)} %slice.1492), channel_id=1, source_target_pairs={{0,1},{1,0},{2,3},{3,2},{4,5},{5,4},{6,7},{7,6},{8,9},{9,8},{10,11... | collective-permute-start | bytes 2654216 | tf_op jit(solution)/shard_map/ppermute | solution.py:18
  114.2 65.1 %collective-permute-start.24 = (bf16[128,3456]{1,0:T(8,128)(2,1)S(1)}, bf16[128,3456]{1,0:T(8,128)(2,1)S(1)}, u32[]{:S(2)}, u32[]{:S(2)}) collective-permute-start(bf16[128,3456]{1,0:T(8,128)(2,1)S(1)} %constant_dynamic-update-slice_fusion.5.refs_1_), channel_id=1, source_target_pairs={{0,1},{1,0},{2,3},{3,2},{4,5},{5,4},{6,7},{7,6},{8,9},{9,8},{10,11... | collective-permute-start | bytes 2654216 | tf_op jit(solution)/shard_map/ppermute | solution.py:18
  156.4 63.8 %collective-permute-start.19 = (bf16[96,5760]{1,0:T(8,128)(2,1)S(1)}, bf16[96,5760]{1,0:T(8,128)(2,1)S(1)}, u32[]{:S(2)}, u32[]{:S(2)}) collective-permute-start(bf16[96,5760]{1,0:T(8,128)(2,1)S(1)} %pad_maximum_fusion.5), channel_id=1, source_target_pairs={{0,16},{16,0},{1,17},{17,1},{2,18},{18,2},{3,19},{19,3},{4,20},{20... | collective-permute-start | bytes 3317768 | tf_op jit(solution)/shard_map/ppermute | solution.py:18
  224.6 73.2 %collective-permute-start.30 = (bf16[192,5760]{1,0:T(8,128)(2,1)S(1)}, bf16[192,5760]{1,0:T(8,128)(2,1)}, u32[]{:S(2)}, u32[]{:S(2)}) collective-permute-start(bf16[192,5760]{1,0:T(8,128)(2,1)S(1)} %constant_dynamic-update-slice_fusion.10.refs_0_), channel_id=1, source_target_pairs={{0,2},{1,3},{2,0},{3,1},{4,6},{5,7},{6,4},{7,5},{8,10},{9,11},{10,... | collective-permute-start | bytes 6635528 | tf_op jit(solution)/shard_map/ppermute | solution.py:18
  227.2 70.7 %collective-permute-start.31 = (bf16[128,5760]{1,0:T(8,128)(2,1)}, bf16[128,5760]{1,0:T(8,128)(2,1)}, u32[]{:S(2)}, u32[]{:S(2)}) collective-permute-start(bf16[128,5760]{1,0:T(8,128)(2,1)} %constant_dynamic-update-slice_fusion.15.refs_1_), channel_id=1, source_target_pairs={{0,16},{16,0},{1,17},{17,1},{2,18},{18,2},{3,19},{19,3},{4,20},{20... | collective-permute-start | bytes 4423688 | tf_op jit(solution)/shard_map/ppermute | solution.py:18
  320.0 54.6 %collective-permute-start.43 = (bf16[576,1152]{1,0:T(8,128)(2,1)}, bf16[576,1152]{1,0:T(8,128)(2,1)}, u32[]{:S(2)}, u32[]{:S(2)}) collective-permute-start(bf16[576,1152]{1,0:T(8,128)(2,1)} %constant_dynamic-update-slice_fusion.20), channel_id=1, source_target_pairs={{0,2},{1,3},{2,0},{3,1},{4,6},{5,7},{6,4},{7,5},{8,10},{9,11},{10,... | collective-permute-start | bytes 3981320 | tf_op jit(solution)/shard_map/ppermute | solution.py:18
  321.5 53.1 %collective-permute-start.44 = (bf16[576,1152]{1,0:T(8,128)(2,1)}, bf16[576,1152]{1,0:T(8,128)(2,1)}, u32[]{:S(2)}, u32[]{:S(2)}) collective-permute-start(bf16[576,1152]{1,0:T(8,128)(2,1)} %constant_dynamic-update-slice_fusion.25), channel_id=1, source_target_pairs={{0,16},{16,0},{1,17},{17,1},{2,18},{18,2},{3,19},{19,3},{4,20},{20... | collective-permute-start | bytes 3981320 | tf_op jit(solution)/shard_map/ppermute | solution.py:18
  377.7 57.8 %collective-permute-start.52 = (bf16[192,3456]{1,0:T(8,128)(2,1)}, bf16[192,3456]{1,0:T(8,128)(2,1)}, u32[]{:S(2)}, u32[]{:S(2)}) collective-permute-start(bf16[192,3456]{1,0:T(8,128)(2,1)} %constant_dynamic-update-slice_fusion.30.refs_0_), channel_id=1, source_target_pairs={{0,2},{1,3},{2,0},{3,1},{4,6},{5,7},{6,4},{7,5},{8,10},{9,11},{10,... | collective-permute-start | bytes 3981320 | tf_op jit(solution)/shard_map/ppermute | solution.py:18
  464.7 63.2 %collective-permute-start.63 = (bf16[192,5760]{1,0:T(8,128)(2,1)}, bf16[192,5760]{1,0:T(8,128)(2,1)}, u32[]{:S(2)}, u32[]{:S(2)}) collective-permute-start(bf16[192,5760]{1,0:T(8,128)(2,1)} %constant_dynamic-update-slice_fusion.40.refs_0_), channel_id=1, source_target_pairs={{0,2},{1,3},{2,0},{3,1},{4,6},{5,7},{6,4},{7,5},{8,10},{9,11},{10,... | collective-permute-start | bytes 6635528 | tf_op jit(solution)/shard_map/ppermute | solution.py:18
  467.2 74.6 %collective-permute-start.67 = (bf16[192,5760]{1,0:T(8,128)(2,1)}, bf16[192,5760]{1,0:T(8,128)(2,1)}, u32[]{:S(2)}, u32[]{:S(2)}) collective-permute-start(bf16[192,5760]{1,0:T(8,128)(2,1)} %constant_dynamic-update-slice_fusion.40.refs_0_), channel_id=1, source_target_pairs={{0,1},{1,0},{2,3},{3,2},{4,5},{5,4},{6,7},{7,6},{8,9},{9,8},{10,11... | collective-permute-start | bytes 6635528 | tf_op jit(solution)/shard_map/ppermute | solution.py:18
  468.2 52.2 %collective-permute-start.64 = (bf16[128,5760]{1,0:T(8,128)(2,1)}, bf16[128,5760]{1,0:T(8,128)(2,1)}, u32[]{:S(2)}, u32[]{:S(2)}) collective-permute-start(bf16[128,5760]{1,0:T(8,128)(2,1)} %constant_dynamic-update-slice_fusion.45.refs_1_), channel_id=1, source_target_pairs={{0,16},{16,0},{1,17},{17,1},{2,18},{18,2},{3,19},{19,3},{4,20},{20... | collective-permute-start | bytes 4423688 | tf_op jit(solution)/shard_map/ppermute | solution.py:18
  626.2 70.7 %collective-permute-start.78 = (bf16[640,4608]{1,0:T(8,128)(2,1)}, bf16[640,4608]{1,0:T(8,128)(2,1)}, u32[]{:S(2)}, u32[]{:S(2)}) collective-permute-start(bf16[640,4608]{1,0:T(8,128)(2,1)} %convolution_convert_fusion.3), channel_id=1, source_target_pairs={{0,1},{1,0},{2,3},{3,2},{4,5},{5,4},{6,7},{7,6},{8,9},{9,8},{10,11... | collective-permute-start | bytes 17694728 | tf_op jit(solution)/shard_map/ppermute | solution.py:18
  757.8 60.6 %collective-permute-start.84 = (bf16[288,1152]{1,0:T(8,128)(2,1)}, bf16[288,1152]{1,0:T(8,128)(2,1)}, u32[]{:S(2)}, u32[]{:S(2)}) collective-permute-start(bf16[288,1152]{1,0:T(8,128)(2,1)} %get-tuple-element.563), channel_id=1, source_target_pairs={{0,16},{16,0},{1,17},{17,1},{2,18},{18,2},{3,19},{19,3},{4,20},{20... | collective-permute-start | bytes 1990664 | tf_op jit(solution)/shard_map/ppermute | solution.py:18
  758.4 60.0 %collective-permute-start.85 = (bf16[288,1152]{1,0:T(8,128)(2,1)}, bf16[288,1152]{1,0:T(8,128)(2,1)}, u32[]{:S(2)}, u32[]{:S(2)}) collective-permute-start(bf16[288,1152]{1,0:T(8,128)(2,1)} %get-tuple-element.576), channel_id=1, source_target_pairs={{0,2},{1,3},{2,0},{3,1},{4,6},{5,7},{6,4},{7,5},{8,10},{9,11},{10,... | collective-permute-start | bytes 1990664 | tf_op jit(solution)/shard_map/ppermute | solution.py:18
  779.3 98.6 %collective-permute-start.89 = (bf16[96,4608]{1,0:T(8,128)(2,1)}, bf16[96,4608]{1,0:T(8,128)(2,1)}, u32[]{:S(2)}, u32[]{:S(2)}) collective-permute-start(bf16[96,4608]{1,0:T(8,128)(2,1)} %get-tuple-element.553), channel_id=1, source_target_pairs={{0,16},{16,0},{1,17},{17,1},{2,18},{18,2},{3,19},{19,3},{4,20},{20... | collective-permute-start | bytes 2654216 | tf_op jit(solution)/shard_map/ppermute | solution.py:18
  818.4 54.3 %collective-permute-start.88 = (bf16[512,2304]{1,0:T(8,128)(2,1)}, bf16[512,2304]{1,0:T(8,128)(2,1)S(1)}, u32[]{:S(2)}, u32[]{:S(2)}) collective-permute-start(bf16[512,2304]{1,0:T(8,128)(2,1)} %get-tuple-element.343), channel_id=1, source_target_pairs={{0,16},{16,0},{1,17},{17,1},{2,18},{18,2},{3,19},{19,3},{4,20},{20... | collective-permute-start | bytes 7077896 | tf_op jit(solution)/shard_map/ppermute | solution.py:18
  822.7 53.1 %collective-permute-start.90 = (bf16[64,4608]{1,0:T(8,128)(2,1)S(1)}, bf16[64,4608]{1,0:T(8,128)(2,1)S(1)}, u32[]{:S(2)}, u32[]{:S(2)}) collective-permute-start(bf16[64,4608]{1,0:T(8,128)(2,1)S(1)} %get-tuple-element.557), channel_id=1, source_target_pairs={{0,2},{1,3},{2,0},{3,1},{4,6},{5,7},{6,4},{7,5},{8,10},{9,11},{10,... | collective-permute-start | bytes 1769480 | tf_op jit(solution)/shard_map/ppermute | solution.py:18
  951.5 72.0 %collective-permute-start.101 = (bf16[192,3456]{1,0:T(8,128)(2,1)}, bf16[192,3456]{1,0:T(8,128)(2,1)}, u32[]{:S(2)}, u32[]{:S(2)}) collective-permute-start(bf16[192,3456]{1,0:T(8,128)(2,1)} %get-tuple-element.366), channel_id=1, source_target_pairs={{0,2},{1,3},{2,0},{3,1},{4,6},{5,7},{6,4},{7,5},{8,10},{9,11},{10,... | collective-permute-start | bytes 3981320 | tf_op jit(solution)/shard_map/ppermute | solution.py:18
  953.0 70.4 %collective-permute-start.102 = (bf16[128,3456]{1,0:T(8,128)(2,1)}, bf16[128,3456]{1,0:T(8,128)(2,1)}, u32[]{:S(2)}, u32[]{:S(2)}) collective-permute-start(bf16[128,3456]{1,0:T(8,128)(2,1)} %get-tuple-element.367), channel_id=1, source_target_pairs={{0,16},{16,0},{1,17},{17,1},{2,18},{18,2},{3,19},{19,3},{4,20},{20... | collective-permute-start | bytes 2654216 | tf_op jit(solution)/shard_map/ppermute | solution.py:18
  1034.8 61.3 %collective-permute-start.106 = (bf16[96,3456]{1,0:T(8,128)(2,1)}, bf16[96,3456]{1,0:T(8,128)(2,1)}, u32[]{:S(2)}, u32[]{:S(2)}) collective-permute-start(bf16[96,3456]{1,0:T(8,128)(2,1)} %get-tuple-element.569), channel_id=1, source_target_pairs={{0,16},{16,0},{1,17},{17,1},{2,18},{18,2},{3,19},{19,3},{4,20},{20... | collective-permute-start | bytes 1990664 | tf_op jit(solution)/shard_map/ppermute | solution.py:18
  1045.1 52.5 %collective-permute-start.108 = (bf16[192,4608]{1,0:T(8,128)(2,1)}, bf16[192,4608]{1,0:T(8,128)(2,1)}, u32[]{:S(2)}, u32[]{:S(2)}) collective-permute-start(bf16[192,4608]{1,0:T(8,128)(2,1)} %get-tuple-element.378), channel_id=1, source_target_pairs={{0,2},{1,3},{2,0},{3,1},{4,6},{5,7},{6,4},{7,5},{8,10},{9,11},{10,... | collective-permute-start | bytes 5308424 | tf_op jit(solution)/shard_map/ppermute | solution.py:18
  1094.6 56.4 %collective-permute-start.111 = (bf16[288,1152]{1,0:T(8,128)(2,1)}, bf16[288,1152]{1,0:T(8,128)(2,1)}, u32[]{:S(2)}, u32[]{:S(2)}) collective-permute-start(bf16[288,1152]{1,0:T(8,128)(2,1)} %get-tuple-element.559), channel_id=1, source_target_pairs={{0,16},{16,0},{1,17},{17,1},{2,18},{18,2},{3,19},{19,3},{4,20},{20... | collective-permute-start | bytes 1990664 | tf_op jit(solution)/shard_map/ppermute | solution.py:18
  1096.1 56.5 %collective-permute-start.112 = (bf16[288,1152]{1,0:T(8,128)(2,1)}, bf16[288,1152]{1,0:T(8,128)(2,1)}, u32[]{:S(2)}, u32[]{:S(2)}) collective-permute-start(bf16[288,1152]{1,0:T(8,128)(2,1)} %get-tuple-element.574), channel_id=1, source_target_pairs={{0,2},{1,3},{2,0},{3,1},{4,6},{5,7},{6,4},{7,5},{8,10},{9,11},{10,... | collective-permute-start | bytes 1990664 | tf_op jit(solution)/shard_map/ppermute | solution.py:18
  1101.2 52.8 %collective-permute-start.113 = (bf16[80,3456]{1,0:T(8,128)(2,1)}, bf16[80,3456]{1,0:T(8,128)(2,1)}, u32[]{:S(2)}, u32[]{:S(2)}) collective-permute-start(bf16[80,3456]{1,0:T(8,128)(2,1)} %pad_maximum_fusion.30), channel_id=1, source_target_pairs={{0,4},{1,5},{2,6},{3,7},{4,0},{5,1},{6,2},{7,3},{8,12},{9,13},{10,... | collective-permute-start | bytes 1658888 | tf_op jit(solution)/shard_map/ppermute | solution.py:18
  1151.0 77.7 %collective-permute-start.117 = (bf16[96,4608]{1,0:T(8,128)(2,1)S(1)}, bf16[96,4608]{1,0:T(8,128)(2,1)S(1)}, u32[]{:S(2)}, u32[]{:S(2)}) collective-permute-start(bf16[96,4608]{1,0:T(8,128)(2,1)S(1)} %get-tuple-element.551), channel_id=1, source_target_pairs={{0,16},{16,0},{1,17},{17,1},{2,18},{18,2},{3,19},{19,3},{4,20},{20... | collective-permute-start | bytes 2654216 | tf_op jit(solution)/shard_map/ppermute | solution.py:18
  1152.6 70.9 %collective-permute-start.118 = (bf16[64,4608]{1,0:T(8,128)(2,1)S(1)}, bf16[64,4608]{1,0:T(8,128)(2,1)S(1)}, u32[]{:S(2)}, u32[]{:S(2)}) collective-permute-start(bf16[64,4608]{1,0:T(8,128)(2,1)S(1)} %get-tuple-element.555), channel_id=1, source_target_pairs={{0,2},{1,3},{2,0},{3,1},{4,6},{5,7},{6,4},{7,5},{8,10},{9,11},{10,... | collective-permute-start | bytes 1769480 | tf_op jit(solution)/shard_map/ppermute | solution.py:18
  1154.0 67.4 %collective-permute-start.116 = (bf16[512,2304]{1,0:T(8,128)(2,1)S(1)}, bf16[512,2304]{1,0:T(8,128)(2,1)S(1)}, u32[]{:S(2)}, u32[]{:S(2)}) collective-permute-start(bf16[512,2304]{1,0:T(8,128)(2,1)S(1)} %copy-done.196), channel_id=1, source_target_pairs={{0,16},{16,0},{1,17},{17,1},{2,18},{18,2},{3,19},{19,3},{4,20},{20... | collective-permute-start | bytes 7077896 | tf_op jit(solution)/shard_map/ppermute | solution.py:18
  1157.6 71.1 %collective-permute-start.119 = (bf16[288,1152]{1,0:T(8,128)(2,1)S(1)}, bf16[288,1152]{1,0:T(8,128)(2,1)S(1)}, u32[]{:S(2)}, u32[]{:S(2)}) collective-permute-start(bf16[288,1152]{1,0:T(8,128)(2,1)S(1)} %pad_maximum_fusion.25), channel_id=1, source_target_pairs={{0,4},{1,5},{2,6},{3,7},{4,0},{5,1},{6,2},{7,3},{8,12},{9,13},{10,... | collective-permute-start | bytes 1990664 | tf_op jit(solution)/shard_map/ppermute | solution.py:18
  1159.8 68.8 %collective-permute-start.120 = (bf16[40,3456]{1,0:T(8,128)(2,1)S(1)}, bf16[40,3456]{1,0:T(8,128)(2,1)S(1)}, u32[]{:S(2)}, u32[]{:S(2)}) collective-permute-start(bf16[40,3456]{1,0:T(8,128)(2,1)S(1)} %pad_maximum_fusion.39), channel_id=1, source_target_pairs={{0,8},{1,9},{2,10},{3,11},{4,12},{5,13},{6,14},{7,15},{8,0},{9,1},... | collective-permute-start | bytes 829448 | tf_op jit(solution)/shard_map/ppermute | solution.py:18
  1271.8 138.4 %all-gather.3.cloned.1.call-start = ((), (), s32[]{:S(2)}) async-start(), calls=%async_computation | async-start | bytes 3649536 | tf_op jit(solution)/shard_map/all_gather | solution.py:1038
  (307 other events, 4582.7 us)
Sparse Core Ops, SparseCore 0:
  1271.9 73.9 all-gather.4
  1349.4 60.7 all-gather.2

commit v2 on v1

--- a/solution.py
+++ b/solution.py
@@ -76,12 +76,16 @@
         return value
 
 
-def reduce_flight(away, stay, right, side, routes, cuts, rows, waits, result):
+def reduce_flight(grads, routes, cuts, rows, waits, result):
     core_stage, first_route, second_route, far_stages = routes
     first, second = cuts
-    arrived = yield waits[0], swap_bit(contract(away, right, side, 0).astype(BF), core_stage)
-    kept, first_sent, second_sent = keep_grad(stay, right, side, arrived, first, second)
-    first_arrived, second_arrived = yield waits[1], (
+    waits = list(waits) + [1] * 8
+    arrived = yield waits[0], swap_bit(grads.away(), core_stage)
+    parts = grads.stay(arrived, first, second)
+    if waits[1]:
+        parts = yield waits[1], parts
+    kept, first_sent, second_sent = parts
+    first_arrived, second_arrived = yield waits[2], (
         swap_bit(first_sent, first_route[0]),
         swap_bit(second_sent, second_route[0]),
     )
@@ -95,7 +99,7 @@
     second_sent = add(second_kept, second_arrived, half_second, second).astype(BF)
     first_kept = add(first_kept, first_arrived, 0, half_first).astype(BF)
     second_kept = add(second_kept, second_arrived, 0, half_second).astype(BF)
-    first_arrived, second_arrived = yield waits[2], (
+    first_arrived, second_arrived = yield waits[3], (
         swap_bit(first_sent, first_route[1]),
         swap_bit(second_sent, second_route[1]),
     )
@@ -111,7 +115,7 @@
         ).astype(BF)
         first_kept = add(first_kept, first_arrived, 0, half_first).astype(BF)
         second_kept = add(second_kept, second_arrived, 0, half_second).astype(BF)
-        arrived = yield 1, swap_bit(sent, stage)
+        arrived = yield waits[4 + index], swap_bit(sent, stage)
         first_arrived, second_arrived = arrived[:half_first], arrived[half_first:]
     block = jnp.concatenate(
         [
@@ -123,48 +127,132 @@
     result.append(block[:rows])
 
 
+class ColumnGrads:
+    def __init__(self, lefts, rights, tile):
+        self.lefts, self.rights, self.tile = lefts, rights, tile
+        self.half = lefts[0].shape[1] // 2
+        self.counts = [right.shape[1] // tile for right in rights]
+
+    def call(self, index, arrived, pieces, name):
+        half, tile = self.half, self.tile
+        tokens = self.lefts[0].shape[0]
+        pairs = len(self.lefts)
+        starts = [sum(self.counts[:pair]) for pair in range(pairs)]
+        columns = sum(self.counts) * tile
+
+        def kernel(*refs):
+            lefts, rights = refs[:pairs], refs[pairs : 2 * pairs]
+            rest = refs[2 * pairs :]
+            if arrived is not None:
+                arrived_ref, rest = rest[0], rest[1:]
+            out_refs, turned_ref = rest[:-1], rest[-1]
+            step = pl.program_id(0)
+
+            def work(left_ref, right_ref, start):
+                @pl.when(step == start)
+                def _():
+                    turned_ref[...] = left_ref[...].astype(F32).T.astype(BF)
+
+                total = jnp.dot(turned_ref[...], right_ref[...], preferred_element_type=F32)
+                if arrived is not None:
+                    total = total + arrived_ref[...].astype(F32)
+                total = total.astype(BF)
+                low = 0
+                for out_ref, count in zip(out_refs, pieces):
+                    out_ref[...] = total[low : low + count]
+                    low += count
+
+            for left_ref, right_ref, start, count in zip(lefts, rights, starts, self.counts):
+                if pairs == 1:
+                    work(left_ref, right_ref, start)
+                else:
+                    pl.when((step >= start) & (step < start + count))(
+                        lambda l=left_ref, r=right_ref, s=start: work(l, r, s)
+                    )
+
+        def right_spec(start, count):
+            return pl.BlockSpec(
+                (tokens, tile), lambda j: (0, jnp.clip(j - start, 0, count - 1))
+            )
+
+        operands = [*self.lefts, *self.rights]
+        in_specs = [pl.BlockSpec((tokens, half), lambda j: (0, index)) for _ in self.lefts]
+        in_specs += [right_spec(*pair) for pair in zip(starts, self.counts)]
+        if arrived is not None:
+            operands.append(arrived)
+            in_specs.append(pl.BlockSpec((half, tile), lambda j: (0, j)))
+        outs = [jax.ShapeDtypeStruct((count, columns), BF) for count in pieces]
+        return pl.pallas_call(
+            kernel,
+            out_shape=outs,
+            grid=(sum(self.counts),),
+            in_specs=in_specs,
+            out_specs=[pl.BlockSpec((count, tile), lambda j: (0, j)) for count in pieces],
+            scratch_shapes=[pltpu.VMEM((half, tokens), BF)],
+            cost_estimate=cost(2 * half * tokens * columns, [*operands, *outs]),
+            name=name,
+        )(*operands)
+
+    def away(self):
+        return self.call(1, None, [self.half], "away_grad")[0]
+
+    def stay(self, arrived, first, second):
+        return self.call(0, arrived, [self.half - first - second, first, second], "stay_grad")
+
+
+class RowGrads:
+    def __init__(self, stay, away, right):
+        self.stay_rows, self.away_rows, self.right = stay, away, right
+
+    def away(self):
+        return contract(self.away_rows, self.right, 1, 0).astype(BF)
+
+    def stay(self, arrived, first, second):
+        left, right = self.stay_rows, self.right
+        tokens, columns = right.shape
+        assert first == second
+
+        def kernel(left_ref, right_ref, arrived_ref, kept_ref, first_ref, second_ref):
+            step = pl.program_id(0)
+            total = jnp.dot(left_ref[...], right_ref[...], preferred_element_type=F32)
+            total = (total + arrived_ref[...].astype(F32)).astype(BF)
+            pl.when(step < 2)(lambda: kept_ref.__setitem__(..., total))
+            pl.when(step == 2)(lambda: first_ref.__setitem__(..., total))
+            pl.when(step == 3)(lambda: second_ref.__setitem__(..., total))
+
+        outs = [jax.ShapeDtypeStruct((count, columns), BF) for count in (2 * first, first, second)]
+        return pl.pallas_call(
+            kernel,
+            out_shape=outs,
+            grid=(4,),
+            in_specs=[
+                pl.BlockSpec((first, tokens), lambda j: (j, 0)),
+                pl.BlockSpec(right.shape, lambda j: (0, 0)),
+                pl.BlockSpec((first, columns), lambda j: (j, 0)),
+            ],
+            out_specs=[
+                pl.BlockSpec((first, columns), lambda j: (jnp.minimum(j, 1), 0)),
+                pl.BlockSpec((first, columns), lambda j: (0, 0)),
+                pl.BlockSpec((first, columns), lambda j: (0, 0)),
+            ],
+            cost_estimate=cost(
+                2 * left.shape[0] * tokens * columns, [left, right, arrived, *outs]
+            ),
+            name="stay_rows",
+        )(left, right, arrived)
+
+
 def wide_tile(columns):
     return next(tile for tile in (1536, 1152, 768, 512, 384, 256, 128) if columns % tile == 0)
 
 
-def keep_grad(left, right, side, arrived, first, second):
-    half = first + second
-    tokens, columns = right.shape
-    tile = wide_tile(columns)
-
-    def kernel(left_ref, right_ref, arrived_ref, kept_ref, first_ref, second_ref, *scratch):
-        if side == 0:
-            turned_ref = scratch[0]
-
-            @pl.when(pl.program_id(0) == 0)
-            def _():
-                turned_ref[...] = left_ref[...].astype(F32).T.astype(BF)
-
-        else:
-            turned_ref = left_ref
-        total = jnp.dot(turned_ref[...], right_ref[...], preferred_element_type=F32)
-        total = (total + arrived_ref[...].astype(F32)).astype(BF)
-        kept_ref[...] = total[:half]
-        first_ref[...] = total[half : half + first]
-        second_ref[...] = total[half + first :]
-
-    outs = [jax.ShapeDtypeStruct((count, columns), BF) for count in (half, first, second)]
-    return pl.pallas_call(
-        kernel,
-        out_shape=outs,
-        grid=(columns // tile,),
-        in_specs=[
-            pl.BlockSpec(left.shape, lambda j: (0, 0)),
-            pl.BlockSpec((tokens, tile), lambda j: (0, j)),
-            pl.BlockSpec((2 * half, tile), lambda j: (0, j)),
-        ],
-        out_specs=[
-            pl.BlockSpec((count, tile), lambda j: (0, j)) for count in (half, first, second)
-        ],
-        scratch_shapes=[pltpu.VMEM((2 * half, tokens), BF)] if side == 0 else [],
-        cost_estimate=cost(4 * half * tokens * columns, [left, right, arrived, *outs]),
-        name="keep_grad",
-    )(left, right, arrived)
+def run_through(flight):
+    parts = None
+    try:
+        while True:
+            _, parts = flight.send(parts)
+    except StopIteration:
+        pass
 
 
 def modulation_flight(block, bias, stages, result):
@@ -176,15 +264,17 @@
     result.append(block + arrived + bias[None])
 
 
-def gather_flight(shard, cut, routes, waits, result):
+def gather_flight(shard, rows, cut, routes, waits, result):
     core_stage, first_route, second_route, far_stages = routes
     waits = [1] * (len(far_stages) - 2) + list(waits)
-    shard = yield 1, shard
+    parts = yield 1, shard
+    shard = jnp.concatenate(parts, axis=1) if len(parts) > 1 else parts[0]
+    if shard.shape[0] < rows:
+        shard = jnp.pad(shard, ((0, rows - shard.shape[0]), (0, 0)))
     blocks = [shard]
     for stage in reversed(far_stages):
         sent = jnp.concatenate(blocks, axis=0) if len(blocks) > 1 else blocks[0]
         arrived = yield waits.pop(0), swap_bit(sent, stage)
-        rows = shard.shape[0]
         blocks = blocks + [
             arrived[start : start + rows] for start in range(0, arrived.shape[0], rows)
         ]
@@ -496,14 +586,16 @@
     span = rows // groups
     factor = 1.0 / math.sqrt(head_size) / math.log(2.0)
 
-    def kernel(qkv_ref, other_ref, head_ref, mask_ref, mixed_ref, total_ref):
+    def kernel(
+        qkv_ref, key_ref, value_ref, head_ref, mask_ref, mixed_ref, wide_ref, total_ref
+    ):
         head = pl.program_id(0)
         start, inside = head_window(head, head_size, width)
         window = pl.ds(start, 256)
         key_window = pl.ds(start + width, 256)
         value_window = pl.ds(start + 2 * width, 256)
-        keys = (qkv_ref[:, key_window], other_ref[:, window])
-        values = (qkv_ref[:, value_window], other_ref[:, key_window])
+        keys = (qkv_ref[:, key_window], key_ref[:, window])
+        values = (qkv_ref[:, value_window], value_ref[:, window])
         for group in range(groups):
             at = pl.ds(group * span, span)
             query = qkv_ref[at, window]
@@ -525,31 +617,46 @@
             for power, value in zip(powers, values):
                 part = jnp.dot((power * inverse).astype(BF), value, preferred_element_type=F32)
                 out = part if out is None else out + part
-            out = (out * head_ref[group : group + 1, window]).astype(BF)
-            mixed_ref[at, window] = jnp.where(inside, out, mixed_ref[at, window])
+            out = out * head_ref[group : group + 1, window]
+            wide_ref[at, window] = jnp.where(inside, out, wide_ref[at, window])
+            mixed_ref[at, window] = jnp.where(inside, out.astype(BF), mixed_ref[at, window])
             lane = lax.broadcasted_iota(jnp.int32, (1, 128), 1)
             total_ref[at, :] = jnp.where(
                 lane == head, largest + jnp.log2(total), total_ref[at, :]
             )
 
     mixed = jax.ShapeDtypeStruct((rows, width), BF)
+    wide = jax.ShapeDtypeStruct((rows, width), F32)
     totals = jax.ShapeDtypeStruct((rows, 128), F32)
+    operands = (qkv, other, other, head_on, block_mask)
+    in_specs = [pl.BlockSpec(array.shape, lambda h: (0, 0)) for array in operands]
+    in_specs[1] = pl.BlockSpec((rows, width), lambda h: (0, 1))
+    in_specs[2] = pl.BlockSpec((rows, width), lambda h: (0, 2))
     return pl.pallas_call(
         kernel,
-        out_shape=[mixed, totals],
+        out_shape=[mixed, wide, totals],
         grid=(head_count,),
-        in_specs=[
-            pl.BlockSpec(array.shape, lambda h: (0, 0)) for array in (qkv, other, head_on, block_mask)
-        ],
-        out_specs=[pl.BlockSpec(array.shape, lambda h: (0, 0)) for array in (mixed, totals)],
+        in_specs=in_specs,
+        out_specs=[pl.BlockSpec(array.shape, lambda h: (0, 0)) for array in (mixed, wide, totals)],
         cost_estimate=cost(
             4 * head_count * rows * 2 * rows * 256, [qkv, other, mixed], head_count * rows * 2 * rows
         ),
         name="attend",
-    )(qkv, other, head_on, block_mask)
-
-
-def attend_back(qkv, other, grad_mixed, totals, block_mask, head_count):
+    )(*operands)
+
+
+def head_terms(key, value, query, grad, row, along, factor):
+    probs = jnp.exp2(contract(key, query, 1, 1) * factor + row)
+    grad_scores = (probs * (contract(value, grad, 1, 1) - along)).astype(BF)
+    return probs.astype(BF), grad_scores
+
+
+def head_rows(ref, window, inside):
+    values = ref[:, window]
+    return jnp.where(inside, values, jnp.zeros_like(values))
+
+
+def attend_back(qkv, other, grad_mixed, totals, along, block_mask, head_count):
     rows = qkv.shape[0]
     width = qkv.shape[1] // 3
     head_size = width // head_count
@@ -558,42 +665,31 @@
     scale = 1.0 / math.sqrt(head_size)
     factor = scale / math.log(2.0)
 
-    def kernel(qkv_ref, other_ref, grad_ref, totals_ref, mask_ref, query_out, own_out, other_out):
+    def kernel(
+        qkv_ref, key_ref, value_ref, grad_ref, totals_ref, along_ref, mask_ref, query_out, pair_out
+    ):
         head = pl.program_id(0)
         start, inside = head_window(head, head_size, width)
         window = pl.ds(start, 256)
         key_window = pl.ds(start + width, 256)
         value_window = pl.ds(start + 2 * width, 256)
-        query = qkv_ref[:, window]
-        query = jnp.where(inside, query, jnp.zeros_like(query))
-        grad = grad_ref[:, window]
-        grad = jnp.where(inside, grad, jnp.zeros_like(grad))
+        query = head_rows(qkv_ref, window, inside)
+        grad = head_rows(grad_ref, window, inside)
         total = totals_ref[pl.ds(head, 1), :]
-        kept = []
-        along = None
+        along = along_ref[pl.ds(head, 1), :]
+        query_grad = None
         for block in range(blocks):
             own = block < blocks // 2
             at = pl.ds((block if own else block - blocks // 2) * span, span)
-            key = qkv_ref[at, key_window] if own else other_ref[at, window]
-            value = qkv_ref[at, value_window] if own else other_ref[at, key_window]
-            scores = contract(key, query, 1, 1)
-            probs = jnp.exp2(scores * factor + (mask_ref[block : block + 1, :] - total))
-            grad_probs = contract(value, grad, 1, 1)
-            part = jnp.sum(probs * grad_probs, axis=0, keepdims=True)
-            along = part if along is None else along + part
-            kept.append((own, at, key, probs, grad_probs))
-        query_grad = None
-        for own, at, key, probs, grad_probs in kept:
-            grad_scores = (probs * (grad_probs - along)).astype(BF)
-            key_part = jnp.dot(grad_scores, query, preferred_element_type=F32) * scale
-            value_part = jnp.dot(probs.astype(BF), grad, preferred_element_type=F32)
-            out_ref = own_out if own else other_out
-            out_ref[at, window] = jnp.where(
-                inside, key_part.astype(out_ref.dtype), out_ref[at, window]
-            )
-            out_ref[at, key_window] = jnp.where(
-                inside, value_part.astype(out_ref.dtype), out_ref[at, key_window]
-            )
+            key = qkv_ref[at, key_window] if own else key_ref[at, window]
+            value = qkv_ref[at, value_window] if own else value_ref[at, window]
+            row = mask_ref[block : block + 1, :] - total
+            probs, grad_scores = head_terms(key, value, query, grad, row, along, factor)
+            if own:
+                key_part = jnp.dot(grad_scores, query, preferred_element_type=F32)
+                value_part = jnp.dot(probs, grad, preferred_element_type=F32)
+                pair_out[at, window] = jnp.where(inside, key_part, pair_out[at, window])
+                pair_out[at, key_window] = jnp.where(inside, value_part, pair_out[at, key_window])
             part = contract(grad_scores, key, 0, 0)
             query_grad = part if query_grad is None else query_grad + part
         query_out[:, window] = jnp.where(
@@ -603,19 +699,90 @@
     outs = [
         jax.ShapeDtypeStruct((rows, width), BF),
         jax.ShapeDtypeStruct((rows, 2 * width), F32),
-        jax.ShapeDtypeStruct((rows, 2 * width), BF),
     ]
-    operands = (qkv, other, grad_mixed, totals, block_mask)
+    operands = (qkv, other, other, grad_mixed, totals, along, block_mask)
+    in_specs = [pl.BlockSpec(array.shape, lambda h: (0, 0)) for array in operands]
+    in_specs[1] = pl.BlockSpec((rows, width), lambda h: (0, 1))
+    in_specs[2] = pl.BlockSpec((rows, width), lambda h: (0, 2))
     return pl.pallas_call(
         kernel,
         out_shape=outs,
         grid=(head_count,),
-        in_specs=[pl.BlockSpec(array.shape, lambda h: (0, 0)) for array in operands],
+        in_specs=in_specs,
         out_specs=[pl.BlockSpec(array.shape, lambda h: (0, 0)) for array in outs],
         cost_estimate=cost(
-            10 * head_count * rows * 2 * rows * 256, [*operands, *outs], head_count * rows * 2 * rows
+            8 * head_count * rows * 2 * rows * 256, [qkv, qkv, *outs], head_count * rows * 2 * rows
         ),
         name="attend_back",
+    )(*operands)
+
+
+def attend_back_other(
+    qkv, other, other_grad, other_totals, other_along, block_mask, query_grad, pair, head_count
+):
+    rows = qkv.shape[0]
+    width = qkv.shape[1] // 3
+    head_size = width // head_count
+    blocks = block_mask.shape[0]
+    span = rows // blocks
+    scale = 1.0 / math.sqrt(head_size)
+    factor = scale / math.log(2.0)
+
+    def kernel(
+        key_ref, value_ref, other_ref, grad_ref, totals_ref, along_ref, mask_ref, query_ref, pair_ref,
+        out_ref,
+    ):
+        head = pl.program_id(0)
+
+        @pl.when(head == 0)
+        def _():
+            out_ref[:, :width] = query_ref[...]
+
+        start, inside = head_window(head, head_size, width)
+        window = pl.ds(start, 256)
+        key_window = pl.ds(start + width, 256)
+        value_window = pl.ds(start + 2 * width, 256)
+        query = head_rows(other_ref, window, inside)
+        grad = head_rows(grad_ref, window, inside)
+        total = totals_ref[pl.ds(head, 1), :]
+        along = along_ref[pl.ds(head, 1), :]
+        for block in range(blocks):
+            at = pl.ds(block * span, span)
+            row = mask_ref[block : block + 1, :] - total
+            probs, grad_scores = head_terms(
+                key_ref[at, window], value_ref[at, window], query, grad, row, along, factor
+            )
+            key_part = pair_ref[at, window] + jnp.dot(
+                grad_scores, query, preferred_element_type=F32
+            )
+            value_part = pair_ref[at, key_window] + jnp.dot(
+                probs, grad, preferred_element_type=F32
+            )
+            out_ref[at, key_window] = jnp.where(
+                inside, (key_part * scale).astype(BF), out_ref[at, key_window]
+            )
+            out_ref[at, value_window] = jnp.where(
+                inside, value_part.astype(BF), out_ref[at, value_window]
+            )
+
+    out = jax.ShapeDtypeStruct(qkv.shape, BF)
+    operands = (
+        qkv, qkv, other, other_grad, other_totals, other_along, block_mask, query_grad, pair
+    )
+    in_specs = [pl.BlockSpec(array.shape, lambda h: (0, 0)) for array in operands]
+    in_specs[0] = pl.BlockSpec((rows, width), lambda h: (0, 1))
+    in_specs[1] = pl.BlockSpec((rows, width), lambda h: (0, 2))
+    in_specs[2] = pl.BlockSpec((rows, width), lambda h: (0, 0))
+    return pl.pallas_call(
+        kernel,
+        out_shape=out,
+        grid=(head_count,),
+        in_specs=in_specs,
+        out_specs=pl.BlockSpec(out.shape, lambda h: (0, 0)),
+        cost_estimate=cost(
+            8 * head_count * rows * rows * 256, [qkv, pair, out], head_count * rows * rows
+        ),
+        name="attend_back_other",
     )(*operands)
 
 
@@ -721,53 +888,42 @@
         ]
     ).astype(jnp.int32)
 
-    def scatter_ordered(left, right, waits, result):
-        half = left.shape[1] // 2
-        cuts = (2 * far_count * row_cut, 2 * far_count * (padded_rows - row_cut))
-        feed.start(
-            reduce_flight(
-                left[:, half:], left[:, :half], right, 0, routes, cuts, shard_rows, waits, result
-            )
-        )
+    def scatter_ordered(lefts, rights, waits, result):
+        cuts = (far_count * 2 * row_cut, far_count * 2 * (padded_rows - row_cut))
+        grads = ColumnGrads(lefts, rights, width)
+        feed.start(reduce_flight(grads, routes, cuts, shard_rows, waits, result))
 
     def scatter_chunks(turned, right, waits, result):
         rows = turned.shape[0] // device_count
-        stay, away = take_chunks(turned, place_table, rows)
+        grads = RowGrads(*take_chunks(turned, place_table, rows), right)
         cuts = (far_count * rows, far_count * rows)
-        feed.start(reduce_flight(away, stay, right, 1, routes, cuts, rows, waits, result))
+        feed.start(reduce_flight(grads, routes, cuts, rows, waits, result))
 
     gathered = []
 
     def unit_ticks(unit):
-        early = ((0, 1, 2, 3, 5, 6), (1, 3, 4, 6, 8, 9), (4, 6, 7, 8, 11, 12))
-        late = ((7, 8, 10, 11, 13, 14), (8, 10, 11, 13, 16, 17), (11, 13, 15, 16, 19, 20))
+        early = ((0, 1, 2, 4, 7, 8), (0, 2, 4, 9, 11, 12), (5, 9, 10, 12, 14, 15))
+        late = ((9, 10, 13, 14, 16, 17), (10, 13, 14, 16, 20, 21), (14, 16, 19, 20, 24, 25))
         if unit < 3:
             return early[unit]
-        return tuple(tick + 8 * (unit // 3 - 1) for tick in late[unit % 3])
-
-    def padded(shard):
-        return jnp.pad(shard, ((0, padded_rows - shard_rows), (0, 0)))
+        return tuple(tick + 10 * (unit // 3 - 1) for tick in late[unit % 3])
 
     for layer in range(layer_count):
-        up_out = jnp.concatenate([up_weight[layer], out_weight[layer]], axis=1)
-        for index, (shard, cut) in enumerate(
+        for index, (shard, rows, cut) in enumerate(
             (
-                (padded(qkv_weight[layer]), row_cut),
-                (padded(up_out), row_cut),
-                (down_weight[layer], down_weight.shape[1] // 2),
+                ((qkv_weight[layer],), padded_rows, row_cut),
+                ((up_weight[layer], out_weight[layer]), padded_rows, row_cut),
+                ((down_weight[layer],), down_weight.shape[1], down_weight.shape[1] // 2),
             )
         ):
             result = []
             gathered.append(result)
             start, *due = unit_ticks(3 * layer + index)
             waits = [after - before for before, after in zip([start] + due, due)]
-            feed.at(start, gather_flight(shard, cut, routes, waits, result))
+            feed.at(start, gather_flight(list(shard), rows, cut, routes, waits, result))
 
     def qkv_tiles(layer):
         return Tiles(gathered[3 * layer], width, 0, 3)
-
-    def pair_tiles(layer):
-        return Tiles(gathered[3 * layer], width, 1, 2)
 
     def up_tiles(layer):
         tile = wide_tile(hidden_width) // 2
@@ -779,10 +935,11 @@
     biases = (qv_bias, out_bias, up_bias, down_bias, mod_bias)
     steps_high = (timesteps // 32).astype(BF)
     steps_low = (timesteps % 32).astype(BF)
-    small = jnp.concatenate(
-        [bias.reshape(-1) for bias in biases] + [steps_high.reshape(-1), steps_low.reshape(-1)]
-    )
-    small = feed.tick(small[None])
+    step_rows = jnp.concatenate([steps_high, steps_low], axis=0)
+    if layer_count > 2:
+        step_rows = jnp.pad(step_rows, ((0, layer_count - 2), (0, 0)))
+    small = jnp.concatenate([*biases, step_rows], axis=1)
+    small = feed.tick(small)
     small_stages = [("seq", bit) for bit in reversed(range(seq_bits))] + [x_stage]
     for index, stage in enumerate(small_stages):
         small = jnp.concatenate([small, swap_bit(small, stage)], axis=0)
@@ -790,20 +947,29 @@
             small = feed.tick(small)
     small_masks = jnp.array(relative_masks(list(reversed(small_stages)), flat_mask), jnp.int32)
     put_back = (flat_index ^ small_masks)[None, :] == jnp.arange(device_count)[:, None]
-    every_small = jnp.dot(put_back.astype(BF), small, preferred_element_type=F32)
-    full_biases = []
-    offset = 0
-    for bias in biases:
-        columns = bias.shape[1]
-        full_biases.append(
-            [
-                every_small[:, offset + layer * columns : offset + (layer + 1) * columns]
-                .reshape(-1)
-                for layer in range(layer_count)
-            ]
-        )
-        offset += layer_count * columns
-    step_parts = every_small[:seq_count, offset:]
+    small_columns = small.shape[1]
+    every_small = jnp.dot(
+        put_back.astype(BF),
+        small.reshape(device_count, layer_count * small_columns),
+        preferred_element_type=F32,
+    ).reshape(device_count, layer_count, small_columns)
+    bias_columns = small_columns - item_count
+    every_small, tokens, head_mask, channel_mask, token_keep = feed.tick(
+        (every_small, tokens, head_mask, channel_mask, token_keep)
+    )
+    step_parts = every_small[:seq_count, :2, bias_columns:].reshape(seq_count, 2 * item_count)
+
+    def unpack_biases(every):
+        offset = 0
+        full = []
+        for bias in biases:
+            columns = bias.shape[1]
+            full.append(
+                [every[:, layer, offset : offset + columns].reshape(-1) for layer in range(layer_count)]
+            )
+            offset += columns
+        return full
+
     every_step = step_parts[:, :item_count] * 32.0 + step_parts[:, item_count:]
 
     cond_every = cond_columns(every_step.reshape(-1), flat_index * shard_rows, shard_rows, width)
@@ -831,20 +997,20 @@
     def modulation_part(layer):
         return jnp.dot(cond_relative, mod_weight[layer], preferred_element_type=F32)
 
+    full_biases = unpack_biases(every_small)
     block = feed.tick(modulation_part(0))
     for index, stage in enumerate(mod_stages[:-1]):
         half = block.shape[0] // 2
         block = block[:half] + swap_bit(block[half:], stage)
         if index == 1:
-            block = feed.tick(block)
-    block = block + swap_bit(block, mod_stages[-1]) + full_biases[4][0][None]
-    modulations[0].append(feed.tick(block))
+            block, full_biases = feed.tick((block, full_biases))
+    block = feed.tick(block + swap_bit(block, mod_stages[-1]))
+    modulations[0].append(block + full_biases[4][0][None])
     for layer in range(1, layer_count):
-        feed.start(
-            modulation_flight(
-                modulation_part(layer), full_biases[4][layer], mod_stages, modulations[layer]
-            )
-        )
+        flight = modulation_flight(
+            modulation_part(layer), full_biases[4][layer], mod_stages, modulations[layer]
+        )
+        feed.at(10 * layer - 1, flight)
 
     group_item = (
         (half_index * local_rows + jnp.arange(group_count, dtype=jnp.int32) * group_rows)
@@ -867,6 +1033,12 @@
     block_mask = jnp.where(group_item[:, None] == block_item[None, :], 0.0, -1e30).astype(F32)
     query_mask = jnp.repeat(block_mask, group_rows, axis=1)
     key_mask = jnp.repeat(block_mask.T, group_rows, axis=1)
+    cross_mask = jnp.repeat(block_mask[:, group_count:], group_rows, axis=1)
+
+    head_lanes = (
+        jnp.arange(width, dtype=jnp.int32)[None, :] // head_size
+        == jnp.arange(head_count, dtype=jnp.int32)[:, None]
+    ).astype(F32)
 
     def grouped(values):
         return values.reshape(group_count, group_rows, values.shape[-1])
@@ -895,16 +1067,20 @@
         )
         low_one = feed.tick(low_one)
         low_one = feed.tick(ordered(low_one))
+        low_one = feed.tick(low_one)
         low_one = feed.until(gathered[3 * layer], low_one)
         qkv_low = project(low_one, qkv_tiles(layer), bias_three, BF, "project_qkv")
+        qkv_low, other_one = lax.optimization_barrier((qkv_low, other_one))
         other_low = project(
-            ordered(other_one), pair_tiles(layer), bias_three[width:], BF, "project_pair"
+            ordered(other_one), qkv_tiles(layer), bias_three, BF, "project_other"
         )
         other_low = feed.tick(other_low)
-        mixed_low, totals = attend(qkv_low, other_low, head_on, query_mask, head_count)
+        mixed_low, mixed_wide, totals = attend(qkv_low, other_low, head_on, query_mask, head_count)
         totals = totals[:, :head_count].T
+        other_totals = swap_bit(totals, x_stage)
         mixed_low = feed.tick(mixed_low)
         mixed_low = feed.tick(ordered(mixed_low))
+        mixed_low = feed.tick(mixed_low)
         mixed_low = feed.until(gathered[3 * layer + 1], mixed_low)
         branch_one = grouped(project(mixed_low, out_tiles(layer), out_b, F32, "project_out"))
         after_attn = current + gate_one * branch_one
@@ -932,7 +1108,9 @@
                 qkv_low=qkv_low,
                 other_low=other_low,
                 totals=totals,
+                other_totals=other_totals,
                 mixed_low=mixed_low,
+                mixed_wide=mixed_wide,
                 branch_one=branch_one,
                 after_attn=after_attn,
                 low_two=low_two,
@@ -953,6 +1131,25 @@
         axis=1,
     ).reshape(seq_count * 8, shard_rows)
     cond_twice = jnp.concatenate([cond_rows, cond_rows], axis=0)
+
+    def packet_flight(packet, wait, result):
+        every = yield wait, lax.all_gather(packet, AXES, axis=0, tiled=True)
+        grad_mod_weight = contract(cond_twice, every, 0, 0)
+        sums = jnp.sum(every.astype(F32).reshape(device_count, *packet.shape), axis=0)
+
+        def shard_of(row, start, columns):
+            return lax.dynamic_slice_in_dim(row, start + flat_index * columns, columns, 0)
+
+        grad_mod_bias = shard_of(jnp.sum(sums[:item_count], axis=0), 0, mod_bias.shape[1])
+        bias_sum = sums[item_count:].reshape(-1)
+        parts = []
+        start = 0
+        for bias in (qv_bias, out_bias, up_bias, down_bias):
+            parts.append(shard_of(bias_sum, start, bias.shape[1]))
+            start += device_count * bias.shape[1]
+        grads = yield 1, (grad_mod_weight, *parts, grad_mod_bias)
+        result.append(grads)
+
     grad_current = grouped(cotangent)
     layer_totals = [None] * layer_count
     for layer in reversed(range(layer_count)):
@@ -962,13 +1159,13 @@
         grad_gate_two = jnp.sum(kept_grad * saved["branch_two"], axis=1)
         grad_down_bias = jnp.sum(down_grad.astype(F32), axis=0)
         down_rows, up_rows, out_rows, qkv_rows = [], [], [], []
-        scatter_chunks(saved["hidden_turned"], down_grad, (1, 2, 2), down_rows)
+        last = layer == 0
+        scatter_chunks(saved["hidden_turned"], down_grad, (1, 1, 1, 2, 1, 1), down_rows)
         up_grad, grad_up_bias = hidden_back(
             down_grad, full_downs[layer], saved["hidden_pre"], saved["channel_on"], wide_tile(hidden_width) // 2
         )
         grad_up_bias = grad_up_bias[0]
-        up_grad = feed.tick(up_grad)
-        scatter_ordered(saved["low_two"], up_grad, (1, 2, 2), up_rows)
+        up_grad = feed.tick(feed.tick(up_grad))
         grad_h2 = grouped(project_back(up_grad, up_tiles(layer), order, 2, "back_up"))
         grad_h2 = feed.tick(grad_h2)
         normed_two, inverse_two = normalize(saved["after_attn"])
@@ -981,7 +1178,9 @@
         grad_gate_one = jnp.sum(grad_after * saved["branch_one"], axis=1)
         grad_out_bias = jnp.sum(out_grad.astype(F32), axis=0)
         out_grad = feed.tick(out_grad)
-        scatter_ordered(saved["mixed_low"], out_grad, (1, 1, 1), out_rows)
+        lefts, rights = (saved["low_two"], saved["mixed_low"]), (up_grad, out_grad)
+        up_waits = (2, 0, 2, 2, 2, 1) if last else (2, 0, 2, 2, 2, 3)
+        scatter_ordered(lefts, rights, up_waits, up_rows)
         grad_mixed = ungrouped(
             (
                 grouped(project_back(out_grad, out_tiles(layer), order, 1, "back_out"))
@@ -989,17 +1188,42 @@
             ).astype(BF)
         )
         grad_mixed = feed.tick(grad_mixed)
-        grad_query, own_pair, other_pair = attend_back(
-            saved["qkv_low"], saved["other_low"], grad_mixed, saved["totals"], key_mask, head_count
-        )
-        other_pair = feed.tick(other_pair)
-        back_pair = swap_bit(other_pair, x_stage)
-        grad_qkv = jnp.concatenate(
-            [grad_query, (own_pair + back_pair.astype(F32)).astype(BF)], axis=1
+        other_mixed = swap_bit(grad_mixed, x_stage)
+        along = lax.dot_general(
+            head_lanes,
+            saved["mixed_wide"] * grad_mixed.astype(F32),
+            (((1,), (1,)), ((), ())),
+            precision=lax.Precision.HIGHEST,
+            preferred_element_type=F32,
+        )
+        other_along = swap_bit(along, x_stage)
+        grad_query, grad_pair = attend_back(
+            saved["qkv_low"],
+            saved["other_low"],
+            grad_mixed,
+            saved["totals"],
+            along,
+            key_mask,
+            head_count,
+        )
+        grad_pair = feed.tick(grad_pair)
+        grad_qkv = attend_back_other(
+            saved["qkv_low"],
+            saved["other_low"],
+            other_mixed,
+            saved["other_totals"],
+            other_along,
+            cross_mask,
+            grad_query,
+            grad_pair,
+            head_count,
         )
         grad_qkv = feed.tick(grad_qkv)
         grad_qkv_bias = jnp.sum(grad_qkv.astype(F32), axis=0)
-        scatter_ordered(saved["low_one"], grad_qkv, (1, 2, 2), qkv_rows)
+        qkv_waits = (1, 1, 3, 1) if last else (1, 0, 4, 2, 1, 2)
+        scatter_ordered((saved["low_one"],), (grad_qkv,), qkv_waits, qkv_rows)
+        if last:
+            grad_qkv = feed.tick(feed.tick(grad_qkv))
         grad_h1 = grouped(project_back(grad_qkv, qkv_tiles(layer), order, 2, "back_qkv"))
         grad_h1 = feed.tick(grad_h1)
         normed_one, inverse_one = normalize(saved["inputs"])
@@ -1035,37 +1259,28 @@
             [grad_slots, jnp.concatenate([bias_row, spare]).reshape(8 - item_count, mod_width)],
             axis=0,
         ).astype(BF)
-        every_packet = lax.all_gather(packet, AXES, axis=0, tiled=True)
-        grad_mod_weight = contract(cond_twice, every_packet, 0, 0)
-        packet_sum = jnp.sum(
-            every_packet.astype(F32).reshape(device_count, 8, mod_width), axis=0
-        )
-        mod_cols = mod_bias.shape[1]
-        grad_mod_bias = lax.dynamic_slice_in_dim(
-            jnp.sum(packet_sum[:item_count], axis=0), flat_index * mod_cols, mod_cols, 0
-        )
-        bias_sum = packet_sum[item_count:].reshape(-1)
-        parts = []
-        start = 0
-        for bias in (qv_bias, out_bias, up_bias, down_bias):
-            columns = bias.shape[1]
-            parts.append(
-                lax.dynamic_slice_in_dim(bias_sum, start + flat_index * columns, columns, 0)
-            )
-            start += device_count * columns
-        grad_current = grad_inputs
+        if last:
+            grad_inputs, packet = feed.tick((grad_inputs, packet))
+        shared_grads = []
+        feed.start(packet_flight(packet, 3 if last else 7, shared_grads))
+        grad_current = grad_inputs if last else feed.tick(grad_inputs)
         layer_totals[layer] = (
             qkv_rows,
-            out_rows,
+            up_rows,
             up_rows,
             down_rows,
-            grad_mod_weight,
-            *parts,
-            grad_mod_bias,
+            shared_grads,
         )
     grad_current = feed.finish(grad_current)
     layer_totals = [
-        [part[0] if isinstance(part, list) else part for part in totals] for totals in layer_totals
+        (
+            qkv[0],
+            up[0][:, hidden_width:],
+            up[0][:, :hidden_width],
+            down[0],
+            *shared[0],
+        )
+        for qkv, up, _, down, shared in layer_totals
     ]
     stacked = tuple(
         jnp.stack([layer_totals[layer][index] for layer in range(layer_count)])

time: 1440 us -> 1310 us (0.910)
  waiting for transfers between devices: 374 us -> 235 us
  Pallas kernels: 407 us -> 478 us
  matrix products: 105 us -> 81.3 us
  starting transfers between devices: 126 us -> 106 us
    ppermute x135 -> x125, waiting for transfers between devices: 344 us -> 233 us  [swap_bit(): lax.ppermute(block, axis, [(low, low ^ 1 << bit) for low in range(count)])]
    pallas_call x12 -> x16, Pallas kernels: 190 us -> 255 us  [the longest x8 73.3 us: call(): pl.pallas_call(kernel, out_shape=outs, grid=(sum(self.counts),), in_specs...]
    all_gather x2, waiting for transfers between devices: 30.3 us -> 2.34 us  [packet_flight(): every = (yield (wait, lax.all_gather(packet, AXES, axis=0, tiled=True)))]
    dot_general x20 -> x14, matrix products: 102 us -> 74.4 us  [contract(): lax.dot_general(left, right, (((left_dim,), (right_dim,)), ((), ())), pre...]
    ppermute x135 -> x125, starting transfers between devices: 126 us -> 105 us  [swap_bit(): lax.ppermute(block, axis, [(low, low ^ 1 << bit) for low in range(count)])]
    convert_element_type x16 -> x12, other arithmetic: 31.3 us -> 25.7 us  [reduce_flight(): first_kept = add(first_kept, first_arrived, 0, half_first).astype(BF)]
    unnamed x481 -> x479, local copies, waits for them, and re-layouts: 102 us -> 106 us
  transfers between devices with their start and end apart: 137 -> 127, of which waited for: 36 -> 38; matrix products, arithmetic and copies ran while one was open for 29% -> 30% of each run, Pallas kernels for 27% -> 34%
where the time goes in v2:
time: 1310 us; the launch traced here: 1300 us
  Pallas kernels  478 us (36%)
  waiting for transfers between devices  235 us (18%)
  other arithmetic  193 us (15%)
  local copies, waits for them, and re-layouts  192 us (15%)
  starting transfers between devices  106 us (8%)
  matrix products  81.3 us (6%)
  between operations  17.2 us (1%)
    ppermute x125, waiting for transfers between devices, swap_bit(): lax.ppermute(block, axis, [(low, low ^ 1 << bit) for low in range(count)])  233 us
    unnamed x479, local copies, waits for them, and re-layouts  106 us
    ppermute x125, starting transfers between devices, swap_bit(): lax.ppermute(block, axis, [(low, low ^ 1 << bit) for low in range(count)])  105 us
    pallas_call x6, Pallas kernels, project_back(): pl.pallas_call(kernel, out_shape=out, grid=(tiles.count,), in_specs=[pl.B...  80 us
    dot_general x14, matrix products, contract(): lax.dot_general(left, right, (((left_dim,), (right_dim,)), ((), ())), pre...  74.4 us
    pallas_call x8, Pallas kernels, call(): pl.pallas_call(kernel, out_shape=outs, grid=(sum(self.counts),), in_specs...  73.3 us
    pallas_call x2, Pallas kernels, attend_back(): pl.pallas_call(kernel, out_shape=outs, grid=(head_count,), in_specs=in_sp...  66.2 us
    pallas_call x2, Pallas kernels, attend(): pl.pallas_call(kernel, out_shape=[mixed, wide, totals], grid=(head_count,...  54.3 us
  transfers between devices with their start and end apart: 127, of which 38 were waited for; matrix products, arithmetic and copies ran while one was open for 30% of the time, Pallas kernels for 34%

profile of v2, /device:TPU:0, one launch (start us, length us, event | category | flops | bytes accessed | tf_op | source)
XLA Modules:
  0.0 1302.3 jit_solution(17675536227968326762)
XLA Ops:
  109.5 10.9 collective-permute-done.9
  167.2 10.2 project_qkv.2.qkv_ref.key_ref.value_ref
  190.0 9.8 project_other.2.key_ref.value_ref.other_ref
  221.9 27.1 %attend.2 = (bf16[512,1152]{1,0:T(8,128)(2,1)}, f32[512,1152]{1,0:T(8,128)}, f32[512,128]{1,0:T(8,128)}) custom-call(bf16[512,3456]{1,0:T(8,128)(2,1)} %project_qkv.2.qkv_ref.key_ref.value_ref, bf16[512,3456]{1,0:T(8,128)(2,1)} %project_other.2.key_ref.value_ref.other_ref, bf16[512,3456]{1,0:T(8,128)(2,1)} %project_other.2.key_ref.value_ref.other_ref, ...), custom_call_target="tpu_custom_call" | custom-call | flops 8589934592 | bytes 8257536 | tf_op jit(solution)/shard_map/attend/pallas_call | solution.py:635
  253.2 15.6 %collective-permute-done.29 = f32[16,6912]{1,0:T(8,128)} collective-permute-done((f32[16,6912]{1,0:T(8,128)}, f32[16,6912]{1,0:T(8,128)}, u32[]{:S(2)}, u32[]{:S(2)}) %collective-permute-start.29) | collective-permute-done | bytes 442400 | tf_op jit(solution)/shard_map/ppermute | solution.py:18
  289.6 11.3 collective-permute-done.33
  351.9 14.6 %project_up.2 = (f32[512,4608]{1,0:T(8,128)}, bf16[4608,512]{1,0:T(8,128)(2,1)}) custom-call(bf16[512,1280]{1,0:T(8,128)(2,1)} %fusion.12.left_ref.refs_0_, f32[1,4608]{1,0:T(1,128)} %reshape.647.bias_ref, f32[2,4608]{1,0:T(2,128)} %get-tuple-element.581.channel_ref, bf16[192,5760]{1,0:T(8,128)(2,1)} %copy-done.14, ...), custom_call_target="tpu_custom_call" | custom-call | flops 6039797760 | bytes 30212096 | tf_op jit(solution)/shard_map/project_up/pallas_call | solution.py:461
  405.9 12.7 fusion.95
  455.7 9.9 project_qkv.3.qkv_ref.key_ref.value_ref
  470.1 10.0 project_other.3.key_ref.value_ref.other_ref
  487.2 27.1 %attend.3 = (bf16[512,1152]{1,0:T(8,128)(2,1)}, f32[512,1152]{1,0:T(8,128)}, f32[512,128]{1,0:T(8,128)}) custom-call(bf16[512,3456]{1,0:T(8,128)(2,1)} %project_qkv.3.qkv_ref.key_ref.value_ref, bf16[512,3456]{1,0:T(8,128)(2,1)} %project_other.3.key_ref.value_ref.other_ref, bf16[512,3456]{1,0:T(8,128)(2,1)} %project_other.3.key_ref.value_ref.other_ref, ...), custom_call_target="tpu_custom_call" | custom-call | flops 8589934592 | bytes 8257536 | tf_op jit(solution)/shard_map/attend/pallas_call | solution.py:635
  543.6 14.6 %project_up.3 = (f32[512,4608]{1,0:T(8,128)}, bf16[4608,512]{1,0:T(8,128)(2,1)}) custom-call(bf16[512,1280]{1,0:T(8,128)(2,1)} %fusion.16.left_ref.refs_0_, f32[1,4608]{1,0:T(1,128)} %reshape.659.bias_ref, f32[2,4608]{1,0:T(2,128)} %get-tuple-element.580.channel_ref, bf16[192,5760]{1,0:T(8,128)(2,1)} %constant_dynamic-update-slice_fusion.44.refs_0_, ...), custom_call_target="tpu_custom_call" | custom-call | flops 6039797760 | bytes 30212096 | tf_op jit(solution)/shard_map/project_up/pallas_call | solution.py:461
  592.8 16.3 %hidden_back.2 = (bf16[512,4608]{1,0:T(8,128)(2,1)}, f32[1,4608]{1,0:T(1,128)}) custom-call(bf16[512,1152]{1,0:T(8,128)(2,1)} %get-tuple-element.593.grad_ref.right_ref, bf16[4608,1152]{1,0:T(8,128)(2,1)} %bitcast.302, f32[512,4608]{1,0:T(8,128)} %get-tuple-element.367.pre_ref, f32[2,4608]{1,0:T(2,128)} %get-tuple-element.580.channel_ref), custom_call_target="tpu_custom_call" | custom-call | flops 5435817984 | bytes 25952256 | tf_op jit(solution)/shard_map/hidden_back/pallas_call | solution.py:553
  623.6 16.4 %back_up.2 = f32[512,1152]{1,0:T(8,128)} custom-call(bf16[512,4608]{1,0:T(8,128)(2,1)} %get-tuple-element.376.right_ref.refs_2_, bf16[1280,1152]{1,0:T(8,128)(2,1)} %fusion.order_ref, bf16[192,5760]{1,0:T(8,128)(2,1)} %constant_dynamic-update-slice_fusion.44.refs_0_, bf16[128,5760]{1,0:T(8,128)(2,1)} %constant_dynamic-update-slice_fusion.49.refs_1_, ...), custom_call_target="tpu_custom_call" | custom-call | flops 9059696640 | bytes 24772608 | tf_op jit(solution)/shard_map/back_up/pallas_call | solution.py:510
  706.0 33.1 %attend_back.2 = (bf16[512,1152]{1,0:T(8,128)(2,1)}, f32[512,2304]{1,0:T(8,128)}) custom-call(bf16[512,3456]{1,0:T(8,128)(2,1)} %project_qkv.3.qkv_ref.key_ref.value_ref, bf16[512,3456]{1,0:T(8,128)(2,1)} %project_other.3.key_ref.value_ref.other_ref, bf16[512,3456]{1,0:T(8,128)(2,1)} %project_other.3.key_ref.value_ref.other_ref, ...), custom_call_target="tpu_custom_call" | custom-call | flops 17179869184 | bytes 12976128 | tf_op jit(solution)/shard_map/attend_back/pallas_call | solution.py:707
  742.0 21.4 %attend_back_other.2.right_ref.refs_1_ = bf16[512,3456]{1,0:T(8,128)(2,1)} custom-call(bf16[512,3456]{1,0:T(8,128)(2,1)} %project_qkv.3.qkv_ref.key_ref.value_ref, bf16[512,3456]{1,0:T(8,128)(2,1)} %project_qkv.3.qkv_ref.key_ref.value_ref, bf16[512,3456]{1,0:T(8,128)(2,1)} %project_other.3.key_ref.value_ref.other_ref, ...), custom_call_target="tpu_custom_call" | custom-call | flops 8589934592 | bytes 11796480 | tf_op jit(solution)/shard_map/attend_back_other/pallas_call | solution.py:776
  778.4 11.9 stay_grad.4
  801.8 12.5 multiply_reduce_fusion.5
  834.0 15.1 %back_qkv.2 = f32[512,1152]{1,0:T(8,128)} custom-call(bf16[512,3456]{1,0:T(8,128)(2,1)} %attend_back_other.2.right_ref.refs_1_, bf16[1280,1152]{1,0:T(8,128)(2,1)} %fusion.order_ref, bf16[192,3456]{1,0:T(8,128)(2,1)} %constant_dynamic-update-slice_fusion.34.refs_0_, bf16[128,3456]{1,0:T(8,128)(2,1)} %constant_dynamic-update-slice_fusion.39.refs_1_, ...), custom_call_target="tpu_custom_call" | custom-call | flops 7549747200 | bytes 17694720 | tf_op jit(solution)/shard_map/back_qkv/pallas_call | solution.py:510
  890.2 16.5 %hidden_back.3 = (bf16[512,4608]{1,0:T(8,128)(2,1)}, f32[1,4608]{1,0:T(1,128)}) custom-call(bf16[512,1152]{1,0:T(8,128)(2,1)} %bitcast.322, bf16[4608,1152]{1,0:T(8,128)(2,1)} %bitcast.301, f32[512,4608]{1,0:T(8,128)} %get-tuple-element.397.pre_ref, f32[2,4608]{1,0:T(2,128)} %get-tuple-element.581.channel_ref), custom_call_target="tpu_custom_call" | custom-call | flops 5435817984 | bytes 25952256 | tf_op jit(solution)/shard_map/hidden_back/pallas_call | solution.py:553
  925.6 16.9 %back_up.3 = f32[512,1152]{1,0:T(8,128)} custom-call(bf16[512,4608]{1,0:T(8,128)(2,1)} %get-tuple-element.409.right_ref.refs_2_, bf16[1280,1152]{1,0:T(8,128)(2,1)} %fusion.order_ref, bf16[192,5760]{1,0:T(8,128)(2,1)} %copy-done.14, bf16[128,5760]{1,0:T(8,128)(2,1)} %constant_dynamic-update-slice_fusion.17.refs_1_, ...), custom_call_target="tpu_custom_call" | custom-call | flops 9059696640 | bytes 24772608 | tf_op jit(solution)/shard_map/back_up/pallas_call | solution.py:510
  942.4 13.6 %collective-permute-done.96 = bf16[80,5760]{1,0:T(8,128)(2,1)} collective-permute-done((bf16[80,5760]{1,0:T(8,128)(2,1)}, bf16[80,5760]{1,0:T(8,128)(2,1)}, u32[]{:S(2)}, u32[]{:S(2)}) %collective-permute-start.96) | collective-permute-done | bytes 921632 | tf_op jit(solution)/shard_map/ppermute | solution.py:18
  975.4 10.1 away_grad.6
  1008.8 11.2 collective-permute-done.101
  1028.6 33.1 %attend_back.3 = (bf16[512,1152]{1,0:T(8,128)(2,1)}, f32[512,2304]{1,0:T(8,128)}) custom-call(bf16[512,3456]{1,0:T(8,128)(2,1)} %project_qkv.2.qkv_ref.key_ref.value_ref, bf16[512,3456]{1,0:T(8,128)(2,1)} %project_other.2.key_ref.value_ref.other_ref, bf16[512,3456]{1,0:T(8,128)(2,1)} %project_other.2.key_ref.value_ref.other_ref, ...), custom_call_target="tpu_custom_call" | custom-call | flops 17179869184 | bytes 12976128 | tf_op jit(solution)/shard_map/attend_back/pallas_call | solution.py:707
  1075.5 11.9 stay_grad.6
  1095.8 22.0 %attend_back_other.3.refs_1_.right_ref = bf16[512,3456]{1,0:T(8,128)(2,1)} custom-call(bf16[512,3456]{1,0:T(8,128)(2,1)} %project_qkv.2.qkv_ref.key_ref.value_ref, bf16[512,3456]{1,0:T(8,128)(2,1)} %project_qkv.2.qkv_ref.key_ref.value_ref, bf16[512,3456]{1,0:T(8,128)(2,1)} %project_other.2.key_ref.value_ref.other_ref, ...), custom_call_target="tpu_custom_call" | custom-call | flops 8589934592 | bytes 11796480 | tf_op jit(solution)/shard_map/attend_back_other/pallas_call | solution.py:776
  1162.0 15.2 %back_qkv.3 = f32[512,1152]{1,0:T(8,128)} custom-call(bf16[512,3456]{1,0:T(8,128)(2,1)} %attend_back_other.3.refs_1_.right_ref, bf16[1280,1152]{1,0:T(8,128)(2,1)} %fusion.order_ref, bf16[192,3456]{1,0:T(8,128)(2,1)} %copy-done.141, bf16[128,3456]{1,0:T(8,128)(2,1)} %copy-done.164, bf16[192,3456]{1,0:T(8,128)(2,1)} %copy-done.186, ...), custom_call_target="tpu_custom_call" | custom-call | flops 7549747200 | bytes 17694720 | tf_op jit(solution)/shard_map/back_qkv/pallas_call | solution.py:510
  1198.9 11.4 collective-permute-done.119
  1226.6 16.9 %collective-permute-done.122 = bf16[40,5760]{1,0:T(8,128)(2,1)S(1)} collective-permute-done((bf16[40,5760]{1,0:T(8,128)(2,1)S(1)}, bf16[40,5760]{1,0:T(8,128)(2,1)S(1)}, u32[]{:S(2)}, u32[]{:S(2)}) %collective-permute-start.122) | collective-permute-done | bytes 460832 | tf_op jit(solution)/shard_map/ppermute | solution.py:18
  1249.4 17.7 %collective-permute-done.123 = bf16[80,3456]{1,0:T(8,128)(2,1)S(1)} collective-permute-done((bf16[80,3456]{1,0:T(8,128)(2,1)S(1)}, bf16[80,3456]{1,0:T(8,128)(2,1)S(1)}, u32[]{:S(2)}, u32[]{:S(2)}) %collective-permute-start.123) | collective-permute-done | bytes 552992 | tf_op jit(solution)/shard_map/ppermute | solution.py:18
  1276.6 11.5 collective-permute-done.124
  (1048 shorter events, 776.6 us)
Async XLA Ops:
  7.2 1056.6 %all-gather.3.cloned.1.call-start = ((), (), s32[]{:S(2)}) async-start(), calls=%async_computation | async-start | bytes 3649536 | tf_op jit(solution)/shard_map/all_gather | solution.py:1136
  161.4 47.0 %collective-permute-start.23 = (bf16[96,5760]{1,0:T(8,128)(2,1)}, bf16[96,5760]{1,0:T(8,128)(2,1)}, u32[]{:S(2)}, u32[]{:S(2)}) collective-permute-start(bf16[96,5760]{1,0:T(8,128)(2,1)} %pad_maximum_fusion.3), channel_id=1, source_target_pairs={{0,16},{16,0},{1,17},{17,1},{2,18},{18,2},{3,19},{19,3},{4,20},{20... | collective-permute-start | bytes 3317768 | tf_op jit(solution)/shard_map/ppermute | solution.py:18
  209.9 78.2 %collective-permute-start.30 = (bf16[192,5760]{1,0:T(8,128)(2,1)S(1)}, bf16[192,5760]{1,0:T(8,128)(2,1)}, u32[]{:S(2)}, u32[]{:S(2)}) collective-permute-start(bf16[192,5760]{1,0:T(8,128)(2,1)S(1)} %constant_dynamic-update-slice_fusion.12.refs_0_), channel_id=1, source_target_pairs={{0,2},{1,3},{2,0},{3,1},{4,6},{5,7},{6,4},{7,5},{8,10},{9,11},{10,... | collective-permute-start | bytes 6635528 | tf_op jit(solution)/shard_map/ppermute | solution.py:18
  211.5 99.6 %collective-permute-start.35 = (bf16[192,5760]{1,0:T(8,128)(2,1)S(1)}, bf16[192,5760]{1,0:T(8,128)(2,1)}, u32[]{:S(2)}, u32[]{:S(2)}) collective-permute-start(bf16[192,5760]{1,0:T(8,128)(2,1)S(1)} %constant_dynamic-update-slice_fusion.12.refs_0_), channel_id=1, source_target_pairs={{0,1},{1,0},{2,3},{3,2},{4,5},{5,4},{6,7},{7,6},{8,9},{9,8},{10,11... | collective-permute-start | bytes 6635528 | tf_op jit(solution)/shard_map/ppermute | solution.py:18
  215.0 53.8 %collective-permute-start.27 = (bf16[288,1152]{1,0:T(8,128)(2,1)}, bf16[288,1152]{1,0:T(8,128)(2,1)}, u32[]{:S(2)}, u32[]{:S(2)}) collective-permute-start(bf16[288,1152]{1,0:T(8,128)(2,1)} %pad_maximum_fusion.15), channel_id=1, source_target_pairs={{0,4},{1,5},{2,6},{3,7},{4,0},{5,1},{6,2},{7,3},{8,12},{9,13},{10,... | collective-permute-start | bytes 1990664 | tf_op jit(solution)/shard_map/ppermute | solution.py:18
  219.2 49.5 %collective-permute-start.29 = (f32[16,6912]{1,0:T(8,128)}, f32[16,6912]{1,0:T(8,128)}, u32[]{:S(2)}, u32[]{:S(2)}) collective-permute-start(f32[16,6912]{1,0:T(8,128)} %slice.1211), channel_id=1, source_target_pairs={{0,2},{1,3},{2,0},{3,1},{4,6},{5,7},{6,4},{7,5},{8,10},{9,11},{10,... | collective-permute-start | bytes 1327112 | tf_op jit(solution)/shard_map/ppermute | solution.py:18
  325.9 51.5 %collective-permute-start.43 = (bf16[576,1152]{1,0:T(8,128)(2,1)}, bf16[576,1152]{1,0:T(8,128)(2,1)}, u32[]{:S(2)}, u32[]{:S(2)}) collective-permute-start(bf16[576,1152]{1,0:T(8,128)(2,1)} %constant_dynamic-update-slice_fusion.24), channel_id=1, source_target_pairs={{0,2},{1,3},{2,0},{3,1},{4,6},{5,7},{6,4},{7,5},{8,10},{9,11},{10,... | collective-permute-start | bytes 3981320 | tf_op jit(solution)/shard_map/ppermute | solution.py:18
  333.3 44.2 %collective-permute-start.44 = (bf16[576,1152]{1,0:T(8,128)(2,1)}, bf16[576,1152]{1,0:T(8,128)(2,1)}, u32[]{:S(2)}, u32[]{:S(2)}) collective-permute-start(bf16[576,1152]{1,0:T(8,128)(2,1)} %constant_dynamic-update-slice_fusion.29), channel_id=1, source_target_pairs={{0,16},{16,0},{1,17},{17,1},{2,18},{18,2},{3,19},{19,3},{4,20},{20... | collective-permute-start | bytes 3981320 | tf_op jit(solution)/shard_map/ppermute | solution.py:18
  380.1 58.1 %collective-permute-start.52 = (bf16[192,3456]{1,0:T(8,128)(2,1)}, bf16[192,3456]{1,0:T(8,128)(2,1)}, u32[]{:S(2)}, u32[]{:S(2)}) collective-permute-start(bf16[192,3456]{1,0:T(8,128)(2,1)} %constant_dynamic-update-slice_fusion.34.refs_0_), channel_id=1, source_target_pairs={{0,2},{1,3},{2,0},{3,1},{4,6},{5,7},{6,4},{7,5},{8,10},{9,11},{10,... | collective-permute-start | bytes 3981320 | tf_op jit(solution)/shard_map/ppermute | solution.py:18
  392.8 45.5 %collective-permute-start.54 = (bf16[96,5760]{1,0:T(8,128)(2,1)}, bf16[96,5760]{1,0:T(8,128)(2,1)}, u32[]{:S(2)}, u32[]{:S(2)}) collective-permute-start(bf16[96,5760]{1,0:T(8,128)(2,1)} %pad_maximum_fusion.4), channel_id=1, source_target_pairs={{0,16},{16,0},{1,17},{17,1},{2,18},{18,2},{3,19},{19,3},{4,20},{20... | collective-permute-start | bytes 3317768 | tf_op jit(solution)/shard_map/ppermute | solution.py:18
  451.4 64.5 %collective-permute-start.63 = (bf16[192,5760]{1,0:T(8,128)(2,1)}, bf16[192,5760]{1,0:T(8,128)(2,1)}, u32[]{:S(2)}, u32[]{:S(2)}) collective-permute-start(bf16[192,5760]{1,0:T(8,128)(2,1)} %constant_dynamic-update-slice_fusion.44.refs_0_), channel_id=1, source_target_pairs={{0,2},{1,3},{2,0},{3,1},{4,6},{5,7},{6,4},{7,5},{8,10},{9,11},{10,... | collective-permute-start | bytes 6635528 | tf_op jit(solution)/shard_map/ppermute | solution.py:18
  453.6 75.6 %collective-permute-start.67 = (bf16[192,5760]{1,0:T(8,128)(2,1)}, bf16[192,5760]{1,0:T(8,128)(2,1)}, u32[]{:S(2)}, u32[]{:S(2)}) collective-permute-start(bf16[192,5760]{1,0:T(8,128)(2,1)} %constant_dynamic-update-slice_fusion.44.refs_0_), channel_id=1, source_target_pairs={{0,1},{1,0},{2,3},{3,2},{4,5},{5,4},{6,7},{7,6},{8,9},{9,8},{10,11... | collective-permute-start | bytes 6635528 | tf_op jit(solution)/shard_map/ppermute | solution.py:18
  454.5 59.9 %collective-permute-start.64 = (bf16[128,5760]{1,0:T(8,128)(2,1)}, bf16[128,5760]{1,0:T(8,128)(2,1)}, u32[]{:S(2)}, u32[]{:S(2)}) collective-permute-start(bf16[128,5760]{1,0:T(8,128)(2,1)} %constant_dynamic-update-slice_fusion.49.refs_1_), channel_id=1, source_target_pairs={{0,16},{16,0},{1,17},{17,1},{2,18},{18,2},{3,19},{19,3},{4,20},{20... | collective-permute-start | bytes 4423688 | tf_op jit(solution)/shard_map/ppermute | solution.py:18
  670.5 68.6 %collective-permute-start.85 = (bf16[640,5760]{1,0:T(8,128)(2,1)}, bf16[640,5760]{1,0:T(8,128)(2,1)}, u32[]{:S(2)}, u32[]{:S(2)}) collective-permute-start(bf16[640,5760]{1,0:T(8,128)(2,1)} %away_grad.4), channel_id=1, source_target_pairs={{0,1},{1,0},{2,3},{3,2},{4,5},{5,4},{6,7},{7,6},{8,9},{9,8},{10,11... | collective-permute-start | bytes 22118408 | tf_op jit(solution)/shard_map/ppermute | solution.py:18
  683.2 58.8 %collective-permute-start.83 = (f32[16,512]{1,0:T(8,128)}, f32[16,512]{1,0:T(8,128)}, u32[]{:S(2)}, u32[]{:S(2)}) collective-permute-start(f32[16,512]{1,0:T(8,128)} %slice_bitcast_fusion.3.totals_ref), channel_id=1, source_target_pairs={{0,16},{16,0},{1,17},{17,1},{2,18},{18,2},{3,19},{19,3},{4,20},{20... | collective-permute-start | bytes 98312 | tf_op jit(solution)/shard_map/ppermute | solution.py:18
  695.1 46.9 %collective-permute-start.82 = (bf16[512,1152]{1,0:T(8,128)(2,1)}, bf16[512,1152]{1,0:T(8,128)(2,1)}, u32[]{:S(2)}, u32[]{:S(2)}) collective-permute-start(bf16[512,1152]{1,0:T(8,128)(2,1)} %fusion.30.grad_ref), channel_id=1, source_target_pairs={{0,16},{16,0},{1,17},{17,1},{2,18},{18,2},{3,19},{19,3},{4,20},{20... | collective-permute-start | bytes 3538952 | tf_op jit(solution)/shard_map/ppermute | solution.py:18
  699.6 42.4 %collective-permute-start.84 = (f32[16,512]{1,0:T(8,128)}, f32[16,512]{1,0:T(8,128)}, u32[]{:S(2)}, u32[]{:S(2)}) collective-permute-start(f32[16,512]{1,0:T(8,128)} %fusion.42.along_ref), channel_id=1, source_target_pairs={{0,16},{16,0},{1,17},{17,1},{2,18},{18,2},{3,19},{19,3},{4,20},{20... | collective-permute-start | bytes 98312 | tf_op jit(solution)/shard_map/ppermute | solution.py:18
  770.6 80.4 %collective-permute-start.90 = (bf16[640,3456]{1,0:T(8,128)(2,1)}, bf16[640,3456]{1,0:T(8,128)(2,1)}, u32[]{:S(2)}, u32[]{:S(2)}) collective-permute-start(bf16[640,3456]{1,0:T(8,128)(2,1)} %away_grad.5), channel_id=1, source_target_pairs={{0,1},{1,0},{2,3},{3,2},{4,5},{5,4},{6,7},{7,6},{8,9},{9,8},{10,11... | collective-permute-start | bytes 13271048 | tf_op jit(solution)/shard_map/ppermute | solution.py:18
  790.2 60.8 %collective-permute-start.88 = (bf16[192,5760]{1,0:T(8,128)(2,1)}, bf16[192,5760]{1,0:T(8,128)(2,1)}, u32[]{:S(2)}, u32[]{:S(2)}) collective-permute-start(bf16[192,5760]{1,0:T(8,128)(2,1)} %get-tuple-element.394), channel_id=1, source_target_pairs={{0,2},{1,3},{2,0},{3,1},{4,6},{5,7},{6,4},{7,5},{8,10},{9,11},{10,... | collective-permute-start | bytes 6635528 | tf_op jit(solution)/shard_map/ppermute | solution.py:18
  865.4 41.4 %collective-permute-start.93 = (bf16[2304,1152]{1,0:T(8,128)(2,1)}, bf16[2304,1152]{1,0:T(8,128)(2,1)}, u32[]{:S(2)}, u32[]{:S(2)}) collective-permute-start(bf16[2304,1152]{1,0:T(8,128)(2,1)} %convolution_convert_fusion), channel_id=1, source_target_pairs={{0,1},{1,0},{2,3},{3,2},{4,5},{5,4},{6,7},{7,6},{8,9},{9,8},{10,11... | collective-permute-start | bytes 15925256 | tf_op jit(solution)/shard_map/ppermute | solution.py:18
  882.4 60.0 %collective-permute-start.94 = (bf16[192,3456]{1,0:T(8,128)(2,1)}, bf16[192,3456]{1,0:T(8,128)(2,1)}, u32[]{:S(2)}, u32[]{:S(2)}) collective-permute-start(bf16[192,3456]{1,0:T(8,128)(2,1)} %get-tuple-element.411), channel_id=1, source_target_pairs={{0,2},{1,3},{2,0},{3,1},{4,6},{5,7},{6,4},{7,5},{8,10},{9,11},{10,... | collective-permute-start | bytes 3981320 | tf_op jit(solution)/shard_map/ppermute | solution.py:18
  883.1 59.4 %collective-permute-start.95 = (bf16[128,3456]{1,0:T(8,128)(2,1)}, bf16[128,3456]{1,0:T(8,128)(2,1)}, u32[]{:S(2)}, u32[]{:S(2)}) collective-permute-start(bf16[128,3456]{1,0:T(8,128)(2,1)} %get-tuple-element.412), channel_id=1, source_target_pairs={{0,16},{16,0},{1,17},{17,1},{2,18},{18,2},{3,19},{19,3},{4,20},{20... | collective-permute-start | bytes 2654216 | tf_op jit(solution)/shard_map/ppermute | solution.py:18
  890.2 379.2 %all-gather.5.cloned.1.call-start = ((), (), s32[]{:S(2)}) async-start(), calls=%async_computation.1 | async-start | bytes 3649536 | tf_op jit(solution)/shard_map/all_gather | solution.py:1136
  915.8 41.8 %collective-permute-start.97 = (bf16[576,1152]{1,0:T(8,128)(2,1)}, bf16[576,1152]{1,0:T(8,128)(2,1)}, u32[]{:S(2)}, u32[]{:S(2)}) collective-permute-start(bf16[576,1152]{1,0:T(8,128)(2,1)} %get-tuple-element.415), channel_id=1, source_target_pairs={{0,2},{1,3},{2,0},{3,1},{4,6},{5,7},{6,4},{7,5},{8,10},{9,11},{10,... | collective-permute-start | bytes 3981320 | tf_op jit(solution)/shard_map/ppermute | solution.py:18
  917.1 40.5 %collective-permute-start.98 = (bf16[576,1152]{1,0:T(8,128)(2,1)}, bf16[576,1152]{1,0:T(8,128)(2,1)}, u32[]{:S(2)}, u32[]{:S(2)}) collective-permute-start(bf16[576,1152]{1,0:T(8,128)(2,1)} %get-tuple-element.416), channel_id=1, source_target_pairs={{0,16},{16,0},{1,17},{17,1},{2,18},{18,2},{3,19},{19,3},{4,20},{20... | collective-permute-start | bytes 3981320 | tf_op jit(solution)/shard_map/ppermute | solution.py:18
  997.1 66.7 %collective-permute-start.107 = (bf16[640,5760]{1,0:T(8,128)(2,1)}, bf16[640,5760]{1,0:T(8,128)(2,1)}, u32[]{:S(2)}, u32[]{:S(2)}) collective-permute-start(bf16[640,5760]{1,0:T(8,128)(2,1)} %away_grad.6), channel_id=1, source_target_pairs={{0,1},{1,0},{2,3},{3,2},{4,5},{5,4},{6,7},{7,6},{8,9},{9,8},{10,11... | collective-permute-start | bytes 22118408 | tf_op jit(solution)/shard_map/ppermute | solution.py:18
  1004.5 89.5 %collective-permute-start.104 = (f32[16,512]{1,0:T(8,128)}, f32[16,512]{1,0:T(8,128)}, u32[]{:S(2)}, u32[]{:S(2)}) collective-permute-start(f32[16,512]{1,0:T(8,128)} %slice_bitcast_fusion.2.totals_ref), channel_id=1, source_target_pairs={{0,16},{16,0},{1,17},{17,1},{2,18},{18,2},{3,19},{19,3},{4,20},{20... | collective-permute-start | bytes 98312 | tf_op jit(solution)/shard_map/ppermute | solution.py:18
  1007.1 54.6 %collective-permute-start.106 = (bf16[40,5760]{1,0:T(8,128)(2,1)}, bf16[40,5760]{1,0:T(8,128)(2,1)}, u32[]{:S(2)}, u32[]{:S(2)}) collective-permute-start(bf16[40,5760]{1,0:T(8,128)(2,1)} %pad_maximum_fusion.30), channel_id=1, source_target_pairs={{0,8},{1,9},{2,10},{3,11},{4,12},{5,13},{6,14},{7,15},{8,0},{9,1},... | collective-permute-start | bytes 1382408 | tf_op jit(solution)/shard_map/ppermute | solution.py:18
  1073.8 47.7 %collective-permute-start.110 = (bf16[144,1152]{1,0:T(8,128)(2,1)}, bf16[144,1152]{1,0:T(8,128)(2,1)}, u32[]{:S(2)}, u32[]{:S(2)}) collective-permute-start(bf16[144,1152]{1,0:T(8,128)(2,1)} %pad_maximum_fusion.36), channel_id=1, source_target_pairs={{0,8},{1,9},{2,10},{3,11},{4,12},{5,13},{6,14},{7,15},{8,0},{9,1},... | collective-permute-start | bytes 995336 | tf_op jit(solution)/shard_map/ppermute | solution.py:18
  1087.4 52.2 %collective-permute-start.111 = (bf16[192,5760]{1,0:T(8,128)(2,1)}, bf16[192,5760]{1,0:T(8,128)(2,1)}, u32[]{:S(2)}, u32[]{:S(2)}) collective-permute-start(bf16[192,5760]{1,0:T(8,128)(2,1)} %get-tuple-element.440), channel_id=1, source_target_pairs={{0,2},{1,3},{2,0},{3,1},{4,6},{5,7},{6,4},{7,5},{8,10},{9,11},{10,... | collective-permute-start | bytes 6635528 | tf_op jit(solution)/shard_map/ppermute | solution.py:18
  1094.0 45.5 %collective-permute-start.112 = (bf16[128,5760]{1,0:T(8,128)(2,1)}, bf16[128,5760]{1,0:T(8,128)(2,1)}, u32[]{:S(2)}, u32[]{:S(2)}) collective-permute-start(bf16[128,5760]{1,0:T(8,128)(2,1)} %get-tuple-element.441), channel_id=1, source_target_pairs={{0,16},{16,0},{1,17},{17,1},{2,18},{18,2},{3,19},{19,3},{4,20},{20... | collective-permute-start | bytes 4423688 | tf_op jit(solution)/shard_map/ppermute | solution.py:18
  1094.9 44.7 %collective-permute-start.113 = (bf16[40,3456]{1,0:T(8,128)(2,1)}, bf16[40,3456]{1,0:T(8,128)(2,1)}, u32[]{:S(2)}, u32[]{:S(2)}) collective-permute-start(bf16[40,3456]{1,0:T(8,128)(2,1)} %pad_maximum_fusion.37), channel_id=1, source_target_pairs={{0,8},{1,9},{2,10},{3,11},{4,12},{5,13},{6,14},{7,15},{8,0},{9,1},... | collective-permute-start | bytes 829448 | tf_op jit(solution)/shard_map/ppermute | solution.py:18
  (294 other events, 3734.6 us)
Sparse Core Ops, SparseCore 0:
  890.3 67.8 all-gather.2
  1193.5 75.8 all-gather.4

commit v3 on v2

--- a/solution.py
+++ b/solution.py
@@ -253,15 +253,6 @@
             _, parts = flight.send(parts)
     except StopIteration:
         pass
-
-
-def modulation_flight(block, bias, stages, result):
-    for stage in stages[:-1]:
-        half = block.shape[0] // 2
-        arrived = yield 1, swap_bit(block[half:], stage)
-        block = block[:half] + arrived
-    arrived = yield 1, swap_bit(block, stages[-1])
-    result.append(block + arrived + bias[None])
 
 
 def gather_flight(shard, rows, cut, routes, waits, result):
@@ -523,6 +514,84 @@
         ),
         name=name,
     )(right, order, *operands)
+
+
+def project_norm_back(right, tiles, order, inputs, residual, scale, branch, gate, name):
+    rows = right.shape[0]
+    operands = tiles.operands()
+    width = order.shape[1]
+    groups = scale.shape[0]
+    span = rows // groups
+    gated = branch is not None
+    chunk = min(span, 128)
+
+    def kernel(right_ref, order_ref, inputs_ref, residual_ref, scale_ref, *refs):
+        if gated:
+            branch_ref, gate_ref, refs = refs[0], refs[1], refs[2:]
+        pieces, refs = refs[:8], refs[8:]
+        if gated:
+            after_ref, product_ref, sums_ref, total_ref = refs
+        else:
+            after_ref, sums_ref, total_ref = refs
+        index = pl.program_id(0)
+
+        @pl.when(index == 0)
+        def _():
+            total_ref[...] = jnp.zeros_like(total_ref)
+
+        total_ref[...] += contract(right_ref[...], tiles.weight(pieces), 1, 1)
+
+        @pl.when(index == tiles.count - 1)
+        def _():
+            sums_ref[...] = jnp.zeros_like(sums_ref)
+
+            def add_sum(row, values):
+                along = jnp.sum(values, axis=0, keepdims=True)
+                sums_ref[row : row + 1, :] = sums_ref[row : row + 1, :] + along
+
+            for low in range(0, rows, chunk):
+                at = pl.ds(low, chunk)
+                group = low // span
+                rest = total_ref[at, :]
+                high = rest.astype(BF)
+                grad = jnp.dot(high, order_ref[...], preferred_element_type=F32)
+                lower = (rest - high.astype(F32)).astype(BF)
+                grad = grad + jnp.dot(lower, order_ref[...], preferred_element_type=F32)
+                normed, inverse = normalize(inputs_ref[at, :])
+                add_sum(group, grad)
+                add_sum(groups + group, grad * normed)
+                after = residual_ref[at, :] + normalize_back(
+                    grad * (1.0 + scale_ref[group : group + 1, :]), normed, inverse
+                )
+                after_ref[at, :] = after
+                if gated:
+                    product = (after * gate_ref[group : group + 1, :]).astype(BF)
+                    product_ref[at, :] = product
+                    add_sum(2 * groups + group, after * branch_ref[at, :])
+                    add_sum(3 * groups, product.astype(F32))
+
+    whole = lambda shape: pl.BlockSpec(shape, lambda j: (0, 0))
+    wide = jax.ShapeDtypeStruct((rows, width), F32)
+    outs = [wide] + ([jax.ShapeDtypeStruct((rows, width), BF)] if gated else [])
+    outs.append(jax.ShapeDtypeStruct((3 * groups + 2, width), F32))
+    extra = [branch, gate] if gated else []
+    others = [order, inputs, residual, scale, *extra]
+    return pl.pallas_call(
+        kernel,
+        out_shape=outs,
+        grid=(tiles.count,),
+        in_specs=[
+            pl.BlockSpec((rows, tiles.tile), lambda j: (0, j)),
+            *[whole(array.shape) for array in others],
+            *tiles.specs(),
+        ],
+        out_specs=[whole(out.shape) for out in outs],
+        scratch_shapes=[pltpu.VMEM((rows, tiles.rows), F32)],
+        cost_estimate=cost(
+            2 * rows * tiles.rows * (tiles.columns() + 2 * width), [right, *others, *outs, *operands]
+        ),
+        name=name,
+    )(right, *others, *operands)
 
 
 def hidden_back(down_grad, full_down, pre, channel_on, tile):
@@ -902,7 +971,7 @@
     gathered = []
 
     def unit_ticks(unit):
-        early = ((0, 1, 2, 4, 7, 8), (0, 2, 4, 9, 11, 12), (5, 9, 10, 12, 14, 15))
+        early = ((0, 1, 2, 4, 7, 8), (0, 2, 4, 9, 11, 12), (5, 9, 10, 13, 14, 15))
         late = ((9, 10, 13, 14, 16, 17), (10, 13, 14, 16, 20, 21), (14, 16, 19, 20, 24, 25))
         if unit < 3:
             return early[unit]
@@ -992,25 +1061,24 @@
     )
 
     mod_stages = [("seq", bit) for bit in range(seq_bits)] + [("fsdp", 0)]
-    modulations = [[] for _ in range(layer_count)]
 
     def modulation_part(layer):
         return jnp.dot(cond_relative, mod_weight[layer], preferred_element_type=F32)
 
     full_biases = unpack_biases(every_small)
-    block = feed.tick(modulation_part(0))
+    block = jnp.concatenate([modulation_part(layer) for layer in range(layer_count)], axis=1)
+    block = feed.tick(block)
     for index, stage in enumerate(mod_stages[:-1]):
         half = block.shape[0] // 2
         block = block[:half] + swap_bit(block[half:], stage)
         if index == 1:
-            block, full_biases = feed.tick((block, full_biases))
-    block = feed.tick(block + swap_bit(block, mod_stages[-1]))
-    modulations[0].append(block + full_biases[4][0][None])
-    for layer in range(1, layer_count):
-        flight = modulation_flight(
-            modulation_part(layer), full_biases[4][layer], mod_stages, modulations[layer]
-        )
-        feed.at(10 * layer - 1, flight)
+            block = feed.tick(block)
+    block, full_biases = feed.tick((block + swap_bit(block, mod_stages[-1]), full_biases))
+    mod_width = block.shape[1] // layer_count
+    modulations = [
+        block[:, layer * mod_width : (layer + 1) * mod_width] + full_biases[4][layer][None]
+        for layer in range(layer_count)
+    ]
 
     group_item = (
         (half_index * local_rows + jnp.arange(group_count, dtype=jnp.int32) * group_rows)
@@ -1051,8 +1119,7 @@
     full_downs = []
     for layer in range(layer_count):
         pair_bias, out_b, up_b, down_b = (full_biases[index][layer] for index in range(4))
-        current = feed.until(modulations[layer], current)
-        (modulation,) = modulations[layer]
+        modulation = modulations[layer]
         shift_one, scale_one, gate_one, shift_two, scale_two, gate_two = jnp.split(
             of_groups(modulation), 6, axis=2
         )
@@ -1166,18 +1233,22 @@
         )
         grad_up_bias = grad_up_bias[0]
         up_grad = feed.tick(feed.tick(up_grad))
-        grad_h2 = grouped(project_back(up_grad, up_tiles(layer), order, 2, "back_up"))
-        grad_h2 = feed.tick(grad_h2)
-        normed_two, inverse_two = normalize(saved["after_attn"])
-        grad_shift_two = jnp.sum(grad_h2, axis=1)
-        grad_scale_two = jnp.sum(grad_h2 * normed_two, axis=1)
-        grad_after = grad_current + normalize_back(
-            grad_h2 * (1.0 + saved["scale_two"]), normed_two, inverse_two
-        )
-        out_grad = ungrouped((grad_after * saved["gate_one"]).astype(BF))
-        grad_gate_one = jnp.sum(grad_after * saved["branch_one"], axis=1)
-        grad_out_bias = jnp.sum(out_grad.astype(F32), axis=0)
-        out_grad = feed.tick(out_grad)
+        grad_after, out_grad, sums_two = project_norm_back(
+            up_grad,
+            up_tiles(layer),
+            order,
+            ungrouped(saved["after_attn"]),
+            ungrouped(grad_current),
+            saved["scale_two"][:, 0],
+            ungrouped(saved["branch_one"]),
+            saved["gate_one"][:, 0],
+            "back_up",
+        )
+        grad_shift_two, grad_scale_two, grad_gate_one = (
+            sums_two[part * group_count : (part + 1) * group_count] for part in range(3)
+        )
+        grad_out_bias = sums_two[3 * group_count]
+        out_grad = feed.tick(feed.tick(out_grad))
         lefts, rights = (saved["low_two"], saved["mixed_low"]), (up_grad, out_grad)
         up_waits = (2, 0, 2, 2, 2, 1) if last else (2, 0, 2, 2, 2, 3)
         scatter_ordered(lefts, rights, up_waits, up_rows)
@@ -1220,17 +1291,24 @@
         )
         grad_qkv = feed.tick(grad_qkv)
         grad_qkv_bias = jnp.sum(grad_qkv.astype(F32), axis=0)
-        qkv_waits = (1, 1, 3, 1) if last else (1, 0, 4, 2, 1, 2)
+        qkv_waits = (1, 1, 1, 2) if last else (1, 0, 4, 2, 1, 2)
         scatter_ordered((saved["low_one"],), (grad_qkv,), qkv_waits, qkv_rows)
         if last:
             grad_qkv = feed.tick(feed.tick(grad_qkv))
-        grad_h1 = grouped(project_back(grad_qkv, qkv_tiles(layer), order, 2, "back_qkv"))
-        grad_h1 = feed.tick(grad_h1)
-        normed_one, inverse_one = normalize(saved["inputs"])
-        grad_shift_one = jnp.sum(grad_h1, axis=1)
-        grad_scale_one = jnp.sum(grad_h1 * normed_one, axis=1)
-        grad_inputs = grad_after + normalize_back(
-            grad_h1 * (1.0 + saved["scale_one"]), normed_one, inverse_one
+        grad_inputs, sums_one = project_norm_back(
+            grad_qkv,
+            qkv_tiles(layer),
+            order,
+            ungrouped(saved["inputs"]),
+            grad_after,
+            saved["scale_one"][:, 0],
+            None,
+            None,
+            "back_qkv",
+        )
+        grad_inputs = grouped(feed.tick(grad_inputs))
+        grad_shift_one, grad_scale_one = (
+            sums_one[part * group_count : (part + 1) * group_count] for part in range(2)
         )
         grad_groups = jnp.concatenate(
             [

time: 1310 us -> 1260 us (0.962)
  other arithmetic: 193 us -> 140 us
  local copies, waits for them, and re-layouts: 192 us -> 155 us
  waiting for transfers between devices: 235 us -> 270 us
    pallas_call x0 -> x4, Pallas kernels: none -> 75.6 us  [project_norm_back(): pl.pallas_call(kernel, out_shape=outs, grid=(tiles.count,), in_specs=[pl....]
    pallas_call x6 -> x2, Pallas kernels: 80 us -> 16.3 us  [project_back(): pl.pallas_call(kernel, out_shape=out, grid=(tiles.count,), in_specs=[pl.B...]
    ppermute x125 -> x120, waiting for transfers between devices: 233 us -> 267 us  [swap_bit(): lax.ppermute(block, axis, [(low, low ^ 1 << bit) for low in range(count)])]
    reduce_sum x8 -> x1, other arithmetic: 26.5 us -> 2.58 us  [body(): grad_gate_two = jnp.sum(kept_grad * saved['branch_two'], axis=1)]
    unnamed x479 -> x413, local copies, waits for them, and re-layouts: 106 us -> 86.5 us
    ppermute x125 -> x120, starting transfers between devices: 105 us -> 104 us  [swap_bit(): lax.ppermute(block, axis, [(low, low ^ 1 << bit) for low in range(count)])]
  transfers between devices with their start and end apart: 127 -> 122, of which waited for: 38 -> 37; matrix products, arithmetic and copies ran while one was open for 30% -> 25% of each run, Pallas kernels for 34% -> 36%
where the time goes in v3:
time: 1260 us; the launch traced here: 1250 us
  Pallas kernels  490 us (39%)
  waiting for transfers between devices  270 us (21%)
  local copies, waits for them, and re-layouts  155 us (12%)
  other arithmetic  140 us (11%)
  starting transfers between devices  104 us (8%)
  matrix products  78.2 us (6%)
  between operations  16.9 us (1%)
    ppermute x120, waiting for transfers between devices, swap_bit(): lax.ppermute(block, axis, [(low, low ^ 1 << bit) for low in range(count)])  267 us
    ppermute x120, starting transfers between devices, swap_bit(): lax.ppermute(block, axis, [(low, low ^ 1 << bit) for low in range(count)])  104 us
    unnamed x413, local copies, waits for them, and re-layouts  86.5 us
    pallas_call x4, Pallas kernels, project_norm_back(): pl.pallas_call(kernel, out_shape=outs, grid=(tiles.count,), in_specs=[pl....  75.6 us
    pallas_call x8, Pallas kernels, call(): pl.pallas_call(kernel, out_shape=outs, grid=(sum(self.counts),), in_specs...  73.8 us
    dot_general x14, matrix products, contract(): lax.dot_general(left, right, (((left_dim,), (right_dim,)), ((), ())), pre...  72.8 us
    pallas_call x2, Pallas kernels, attend_back(): pl.pallas_call(kernel, out_shape=outs, grid=(head_count,), in_specs=in_sp...  66.3 us
    pallas_call x2, Pallas kernels, attend(): pl.pallas_call(kernel, out_shape=[mixed, wide, totals], grid=(head_count,...  54.5 us
  transfers between devices with their start and end apart: 122, of which 37 were waited for; matrix products, arithmetic and copies ran while one was open for 25% of the time, Pallas kernels for 36%

profile of v3, /device:TPU:0, one launch (start us, length us, event | category | flops | bytes accessed | tf_op | source)
XLA Modules:
  0.0 1254.6 jit_solution(18196060722998935201)
XLA Ops:
  54.7 10.7 collective-permute-done.7
  111.4 19.2 %collective-permute-done.9 = f32[16,13824]{1,0:T(8,128)S(1)} collective-permute-done((f32[16,13824]{1,0:T(8,128)S(1)}, f32[16,13824]{1,0:T(8,128)S(1)}, u32[]{:S(2)}, u32[]{:S(2)}) %collective-permute-start.9) | collective-permute-done | bytes 884768 | tf_op jit(solution)/shard_map/ppermute | solution.py:18
  183.9 10.3 project_qkv.2.qkv_ref.key_ref.value_ref
  238.7 27.1 %attend.2 = (bf16[512,1152]{1,0:T(8,128)(2,1)}, f32[512,1152]{1,0:T(8,128)}, f32[512,128]{1,0:T(8,128)}) custom-call(bf16[512,3456]{1,0:T(8,128)(2,1)} %project_qkv.2.qkv_ref.key_ref.value_ref, bf16[512,3456]{1,0:T(8,128)(2,1)} %project_other.2.key_ref.value_ref.other_ref, bf16[512,3456]{1,0:T(8,128)(2,1)} %project_other.2.key_ref.value_ref.other_ref, ...), custom_call_target="tpu_custom_call" | custom-call | flops 8589934592 | bytes 8257536 | tf_op jit(solution)/shard_map/attend/pallas_call | solution.py:704
  304.2 10.7 collective-permute-done.37
  330.7 14.5 %project_up.2 = (f32[512,4608]{1,0:T(8,128)}, bf16[4608,512]{1,0:T(8,128)(2,1)}) custom-call(bf16[512,1280]{1,0:T(8,128)(2,1)} %fusion.12.left_ref.refs_0_, f32[1,4608]{1,0:T(1,128)} %reshape.577.bias_ref, f32[2,4608]{1,0:T(2,128)} %get-tuple-element.575.channel_ref, bf16[192,5760]{1,0:T(8,128)(2,1)} %copy-done.10, ...), custom_call_target="tpu_custom_call" | custom-call | flops 6039797760 | bytes 30212096 | tf_op jit(solution)/shard_map/project_up/pallas_call | solution.py:452
  345.2 10.9 collective-permute-done.41
  389.2 13.1 %fusion.90 = (f32[512]{0:T(512)S(1)}, f32[512,1152]{1,0:T(8,128)S(1)}, f32[512,1152]{1,0:T(8,128)}) fusion(f32[512,1152]{1,0:T(8,128)} %copy-done.3, f32[2,1152]{1,0:T(2,128)S(1)} %get-tuple-element.770, f32[512]{0:T(512)S(1)} %bitcast.318, f32[1152]{0:T(1024)} %reshape_squeeze.36, bf16[4608,512]{1,0:T(8,128)(2,1)} %get-tuple-element.317, ...), kind=kOutput, calls=%fused_computation.443 | convolution fusion | flops 5438766592 | bytes 22431232 | tf_op jit(solution)/shard_map/dot_general | solution.py:27
  451.6 9.9 project_other.3.key_ref.value_ref.other_ref
  469.1 27.4 %attend.3 = (bf16[512,1152]{1,0:T(8,128)(2,1)}, f32[512,1152]{1,0:T(8,128)}, f32[512,128]{1,0:T(8,128)}) custom-call(bf16[512,3456]{1,0:T(8,128)(2,1)} %project_qkv.3.qkv_ref.key_ref.value_ref, bf16[512,3456]{1,0:T(8,128)(2,1)} %project_other.3.key_ref.value_ref.other_ref, bf16[512,3456]{1,0:T(8,128)(2,1)} %project_other.3.key_ref.value_ref.other_ref, ...), custom_call_target="tpu_custom_call" | custom-call | flops 8589934592 | bytes 8257536 | tf_op jit(solution)/shard_map/attend/pallas_call | solution.py:704
  523.9 14.5 %project_up.3 = (f32[512,4608]{1,0:T(8,128)}, bf16[4608,512]{1,0:T(8,128)(2,1)}) custom-call(bf16[512,1280]{1,0:T(8,128)(2,1)} %fusion.16.left_ref.refs_0_, f32[1,4608]{1,0:T(1,128)} %reshape.589.bias_ref, f32[2,4608]{1,0:T(2,128)} %get-tuple-element.574.channel_ref, bf16[192,5760]{1,0:T(8,128)(2,1)} %constant_dynamic-update-slice_fusion.44.refs_0_.refs_2_, ...), custom_call_target="tpu_custom_call" | custom-call | flops 6039797760 | bytes 30212096 | tf_op jit(solution)/shard_map/project_up/pallas_call | solution.py:452
  569.6 16.3 %hidden_back.2 = (bf16[512,4608]{1,0:T(8,128)(2,1)}, f32[1,4608]{1,0:T(1,128)}) custom-call(bf16[512,1152]{1,0:T(8,128)(2,1)} %copy-done.15, bf16[4608,1152]{1,0:T(8,128)(2,1)} %bitcast.284, f32[512,4608]{1,0:T(8,128)} %get-tuple-element.367.pre_ref, f32[2,4608]{1,0:T(2,128)} %get-tuple-element.574.channel_ref), custom_call_target="tpu_custom_call" | custom-call | flops 5435817984 | bytes 25952256 | tf_op jit(solution)/shard_map/hidden_back/pallas_call | solution.py:622
  600.3 20.5 %back_up.2 = (f32[512,1152]{1,0:T(8,128)}, bf16[512,1152]{1,0:T(8,128)(2,1)}, f32[8,1152]{1,0:T(8,128)}) custom-call(bf16[512,4608]{1,0:T(8,128)(2,1)} %get-tuple-element.376.right_ref.refs_2_, bf16[1280,1152]{1,0:T(8,128)(2,1)} %fusion.order_ref, f32[512,1152]{1,0:T(8,128)} %copy-done.1, f32[512,1152]{1,0:T(8,128)} %residual_ref.1, ...), custom_call_target="tpu_custom_call" | custom-call | flops 9059696640 | bytes 33085440 | tf_op jit(solution)/shard_map/back_up/pallas_call | solution.py:579
  656.6 12.7 %multiply_reduce_fusion.1 = (f32[2,1152]{1,0:T(2,128)}, f32[512,1152]{1,0:T(8,128)S(1)}) fusion(f32[2,256]{1,0:T(2,128)S(1)} %convert_element_type.971, f32[512,1152]{1,0:T(8,128)} %residual_ref.1, f32[1152]{0:T(1024)S(1)} %copy-done.134, bf16[4608,512]{1,0:T(8,128)(2,1)} %get-tuple-element.361, bf16[4608,1152]{1,0:T(8,128)(2,1)} %bitcast.285), kind=kOutput, calls=%fused_computation.63 | convolution fusion | flops 5438175232 | bytes 20069888 | tf_op jit(solution)/shard_map/dot_general | solution.py:27
  687.5 33.1 %attend_back.2 = (bf16[512,1152]{1,0:T(8,128)(2,1)}, f32[512,2304]{1,0:T(8,128)}) custom-call(bf16[512,3456]{1,0:T(8,128)(2,1)} %project_qkv.3.qkv_ref.key_ref.value_ref, bf16[512,3456]{1,0:T(8,128)(2,1)} %project_other.3.key_ref.value_ref.other_ref, bf16[512,3456]{1,0:T(8,128)(2,1)} %project_other.3.key_ref.value_ref.other_ref, ...), custom_call_target="tpu_custom_call" | custom-call | flops 17179869184 | bytes 12976128 | tf_op jit(solution)/shard_map/attend_back/pallas_call | solution.py:776
  723.1 21.5 %attend_back_other.2.right_ref.refs_1_ = bf16[512,3456]{1,0:T(8,128)(2,1)} custom-call(bf16[512,3456]{1,0:T(8,128)(2,1)} %project_qkv.3.qkv_ref.key_ref.value_ref, bf16[512,3456]{1,0:T(8,128)(2,1)} %project_qkv.3.qkv_ref.key_ref.value_ref, bf16[512,3456]{1,0:T(8,128)(2,1)} %project_other.3.key_ref.value_ref.other_ref, ...), custom_call_target="tpu_custom_call" | custom-call | flops 8589934592 | bytes 11796480 | tf_op jit(solution)/shard_map/attend_back_other/pallas_call | solution.py:845
  753.5 12.5 stay_grad.4
  776.7 17.0 %back_qkv.2 = (f32[512,1152]{1,0:T(8,128)}, f32[8,1152]{1,0:T(8,128)}) custom-call(bf16[512,3456]{1,0:T(8,128)(2,1)} %attend_back_other.2.right_ref.refs_1_, bf16[1280,1152]{1,0:T(8,128)(2,1)} %fusion.order_ref, f32[512,1152]{1,0:T(8,128)} %copy-done, f32[512,1152]{1,0:T(8,128)} %get-tuple-element.394.residual_ref, f32[2,1152]{1,0:T(2,128)} %get-tuple-element.774.scale_ref, ...), custom_call_target="tpu_custom_call" | custom-call | flops 7549747200 | bytes 22459392 | tf_op jit(solution)/shard_map/back_qkv/pallas_call | solution.py:579
  802.0 14.7 %collective-permute-done.83 = bf16[192,5760]{1,0:T(8,128)(2,1)} collective-permute-done((bf16[192,5760]{1,0:T(8,128)(2,1)}, bf16[192,5760]{1,0:T(8,128)(2,1)}, u32[]{:S(2)}, u32[]{:S(2)}) %collective-permute-start.83) | collective-permute-done | bytes 2211872 | tf_op jit(solution)/shard_map/ppermute | solution.py:18
  845.7 16.4 %hidden_back.3 = (bf16[512,4608]{1,0:T(8,128)(2,1)}, f32[1,4608]{1,0:T(1,128)}) custom-call(bf16[512,1152]{1,0:T(8,128)(2,1)} %bitcast.290, bf16[4608,1152]{1,0:T(8,128)(2,1)} %bitcast.283, f32[512,4608]{1,0:T(8,128)} %get-tuple-element.400.pre_ref, f32[2,4608]{1,0:T(2,128)} %get-tuple-element.575.channel_ref), custom_call_target="tpu_custom_call" | custom-call | flops 5435817984 | bytes 25952256 | tf_op jit(solution)/shard_map/hidden_back/pallas_call | solution.py:622
  882.8 20.9 %back_up.3 = (f32[512,1152]{1,0:T(8,128)}, bf16[512,1152]{1,0:T(8,128)(2,1)}, f32[8,1152]{1,0:T(8,128)}) custom-call(bf16[512,4608]{1,0:T(8,128)(2,1)} %get-tuple-element.412.right_ref.refs_2_, bf16[1280,1152]{1,0:T(8,128)(2,1)} %fusion.order_ref, f32[512,1152]{1,0:T(8,128)} %copy-done.3, f32[512,1152]{1,0:T(8,128)} %get-tuple-element.399, ...), custom_call_target="tpu_custom_call" | custom-call | flops 9059696640 | bytes 33085440 | tf_op jit(solution)/shard_map/back_up/pallas_call | solution.py:579
  907.6 11.2 collective-permute-done.92
  926.9 9.9 away_grad.6
  958.8 12.2 collective-permute-done.96
  978.2 33.1 %attend_back.3 = (bf16[512,1152]{1,0:T(8,128)(2,1)}, f32[512,2304]{1,0:T(8,128)}) custom-call(bf16[512,3456]{1,0:T(8,128)(2,1)} %project_qkv.2.qkv_ref.key_ref.value_ref, bf16[512,3456]{1,0:T(8,128)(2,1)} %project_other.2.key_ref.value_ref.other_ref, bf16[512,3456]{1,0:T(8,128)(2,1)} %project_other.2.key_ref.value_ref.other_ref, ...), custom_call_target="tpu_custom_call" | custom-call | flops 17179869184 | bytes 12976128 | tf_op jit(solution)/shard_map/attend_back/pallas_call | solution.py:776
  1020.7 12.0 stay_grad.6
  1041.4 21.6 %attend_back_other.3.refs_1_.right_ref = bf16[512,3456]{1,0:T(8,128)(2,1)} custom-call(bf16[512,3456]{1,0:T(8,128)(2,1)} %project_qkv.2.qkv_ref.key_ref.value_ref, bf16[512,3456]{1,0:T(8,128)(2,1)} %project_qkv.2.qkv_ref.key_ref.value_ref, bf16[512,3456]{1,0:T(8,128)(2,1)} %project_other.2.key_ref.value_ref.other_ref, ...), custom_call_target="tpu_custom_call" | custom-call | flops 8589934592 | bytes 11796480 | tf_op jit(solution)/shard_map/attend_back_other/pallas_call | solution.py:845
  1107.6 17.2 %back_qkv.3 = (f32[512,1152]{1,0:T(8,128)}, f32[8,1152]{1,0:T(8,128)}) custom-call(bf16[512,3456]{1,0:T(8,128)(2,1)} %attend_back_other.3.refs_1_.right_ref, bf16[1280,1152]{1,0:T(8,128)(2,1)} %fusion.order_ref, f32[512,1152]{1,0:T(8,128)} %convert_element_type.876.inputs_ref, f32[512,1152]{1,0:T(8,128)} %get-tuple-element.455.residual_ref, ...), custom_call_target="tpu_custom_call" | custom-call | flops 7549747200 | bytes 22459392 | tf_op jit(solution)/shard_map/back_qkv/pallas_call | solution.py:579
  1128.7 17.9 %collective-permute-done.113 = bf16[128,3456]{1,0:T(8,128)(2,1)} collective-permute-done((bf16[128,3456]{1,0:T(8,128)(2,1)}, bf16[128,3456]{1,0:T(8,128)(2,1)}, u32[]{:S(2)}, u32[]{:S(2)}) %collective-permute-start.113) | collective-permute-done | bytes 884768 | tf_op jit(solution)/shard_map/ppermute | solution.py:18
  1162.8 10.4 collective-permute-done.116
  1185.5 25.7 %collective-permute-done.117 = bf16[40,5760]{1,0:T(8,128)(2,1)S(1)} collective-permute-done((bf16[40,5760]{1,0:T(8,128)(2,1)S(1)}, bf16[40,5760]{1,0:T(8,128)(2,1)S(1)}, u32[]{:S(2)}, u32[]{:S(2)}) %collective-permute-start.117) | collective-permute-done | bytes 460832 | tf_op jit(solution)/shard_map/ppermute | solution.py:18
  1219.6 11.8 collective-permute-done.119
  (940 shorter events, 700.7 us)
Async XLA Ops:
  7.2 1006.3 %all-gather.3.cloned.1.call-start = ((), (), s32[]{:S(2)}) async-start(), calls=%async_computation | async-start | bytes 3649536 | tf_op jit(solution)/shard_map/all_gather | solution.py:1203
  76.9 53.8 %collective-permute-start.10 = (bf16[80,5760]{1,0:T(8,128)(2,1)}, bf16[80,5760]{1,0:T(8,128)(2,1)}, u32[]{:S(2)}, u32[]{:S(2)}) collective-permute-start(bf16[80,5760]{1,0:T(8,128)(2,1)} %pad_maximum_fusion.7), channel_id=1, source_target_pairs={{0,4},{1,5},{2,6},{3,7},{4,0},{5,1},{6,2},{7,3},{8,12},{9,13},{10,... | collective-permute-start | bytes 2764808 | tf_op jit(solution)/shard_map/ppermute | solution.py:18
  79.2 51.5 %collective-permute-start.11 = (bf16[96,3456]{1,0:T(8,128)(2,1)}, bf16[96,3456]{1,0:T(8,128)(2,1)}, u32[]{:S(2)}, u32[]{:S(2)}) collective-permute-start(bf16[96,3456]{1,0:T(8,128)(2,1)} %pad_maximum_fusion.15), channel_id=1, source_target_pairs={{0,16},{16,0},{1,17},{17,1},{2,18},{18,2},{3,19},{19,3},{4,20},{20... | collective-permute-start | bytes 1990664 | tf_op jit(solution)/shard_map/ppermute | solution.py:18
  82.8 47.8 %collective-permute-start.12 = (bf16[64,3456]{1,0:T(8,128)(2,1)}, bf16[64,3456]{1,0:T(8,128)(2,1)}, u32[]{:S(2)}, u32[]{:S(2)}) collective-permute-start(bf16[64,3456]{1,0:T(8,128)(2,1)} %pad_maximum_fusion.33), channel_id=1, source_target_pairs={{0,2},{1,3},{2,0},{3,1},{4,6},{5,7},{6,4},{7,5},{8,10},{9,11},{10,... | collective-permute-start | bytes 1327112 | tf_op jit(solution)/shard_map/ppermute | solution.py:18
  132.4 48.9 %collective-permute-start.18 = (bf16[192,3456]{1,0:T(8,128)(2,1)S(1)}, bf16[192,3456]{1,0:T(8,128)(2,1)S(1)}, u32[]{:S(2)}, u32[]{:S(2)}) collective-permute-start(bf16[192,3456]{1,0:T(8,128)(2,1)S(1)} %constant_dynamic-update-slice_fusion.2.refs_0_), channel_id=1, source_target_pairs={{0,1},{1,0},{2,3},{3,2},{4,5},{5,4},{6,7},{7,6},{8,9},{9,8},{10,11... | collective-permute-start | bytes 3981320 | tf_op jit(solution)/shard_map/ppermute | solution.py:18
  134.1 46.6 %collective-permute-start.20 = (bf16[128,3456]{1,0:T(8,128)(2,1)S(1)}, bf16[128,3456]{1,0:T(8,128)(2,1)S(1)}, u32[]{:S(2)}, u32[]{:S(2)}) collective-permute-start(bf16[128,3456]{1,0:T(8,128)(2,1)S(1)} %constant_dynamic-update-slice_fusion.7.refs_1_), channel_id=1, source_target_pairs={{0,1},{1,0},{2,3},{3,2},{4,5},{5,4},{6,7},{7,6},{8,9},{9,8},{10,11... | collective-permute-start | bytes 2654216 | tf_op jit(solution)/shard_map/ppermute | solution.py:18
  180.7 45.7 %collective-permute-start.23 = (bf16[96,5760]{1,0:T(8,128)(2,1)}, bf16[96,5760]{1,0:T(8,128)(2,1)}, u32[]{:S(2)}, u32[]{:S(2)}) collective-permute-start(bf16[96,5760]{1,0:T(8,128)(2,1)} %pad_maximum_fusion.4), channel_id=1, source_target_pairs={{0,16},{16,0},{1,17},{17,1},{2,18},{18,2},{3,19},{19,3},{4,20},{20... | collective-permute-start | bytes 3317768 | tf_op jit(solution)/shard_map/ppermute | solution.py:18
  227.9 56.6 %collective-permute-start.28 = (bf16[192,5760]{1,0:T(8,128)(2,1)S(1)}, bf16[192,5760]{1,0:T(8,128)(2,1)}, u32[]{:S(2)}, u32[]{:S(2)}) collective-permute-start(bf16[192,5760]{1,0:T(8,128)(2,1)S(1)} %constant_dynamic-update-slice_fusion.12.refs_0_.refs_2_), channel_id=1, source_target_pairs={{0,2},{1,3},{2,0},{3,1},{4,6},{5,7},{6,4},{7,5},{8,10},{9,11},{10,... | collective-permute-start | bytes 6635528 | tf_op jit(solution)/shard_map/ppermute | solution.py:18
  229.4 59.5 %collective-permute-start.30 = (bf16[192,5760]{1,0:T(8,128)(2,1)S(1)}, bf16[192,5760]{1,0:T(8,128)(2,1)}, u32[]{:S(2)}, u32[]{:S(2)}) collective-permute-start(bf16[192,5760]{1,0:T(8,128)(2,1)S(1)} %constant_dynamic-update-slice_fusion.12.refs_0_.refs_2_), channel_id=1, source_target_pairs={{0,1},{1,0},{2,3},{3,2},{4,5},{5,4},{6,7},{7,6},{8,9},{9,8},{10,11... | collective-permute-start | bytes 6635528 | tf_op jit(solution)/shard_map/ppermute | solution.py:18
  237.2 47.2 %collective-permute-start.29 = (bf16[128,5760]{1,0:T(8,128)(2,1)}, bf16[128,5760]{1,0:T(8,128)(2,1)}, u32[]{:S(2)}, u32[]{:S(2)}) collective-permute-start(bf16[128,5760]{1,0:T(8,128)(2,1)} %constant_dynamic-update-slice_fusion.17.refs_1_.refs_3_), channel_id=1, source_target_pairs={{0,16},{16,0},{1,17},{17,1},{2,18},{18,2},{3,19},{19,3},{4,20},{20... | collective-permute-start | bytes 4423688 | tf_op jit(solution)/shard_map/ppermute | solution.py:18
  317.0 46.0 %collective-permute-start.38 = (bf16[576,1152]{1,0:T(8,128)(2,1)}, bf16[576,1152]{1,0:T(8,128)(2,1)}, u32[]{:S(2)}, u32[]{:S(2)}) collective-permute-start(bf16[576,1152]{1,0:T(8,128)(2,1)} %constant_dynamic-update-slice_fusion.24), channel_id=1, source_target_pairs={{0,2},{1,3},{2,0},{3,1},{4,6},{5,7},{6,4},{7,5},{8,10},{9,11},{10,... | collective-permute-start | bytes 3981320 | tf_op jit(solution)/shard_map/ppermute | solution.py:18
  365.7 54.9 %collective-permute-start.47 = (bf16[192,3456]{1,0:T(8,128)(2,1)}, bf16[192,3456]{1,0:T(8,128)(2,1)}, u32[]{:S(2)}, u32[]{:S(2)}) collective-permute-start(bf16[192,3456]{1,0:T(8,128)(2,1)} %constant_dynamic-update-slice_fusion.34.refs_0_), channel_id=1, source_target_pairs={{0,2},{1,3},{2,0},{3,1},{4,6},{5,7},{6,4},{7,5},{8,10},{9,11},{10,... | collective-permute-start | bytes 3981320 | tf_op jit(solution)/shard_map/ppermute | solution.py:18
  375.6 45.0 %collective-permute-start.49 = (bf16[96,5760]{1,0:T(8,128)(2,1)}, bf16[96,5760]{1,0:T(8,128)(2,1)}, u32[]{:S(2)}, u32[]{:S(2)}) collective-permute-start(bf16[96,5760]{1,0:T(8,128)(2,1)} %pad_maximum_fusion.5), channel_id=1, source_target_pairs={{0,16},{16,0},{1,17},{17,1},{2,18},{18,2},{3,19},{19,3},{4,20},{20... | collective-permute-start | bytes 3317768 | tf_op jit(solution)/shard_map/ppermute | solution.py:18
  433.7 64.5 %collective-permute-start.58 = (bf16[192,5760]{1,0:T(8,128)(2,1)}, bf16[192,5760]{1,0:T(8,128)(2,1)}, u32[]{:S(2)}, u32[]{:S(2)}) collective-permute-start(bf16[192,5760]{1,0:T(8,128)(2,1)} %constant_dynamic-update-slice_fusion.44.refs_0_.refs_2_), channel_id=1, source_target_pairs={{0,2},{1,3},{2,0},{3,1},{4,6},{5,7},{6,4},{7,5},{8,10},{9,11},{10,... | collective-permute-start | bytes 6635528 | tf_op jit(solution)/shard_map/ppermute | solution.py:18
  434.2 76.1 %collective-permute-start.62 = (bf16[192,5760]{1,0:T(8,128)(2,1)}, bf16[192,5760]{1,0:T(8,128)(2,1)}, u32[]{:S(2)}, u32[]{:S(2)}) collective-permute-start(bf16[192,5760]{1,0:T(8,128)(2,1)} %constant_dynamic-update-slice_fusion.44.refs_0_.refs_2_), channel_id=1, source_target_pairs={{0,1},{1,0},{2,3},{3,2},{4,5},{5,4},{6,7},{7,6},{8,9},{9,8},{10,11... | collective-permute-start | bytes 6635528 | tf_op jit(solution)/shard_map/ppermute | solution.py:18
  435.9 60.5 %collective-permute-start.59 = (bf16[128,5760]{1,0:T(8,128)(2,1)}, bf16[128,5760]{1,0:T(8,128)(2,1)}, u32[]{:S(2)}, u32[]{:S(2)}) collective-permute-start(bf16[128,5760]{1,0:T(8,128)(2,1)} %constant_dynamic-update-slice_fusion.49.refs_1_.refs_3_), channel_id=1, source_target_pairs={{0,16},{16,0},{1,17},{17,1},{2,18},{18,2},{3,19},{19,3},{4,20},{20... | collective-permute-start | bytes 4423688 | tf_op jit(solution)/shard_map/ppermute | solution.py:18
  637.9 82.8 %collective-permute-start.80 = (bf16[640,5760]{1,0:T(8,128)(2,1)}, bf16[640,5760]{1,0:T(8,128)(2,1)}, u32[]{:S(2)}, u32[]{:S(2)}) collective-permute-start(bf16[640,5760]{1,0:T(8,128)(2,1)} %away_grad.4), channel_id=1, source_target_pairs={{0,1},{1,0},{2,3},{3,2},{4,5},{5,4},{6,7},{7,6},{8,9},{9,8},{10,11... | collective-permute-start | bytes 22118408 | tf_op jit(solution)/shard_map/ppermute | solution.py:18
  656.1 66.9 %collective-permute-start.78 = (f32[16,512]{1,0:T(8,128)}, f32[16,512]{1,0:T(8,128)}, u32[]{:S(2)}, u32[]{:S(2)}) collective-permute-start(f32[16,512]{1,0:T(8,128)} %slice_bitcast_fusion.3.totals_ref), channel_id=1, source_target_pairs={{0,16},{16,0},{1,17},{17,1},{2,18},{18,2},{3,19},{19,3},{4,20},{20... | collective-permute-start | bytes 98312 | tf_op jit(solution)/shard_map/ppermute | solution.py:18
  751.4 65.3 %collective-permute-start.85 = (bf16[640,3456]{1,0:T(8,128)(2,1)}, bf16[640,3456]{1,0:T(8,128)(2,1)}, u32[]{:S(2)}, u32[]{:S(2)}) collective-permute-start(bf16[640,3456]{1,0:T(8,128)(2,1)} %away_grad.5), channel_id=1, source_target_pairs={{0,1},{1,0},{2,3},{3,2},{4,5},{5,4},{6,7},{7,6},{8,9},{9,8},{10,11... | collective-permute-start | bytes 13271048 | tf_op jit(solution)/shard_map/ppermute | solution.py:18
  765.9 50.8 %collective-permute-start.83 = (bf16[192,5760]{1,0:T(8,128)(2,1)}, bf16[192,5760]{1,0:T(8,128)(2,1)}, u32[]{:S(2)}, u32[]{:S(2)}) collective-permute-start(bf16[192,5760]{1,0:T(8,128)(2,1)} %get-tuple-element.397), channel_id=1, source_target_pairs={{0,2},{1,3},{2,0},{3,1},{4,6},{5,7},{6,4},{7,5},{8,10},{9,11},{10,... | collective-permute-start | bytes 6635528 | tf_op jit(solution)/shard_map/ppermute | solution.py:18
  825.3 409.2 %all-gather.5.cloned.1.call-start = ((), (), s32[]{:S(2)}) async-start(), calls=%async_computation.1 | async-start | bytes 3649536 | tf_op jit(solution)/shard_map/all_gather | solution.py:1203
  844.5 60.0 %collective-permute-start.89 = (bf16[192,3456]{1,0:T(8,128)(2,1)}, bf16[192,3456]{1,0:T(8,128)(2,1)}, u32[]{:S(2)}, u32[]{:S(2)}) collective-permute-start(bf16[192,3456]{1,0:T(8,128)(2,1)} %get-tuple-element.415), channel_id=1, source_target_pairs={{0,2},{1,3},{2,0},{3,1},{4,6},{5,7},{6,4},{7,5},{8,10},{9,11},{10,... | collective-permute-start | bytes 3981320 | tf_op jit(solution)/shard_map/ppermute | solution.py:18
  845.1 59.4 %collective-permute-start.90 = (bf16[128,3456]{1,0:T(8,128)(2,1)}, bf16[128,3456]{1,0:T(8,128)(2,1)}, u32[]{:S(2)}, u32[]{:S(2)}) collective-permute-start(bf16[128,3456]{1,0:T(8,128)(2,1)} %get-tuple-element.416), channel_id=1, source_target_pairs={{0,16},{16,0},{1,17},{17,1},{2,18},{18,2},{3,19},{19,3},{4,20},{20... | collective-permute-start | bytes 2654216 | tf_op jit(solution)/shard_map/ppermute | solution.py:18
  948.1 65.3 %collective-permute-start.102 = (bf16[640,5760]{1,0:T(8,128)(2,1)}, bf16[640,5760]{1,0:T(8,128)(2,1)}, u32[]{:S(2)}, u32[]{:S(2)}) collective-permute-start(bf16[640,5760]{1,0:T(8,128)(2,1)} %away_grad.6), channel_id=1, source_target_pairs={{0,1},{1,0},{2,3},{3,2},{4,5},{5,4},{6,7},{7,6},{8,9},{9,8},{10,11... | collective-permute-start | bytes 22118408 | tf_op jit(solution)/shard_map/ppermute | solution.py:18
  955.5 81.7 %collective-permute-start.99 = (f32[16,512]{1,0:T(8,128)}, f32[16,512]{1,0:T(8,128)}, u32[]{:S(2)}, u32[]{:S(2)}) collective-permute-start(f32[16,512]{1,0:T(8,128)} %slice_bitcast_fusion.2.totals_ref), channel_id=1, source_target_pairs={{0,16},{16,0},{1,17},{17,1},{2,18},{18,2},{3,19},{19,3},{4,20},{20... | collective-permute-start | bytes 98312 | tf_op jit(solution)/shard_map/ppermute | solution.py:18
  958.1 53.3 %collective-permute-start.101 = (bf16[40,5760]{1,0:T(8,128)(2,1)}, bf16[40,5760]{1,0:T(8,128)(2,1)}, u32[]{:S(2)}, u32[]{:S(2)}) collective-permute-start(bf16[40,5760]{1,0:T(8,128)(2,1)} %pad_maximum_fusion.31), channel_id=1, source_target_pairs={{0,8},{1,9},{2,10},{3,11},{4,12},{5,13},{6,14},{7,15},{8,0},{9,1},... | collective-permute-start | bytes 1382408 | tf_op jit(solution)/shard_map/ppermute | solution.py:18
  1019.2 45.5 %collective-permute-start.105 = (bf16[144,1152]{1,0:T(8,128)(2,1)}, bf16[144,1152]{1,0:T(8,128)(2,1)}, u32[]{:S(2)}, u32[]{:S(2)}) collective-permute-start(bf16[144,1152]{1,0:T(8,128)(2,1)} %pad_maximum_fusion.37), channel_id=1, source_target_pairs={{0,8},{1,9},{2,10},{3,11},{4,12},{5,13},{6,14},{7,15},{8,0},{9,1},... | collective-permute-start | bytes 995336 | tf_op jit(solution)/shard_map/ppermute | solution.py:18
  1032.6 56.2 %collective-permute-start.106 = (bf16[192,5760]{1,0:T(8,128)(2,1)}, bf16[192,5760]{1,0:T(8,128)(2,1)}, u32[]{:S(2)}, u32[]{:S(2)}) collective-permute-start(bf16[192,5760]{1,0:T(8,128)(2,1)} %get-tuple-element.446), channel_id=1, source_target_pairs={{0,2},{1,3},{2,0},{3,1},{4,6},{5,7},{6,4},{7,5},{8,10},{9,11},{10,... | collective-permute-start | bytes 6635528 | tf_op jit(solution)/shard_map/ppermute | solution.py:18
  1037.2 51.6 %collective-permute-start.107 = (bf16[128,5760]{1,0:T(8,128)(2,1)}, bf16[128,5760]{1,0:T(8,128)(2,1)}, u32[]{:S(2)}, u32[]{:S(2)}) collective-permute-start(bf16[128,5760]{1,0:T(8,128)(2,1)} %get-tuple-element.447), channel_id=1, source_target_pairs={{0,16},{16,0},{1,17},{17,1},{2,18},{18,2},{3,19},{19,3},{4,20},{20... | collective-permute-start | bytes 4423688 | tf_op jit(solution)/shard_map/ppermute | solution.py:18
  1038.4 50.4 %collective-permute-start.108 = (bf16[40,3456]{1,0:T(8,128)(2,1)}, bf16[40,3456]{1,0:T(8,128)(2,1)}, u32[]{:S(2)}, u32[]{:S(2)}) collective-permute-start(bf16[40,3456]{1,0:T(8,128)(2,1)} %pad_maximum_fusion.38), channel_id=1, source_target_pairs={{0,8},{1,9},{2,10},{3,11},{4,12},{5,13},{6,14},{7,15},{8,0},{9,1},... | collective-permute-start | bytes 829448 | tf_op jit(solution)/shard_map/ppermute | solution.py:18
  1100.5 46.1 %collective-permute-start.110 = (bf16[96,5760]{1,0:T(8,128)(2,1)}, bf16[96,5760]{1,0:T(8,128)(2,1)}, u32[]{:S(2)}, u32[]{:S(2)}) collective-permute-start(bf16[96,5760]{1,0:T(8,128)(2,1)} %get-tuple-element.591), channel_id=1, source_target_pairs={{0,16},{16,0},{1,17},{17,1},{2,18},{18,2},{3,19},{19,3},{4,20},{20... | collective-permute-start | bytes 3317768 | tf_op jit(solution)/shard_map/ppermute | solution.py:18
  1105.1 46.4 %collective-permute-start.112 = (bf16[192,3456]{1,0:T(8,128)(2,1)}, bf16[192,3456]{1,0:T(8,128)(2,1)}, u32[]{:S(2)}, u32[]{:S(2)}) collective-permute-start(bf16[192,3456]{1,0:T(8,128)(2,1)} %get-tuple-element.460), channel_id=1, source_target_pairs={{0,2},{1,3},{2,0},{3,1},{4,6},{5,7},{6,4},{7,5},{8,10},{9,11},{10,... | collective-permute-start | bytes 3981320 | tf_op jit(solution)/shard_map/ppermute | solution.py:18
  (256 other events, 4348.5 us)
Sparse Core Ops, SparseCore 0:
  825.4 67.7 all-gather.2
  1162.9 71.5 all-gather.4

commit v4 on v3

--- a/solution.py
+++ b/solution.py
@@ -972,7 +972,7 @@
 
     def unit_ticks(unit):
         early = ((0, 1, 2, 4, 7, 8), (0, 2, 4, 9, 11, 12), (5, 9, 10, 13, 14, 15))
-        late = ((9, 10, 13, 14, 16, 17), (10, 13, 14, 16, 20, 21), (14, 16, 19, 20, 24, 25))
+        late = ((8, 9, 13, 14, 16, 17), (9, 10, 14, 16, 20, 21), (14, 16, 19, 20, 24, 25))
         if unit < 3:
             return early[unit]
         return tuple(tick + 10 * (unit // 3 - 1) for tick in late[unit % 3])
@@ -1250,7 +1250,7 @@
         grad_out_bias = sums_two[3 * group_count]
         out_grad = feed.tick(feed.tick(out_grad))
         lefts, rights = (saved["low_two"], saved["mixed_low"]), (up_grad, out_grad)
-        up_waits = (2, 0, 2, 2, 2, 1) if last else (2, 0, 2, 2, 2, 3)
+        up_waits = (2, 0, 2, 2, 2, 2) if last else (2, 0, 2, 2, 2, 3)
         scatter_ordered(lefts, rights, up_waits, up_rows)
         grad_mixed = ungrouped(
             (

time: 1260 us -> 1270 us (level)
    unnamed x413 -> x433, local copies, waits for them, and re-layouts: 86.5 us -> 95.7 us
where the time goes in v4:
time: 1270 us; the launch traced here: 1260 us
  Pallas kernels  491 us (39%)
  waiting for transfers between devices  279 us (22%)
  local copies, waits for them, and re-layouts  163 us (13%)
  other arithmetic  140 us (11%)
  starting transfers between devices  96.6 us (8%)
  matrix products  78.2 us (6%)
  between operations  17.1 us (1%)
    ppermute x120, waiting for transfers between devices, swap_bit(): lax.ppermute(block, axis, [(low, low ^ 1 << bit) for low in range(count)])  264 us
    ppermute x120, starting transfers between devices, swap_bit(): lax.ppermute(block, axis, [(low, low ^ 1 << bit) for low in range(count)])  96.6 us
    unnamed x433, local copies, waits for them, and re-layouts  95.7 us
    pallas_call x4, Pallas kernels, project_norm_back(): pl.pallas_call(kernel, out_shape=outs, grid=(tiles.count,), in_specs=[pl....  75.7 us
    pallas_call x8, Pallas kernels, call(): pl.pallas_call(kernel, out_shape=outs, grid=(sum(self.counts),), in_specs...  73.9 us
    dot_general x14, matrix products, contract(): lax.dot_general(left, right, (((left_dim,), (right_dim,)), ((), ())), pre...  72.8 us
    pallas_call x2, Pallas kernels, attend_back(): pl.pallas_call(kernel, out_shape=outs, grid=(head_count,), in_specs=in_sp...  66.3 us
    pallas_call x2, Pallas kernels, attend(): pl.pallas_call(kernel, out_shape=[mixed, wide, totals], grid=(head_count,...  54.9 us
  transfers between devices with their start and end apart: 122, of which 37 were waited for; matrix products, arithmetic and copies ran while one was open for 25% of the time, Pallas kernels for 36%

profile of v4, /device:TPU:0, one launch (start us, length us, event | category | flops | bytes accessed | tf_op | source)
XLA Modules:
  0.0 1264.5 jit_solution(9186196693736204628)
XLA Ops:
  54.6 10.7 collective-permute-done.7
  111.3 19.2 %collective-permute-done.9 = f32[16,13824]{1,0:T(8,128)S(1)} collective-permute-done((f32[16,13824]{1,0:T(8,128)S(1)}, f32[16,13824]{1,0:T(8,128)S(1)}, u32[]{:S(2)}, u32[]{:S(2)}) %collective-permute-start.9) | collective-permute-done | bytes 884768 | tf_op jit(solution)/shard_map/ppermute | solution.py:18
  185.3 10.1 project_qkv.2.qkv_ref.key_ref.value_ref
  197.0 18.4 %collective-permute-done.22 = bf16[512,1152]{1,0:T(8,128)(2,1)} collective-permute-done((bf16[512,1152]{1,0:T(8,128)(2,1)}, bf16[512,1152]{1,0:T(8,128)(2,1)}, u32[]{:S(2)}, u32[]{:S(2)}) %collective-permute-start.22) | collective-permute-done | bytes 1179680 | tf_op jit(solution)/shard_map/ppermute | solution.py:18
  248.5 27.5 %attend.2 = (bf16[512,1152]{1,0:T(8,128)(2,1)}, f32[512,1152]{1,0:T(8,128)}, f32[512,128]{1,0:T(8,128)}) custom-call(bf16[512,3456]{1,0:T(8,128)(2,1)} %project_qkv.2.qkv_ref.key_ref.value_ref, bf16[512,3456]{1,0:T(8,128)(2,1)} %project_other.2.key_ref.value_ref.other_ref, bf16[512,3456]{1,0:T(8,128)(2,1)} %project_other.2.key_ref.value_ref.other_ref, ...), custom_call_target="tpu_custom_call" | custom-call | flops 8589934592 | bytes 8257536 | tf_op jit(solution)/shard_map/attend/pallas_call | solution.py:704
  331.2 14.5 %project_up.2 = (f32[512,4608]{1,0:T(8,128)}, bf16[4608,512]{1,0:T(8,128)(2,1)}) custom-call(bf16[512,1280]{1,0:T(8,128)(2,1)} %fusion.12.left_ref.refs_0_, f32[1,4608]{1,0:T(1,128)} %reshape.577.bias_ref, f32[2,4608]{1,0:T(2,128)} %get-tuple-element.575.channel_ref, bf16[192,5760]{1,0:T(8,128)(2,1)} %copy-done.10, ...), custom_call_target="tpu_custom_call" | custom-call | flops 6039797760 | bytes 30212096 | tf_op jit(solution)/shard_map/project_up/pallas_call | solution.py:452
  345.7 19.1 %collective-permute-done.40 = bf16[64,3456]{1,0:T(8,128)(2,1)} collective-permute-done((bf16[64,3456]{1,0:T(8,128)(2,1)}, bf16[64,3456]{1,0:T(8,128)(2,1)}, u32[]{:S(2)}, u32[]{:S(2)}) %collective-permute-start.40) | collective-permute-done | bytes 442400 | tf_op jit(solution)/shard_map/ppermute | solution.py:18
  392.2 13.1 %fusion.90 = (f32[512]{0:T(512)S(1)}, f32[512,1152]{1,0:T(8,128)S(1)}, f32[512,1152]{1,0:T(8,128)}) fusion(f32[512,1152]{1,0:T(8,128)} %copy-done.3, f32[2,1152]{1,0:T(2,128)S(1)} %get-tuple-element.770, f32[512]{0:T(512)S(1)} %bitcast.321, f32[1152]{0:T(1024)} %reshape_squeeze.36, bf16[4608,512]{1,0:T(8,128)(2,1)} %get-tuple-element.317, ...), kind=kOutput, calls=%fused_computation.443 | convolution fusion | flops 5438766592 | bytes 22431232 | tf_op jit(solution)/shard_map/dot_general | solution.py:27
  407.7 10.8 collective-permute-done.48
  454.7 9.9 project_other.3.key_ref.value_ref.other_ref
  472.7 27.4 %attend.3 = (bf16[512,1152]{1,0:T(8,128)(2,1)}, f32[512,1152]{1,0:T(8,128)}, f32[512,128]{1,0:T(8,128)}) custom-call(bf16[512,3456]{1,0:T(8,128)(2,1)} %project_qkv.3.qkv_ref.key_ref.value_ref, bf16[512,3456]{1,0:T(8,128)(2,1)} %project_other.3.key_ref.value_ref.other_ref, bf16[512,3456]{1,0:T(8,128)(2,1)} %project_other.3.key_ref.value_ref.other_ref, ...), custom_call_target="tpu_custom_call" | custom-call | flops 8589934592 | bytes 8257536 | tf_op jit(solution)/shard_map/attend/pallas_call | solution.py:704
  526.0 14.5 %project_up.3 = (f32[512,4608]{1,0:T(8,128)}, bf16[4608,512]{1,0:T(8,128)(2,1)}) custom-call(bf16[512,1280]{1,0:T(8,128)(2,1)} %fusion.16.left_ref.refs_0_, f32[1,4608]{1,0:T(1,128)} %reshape.589.bias_ref, f32[2,4608]{1,0:T(2,128)} %get-tuple-element.574.channel_ref, bf16[192,5760]{1,0:T(8,128)(2,1)} %constant_dynamic-update-slice_fusion.44.refs_0_.refs_2_, ...), custom_call_target="tpu_custom_call" | custom-call | flops 6039797760 | bytes 30212096 | tf_op jit(solution)/shard_map/project_up/pallas_call | solution.py:452
  572.5 16.3 %hidden_back.2 = (bf16[512,4608]{1,0:T(8,128)(2,1)}, f32[1,4608]{1,0:T(1,128)}) custom-call(bf16[512,1152]{1,0:T(8,128)(2,1)} %copy-done.15, bf16[4608,1152]{1,0:T(8,128)(2,1)} %bitcast.284, f32[512,4608]{1,0:T(8,128)} %get-tuple-element.367.pre_ref, f32[2,4608]{1,0:T(2,128)} %get-tuple-element.574.channel_ref), custom_call_target="tpu_custom_call" | custom-call | flops 5435817984 | bytes 25952256 | tf_op jit(solution)/shard_map/hidden_back/pallas_call | solution.py:622
  601.6 20.5 %back_up.2 = (f32[512,1152]{1,0:T(8,128)}, bf16[512,1152]{1,0:T(8,128)(2,1)}, f32[8,1152]{1,0:T(8,128)}) custom-call(bf16[512,4608]{1,0:T(8,128)(2,1)} %get-tuple-element.376.right_ref.refs_2_, bf16[1280,1152]{1,0:T(8,128)(2,1)} %fusion.order_ref, f32[512,1152]{1,0:T(8,128)} %copy-done.1, f32[512,1152]{1,0:T(8,128)} %residual_ref.1, ...), custom_call_target="tpu_custom_call" | custom-call | flops 9059696640 | bytes 33085440 | tf_op jit(solution)/shard_map/back_up/pallas_call | solution.py:579
  659.3 12.7 %multiply_reduce_fusion.1 = (f32[2,1152]{1,0:T(2,128)}, f32[512,1152]{1,0:T(8,128)S(1)}) fusion(f32[2,256]{1,0:T(2,128)S(1)} %convert_element_type.971, f32[512,1152]{1,0:T(8,128)} %residual_ref.1, f32[1152]{0:T(1024)S(1)} %copy-done.143, bf16[4608,512]{1,0:T(8,128)(2,1)} %get-tuple-element.361, bf16[4608,1152]{1,0:T(8,128)(2,1)} %bitcast.285), kind=kOutput, calls=%fused_computation.63 | convolution fusion | flops 5438175232 | bytes 20069888 | tf_op jit(solution)/shard_map/dot_general | solution.py:27
  689.0 33.1 %attend_back.2 = (bf16[512,1152]{1,0:T(8,128)(2,1)}, f32[512,2304]{1,0:T(8,128)}) custom-call(bf16[512,3456]{1,0:T(8,128)(2,1)} %project_qkv.3.qkv_ref.key_ref.value_ref, bf16[512,3456]{1,0:T(8,128)(2,1)} %project_other.3.key_ref.value_ref.other_ref, bf16[512,3456]{1,0:T(8,128)(2,1)} %project_other.3.key_ref.value_ref.other_ref, ...), custom_call_target="tpu_custom_call" | custom-call | flops 17179869184 | bytes 12976128 | tf_op jit(solution)/shard_map/attend_back/pallas_call | solution.py:776
  724.2 21.5 %attend_back_other.2.right_ref.refs_1_ = bf16[512,3456]{1,0:T(8,128)(2,1)} custom-call(bf16[512,3456]{1,0:T(8,128)(2,1)} %project_qkv.3.qkv_ref.key_ref.value_ref, bf16[512,3456]{1,0:T(8,128)(2,1)} %project_qkv.3.qkv_ref.key_ref.value_ref, bf16[512,3456]{1,0:T(8,128)(2,1)} %project_other.3.key_ref.value_ref.other_ref, ...), custom_call_target="tpu_custom_call" | custom-call | flops 8589934592 | bytes 11796480 | tf_op jit(solution)/shard_map/attend_back_other/pallas_call | solution.py:845
  754.7 12.5 stay_grad.4
  776.7 17.0 %back_qkv.2 = (f32[512,1152]{1,0:T(8,128)}, f32[8,1152]{1,0:T(8,128)}) custom-call(bf16[512,3456]{1,0:T(8,128)(2,1)} %attend_back_other.2.right_ref.refs_1_, bf16[1280,1152]{1,0:T(8,128)(2,1)} %fusion.order_ref, f32[512,1152]{1,0:T(8,128)} %copy-done, f32[512,1152]{1,0:T(8,128)} %get-tuple-element.394.residual_ref, f32[2,1152]{1,0:T(2,128)} %get-tuple-element.774.scale_ref, ...), custom_call_target="tpu_custom_call" | custom-call | flops 7549747200 | bytes 22459392 | tf_op jit(solution)/shard_map/back_qkv/pallas_call | solution.py:579
  802.7 15.3 %collective-permute-done.83 = bf16[192,5760]{1,0:T(8,128)(2,1)} collective-permute-done((bf16[192,5760]{1,0:T(8,128)(2,1)}, bf16[192,5760]{1,0:T(8,128)(2,1)}, u32[]{:S(2)}, u32[]{:S(2)}) %collective-permute-start.83) | collective-permute-done | bytes 2211872 | tf_op jit(solution)/shard_map/ppermute | solution.py:18
  847.0 16.4 %hidden_back.3 = (bf16[512,4608]{1,0:T(8,128)(2,1)}, f32[1,4608]{1,0:T(1,128)}) custom-call(bf16[512,1152]{1,0:T(8,128)(2,1)} %bitcast.290, bf16[4608,1152]{1,0:T(8,128)(2,1)} %bitcast.283, f32[512,4608]{1,0:T(8,128)} %get-tuple-element.400.pre_ref, f32[2,4608]{1,0:T(2,128)} %get-tuple-element.575.channel_ref), custom_call_target="tpu_custom_call" | custom-call | flops 5435817984 | bytes 25952256 | tf_op jit(solution)/shard_map/hidden_back/pallas_call | solution.py:622
  883.3 20.8 %back_up.3 = (f32[512,1152]{1,0:T(8,128)}, bf16[512,1152]{1,0:T(8,128)(2,1)}, f32[8,1152]{1,0:T(8,128)}) custom-call(bf16[512,4608]{1,0:T(8,128)(2,1)} %get-tuple-element.412.right_ref.refs_2_, bf16[1280,1152]{1,0:T(8,128)(2,1)} %fusion.order_ref, f32[512,1152]{1,0:T(8,128)} %copy-done.3, f32[512,1152]{1,0:T(8,128)} %get-tuple-element.399, ...), custom_call_target="tpu_custom_call" | custom-call | flops 9059696640 | bytes 33085440 | tf_op jit(solution)/shard_map/back_up/pallas_call | solution.py:579
  907.8 11.6 collective-permute-done.92
  959.9 11.8 collective-permute-done.96
  978.8 33.2 %attend_back.3 = (bf16[512,1152]{1,0:T(8,128)(2,1)}, f32[512,2304]{1,0:T(8,128)}) custom-call(bf16[512,3456]{1,0:T(8,128)(2,1)} %project_qkv.2.qkv_ref.key_ref.value_ref, bf16[512,3456]{1,0:T(8,128)(2,1)} %project_other.2.key_ref.value_ref.other_ref, bf16[512,3456]{1,0:T(8,128)(2,1)} %project_other.2.key_ref.value_ref.other_ref, ...), custom_call_target="tpu_custom_call" | custom-call | flops 17179869184 | bytes 12976128 | tf_op jit(solution)/shard_map/attend_back/pallas_call | solution.py:776
  1021.5 12.0 stay_grad.6
  1042.7 21.6 %attend_back_other.3.refs_1_.right_ref = bf16[512,3456]{1,0:T(8,128)(2,1)} custom-call(bf16[512,3456]{1,0:T(8,128)(2,1)} %project_qkv.2.qkv_ref.key_ref.value_ref, bf16[512,3456]{1,0:T(8,128)(2,1)} %project_qkv.2.qkv_ref.key_ref.value_ref, bf16[512,3456]{1,0:T(8,128)(2,1)} %project_other.2.key_ref.value_ref.other_ref, ...), custom_call_target="tpu_custom_call" | custom-call | flops 8589934592 | bytes 11796480 | tf_op jit(solution)/shard_map/attend_back_other/pallas_call | solution.py:845
  1109.3 17.3 %back_qkv.3 = (f32[512,1152]{1,0:T(8,128)}, f32[8,1152]{1,0:T(8,128)}) custom-call(bf16[512,3456]{1,0:T(8,128)(2,1)} %attend_back_other.3.refs_1_.right_ref, bf16[1280,1152]{1,0:T(8,128)(2,1)} %fusion.order_ref, f32[512,1152]{1,0:T(8,128)} %convert_element_type.876.inputs_ref, f32[512,1152]{1,0:T(8,128)} %get-tuple-element.455.residual_ref, ...), custom_call_target="tpu_custom_call" | custom-call | flops 7549747200 | bytes 22459392 | tf_op jit(solution)/shard_map/back_qkv/pallas_call | solution.py:579
  1130.5 18.1 %collective-permute-done.113 = bf16[128,3456]{1,0:T(8,128)(2,1)} collective-permute-done((bf16[128,3456]{1,0:T(8,128)(2,1)}, bf16[128,3456]{1,0:T(8,128)(2,1)}, u32[]{:S(2)}, u32[]{:S(2)}) %collective-permute-start.113) | collective-permute-done | bytes 884768 | tf_op jit(solution)/shard_map/ppermute | solution.py:18
  1164.5 10.7 collective-permute-done.116
  1186.1 24.0 %collective-permute-done.117 = bf16[80,3456]{1,0:T(8,128)(2,1)S(1)} collective-permute-done((bf16[80,3456]{1,0:T(8,128)(2,1)S(1)}, bf16[80,3456]{1,0:T(8,128)(2,1)S(1)}, u32[]{:S(2)}, u32[]{:S(2)}) %collective-permute-start.117) | collective-permute-done | bytes 552992 | tf_op jit(solution)/shard_map/ppermute | solution.py:18
  1223.8 15.1 %all-gather.5.cloned.1.call-done = bf16[256,6912]{1,0:T(8,128)(2,1)} async-done(((bf16[8,6912]{1,0:T(8,128)(2,1)}), bf16[256,6912]{1,0:T(8,128)(2,1)}) %all-gather.5.cloned.1.call-update) | async-done | bytes 3538960 | tf_op jit(solution)/shard_map/all_gather | solution.py:1203
  (960 shorter events, 690.8 us)
Async XLA Ops:
  7.2 1006.8 %all-gather.3.cloned.1.call-start = ((), (), s32[]{:S(2)}) async-start(), calls=%async_computation | async-start | bytes 3649536 | tf_op jit(solution)/shard_map/all_gather | solution.py:1203
  76.9 53.8 %collective-permute-start.10 = (bf16[80,5760]{1,0:T(8,128)(2,1)}, bf16[80,5760]{1,0:T(8,128)(2,1)}, u32[]{:S(2)}, u32[]{:S(2)}) collective-permute-start(bf16[80,5760]{1,0:T(8,128)(2,1)} %pad_maximum_fusion.7), channel_id=1, source_target_pairs={{0,4},{1,5},{2,6},{3,7},{4,0},{5,1},{6,2},{7,3},{8,12},{9,13},{10,... | collective-permute-start | bytes 2764808 | tf_op jit(solution)/shard_map/ppermute | solution.py:18
  79.2 51.5 %collective-permute-start.11 = (bf16[96,3456]{1,0:T(8,128)(2,1)}, bf16[96,3456]{1,0:T(8,128)(2,1)}, u32[]{:S(2)}, u32[]{:S(2)}) collective-permute-start(bf16[96,3456]{1,0:T(8,128)(2,1)} %pad_maximum_fusion.15), channel_id=1, source_target_pairs={{0,16},{16,0},{1,17},{17,1},{2,18},{18,2},{3,19},{19,3},{4,20},{20... | collective-permute-start | bytes 1990664 | tf_op jit(solution)/shard_map/ppermute | solution.py:18
  82.8 47.8 %collective-permute-start.12 = (bf16[64,3456]{1,0:T(8,128)(2,1)}, bf16[64,3456]{1,0:T(8,128)(2,1)}, u32[]{:S(2)}, u32[]{:S(2)}) collective-permute-start(bf16[64,3456]{1,0:T(8,128)(2,1)} %pad_maximum_fusion.33), channel_id=1, source_target_pairs={{0,2},{1,3},{2,0},{3,1},{4,6},{5,7},{6,4},{7,5},{8,10},{9,11},{10,... | collective-permute-start | bytes 1327112 | tf_op jit(solution)/shard_map/ppermute | solution.py:18
  132.4 50.2 %collective-permute-start.18 = (bf16[192,3456]{1,0:T(8,128)(2,1)S(1)}, bf16[192,3456]{1,0:T(8,128)(2,1)S(1)}, u32[]{:S(2)}, u32[]{:S(2)}) collective-permute-start(bf16[192,3456]{1,0:T(8,128)(2,1)S(1)} %constant_dynamic-update-slice_fusion.2.refs_0_), channel_id=1, source_target_pairs={{0,1},{1,0},{2,3},{3,2},{4,5},{5,4},{6,7},{7,6},{8,9},{9,8},{10,11... | collective-permute-start | bytes 3981320 | tf_op jit(solution)/shard_map/ppermute | solution.py:18
  134.1 46.9 %collective-permute-start.20 = (bf16[128,3456]{1,0:T(8,128)(2,1)S(1)}, bf16[128,3456]{1,0:T(8,128)(2,1)S(1)}, u32[]{:S(2)}, u32[]{:S(2)}) collective-permute-start(bf16[128,3456]{1,0:T(8,128)(2,1)S(1)} %constant_dynamic-update-slice_fusion.7.refs_1_), channel_id=1, source_target_pairs={{0,1},{1,0},{2,3},{3,2},{4,5},{5,4},{6,7},{7,6},{8,9},{9,8},{10,11... | collective-permute-start | bytes 2654216 | tf_op jit(solution)/shard_map/ppermute | solution.py:18
  165.7 65.6 %collective-permute-start.23 = (bf16[96,5760]{1,0:T(8,128)(2,1)}, bf16[96,5760]{1,0:T(8,128)(2,1)}, u32[]{:S(2)}, u32[]{:S(2)}) collective-permute-start(bf16[96,5760]{1,0:T(8,128)(2,1)} %pad_maximum_fusion.4), channel_id=1, source_target_pairs={{0,16},{16,0},{1,17},{17,1},{2,18},{18,2},{3,19},{19,3},{4,20},{20... | collective-permute-start | bytes 3317768 | tf_op jit(solution)/shard_map/ppermute | solution.py:18
  181.0 50.2 %collective-permute-start.24 = (bf16[64,5760]{1,0:T(8,128)(2,1)}, bf16[64,5760]{1,0:T(8,128)(2,1)}, u32[]{:S(2)}, u32[]{:S(2)}) collective-permute-start(bf16[64,5760]{1,0:T(8,128)(2,1)} %pad_maximum_fusion.13), channel_id=1, source_target_pairs={{0,2},{1,3},{2,0},{3,1},{4,6},{5,7},{6,4},{7,5},{8,10},{9,11},{10,... | collective-permute-start | bytes 2211848 | tf_op jit(solution)/shard_map/ppermute | solution.py:18
  183.1 48.1 %collective-permute-start.25 = (bf16[144,1152]{1,0:T(8,128)(2,1)}, bf16[144,1152]{1,0:T(8,128)(2,1)}, u32[]{:S(2)}, u32[]{:S(2)}) collective-permute-start(bf16[144,1152]{1,0:T(8,128)(2,1)} %get-tuple-element.283), channel_id=1, source_target_pairs={{0,8},{1,9},{2,10},{3,11},{4,12},{5,13},{6,14},{7,15},{8,0},{9,1},... | collective-permute-start | bytes 995336 | tf_op jit(solution)/shard_map/ppermute | solution.py:18
  232.7 60.1 %collective-permute-start.29 = (bf16[192,5760]{1,0:T(8,128)(2,1)S(1)}, bf16[192,5760]{1,0:T(8,128)(2,1)}, u32[]{:S(2)}, u32[]{:S(2)}) collective-permute-start(bf16[192,5760]{1,0:T(8,128)(2,1)S(1)} %constant_dynamic-update-slice_fusion.14.refs_0_.refs_2_), channel_id=1, source_target_pairs={{0,2},{1,3},{2,0},{3,1},{4,6},{5,7},{6,4},{7,5},{8,10},{9,11},{10,... | collective-permute-start | bytes 6635528 | tf_op jit(solution)/shard_map/ppermute | solution.py:18
  234.3 64.6 %collective-permute-start.31 = (bf16[192,5760]{1,0:T(8,128)(2,1)S(1)}, bf16[192,5760]{1,0:T(8,128)(2,1)}, u32[]{:S(2)}, u32[]{:S(2)}) collective-permute-start(bf16[192,5760]{1,0:T(8,128)(2,1)S(1)} %constant_dynamic-update-slice_fusion.14.refs_0_.refs_2_), channel_id=1, source_target_pairs={{0,1},{1,0},{2,3},{3,2},{4,5},{5,4},{6,7},{7,6},{8,9},{9,8},{10,11... | collective-permute-start | bytes 6635528 | tf_op jit(solution)/shard_map/ppermute | solution.py:18
  243.8 49.1 %collective-permute-start.30 = (bf16[128,5760]{1,0:T(8,128)(2,1)}, bf16[128,5760]{1,0:T(8,128)(2,1)}, u32[]{:S(2)}, u32[]{:S(2)}) collective-permute-start(bf16[128,5760]{1,0:T(8,128)(2,1)} %constant_dynamic-update-slice_fusion.19.refs_1_.refs_3_), channel_id=1, source_target_pairs={{0,16},{16,0},{1,17},{17,1},{2,18},{18,2},{3,19},{19,3},{4,20},{20... | collective-permute-start | bytes 4423688 | tf_op jit(solution)/shard_map/ppermute | solution.py:18
  371.3 50.9 %collective-permute-start.49 = (bf16[192,3456]{1,0:T(8,128)(2,1)}, bf16[192,3456]{1,0:T(8,128)(2,1)}, u32[]{:S(2)}, u32[]{:S(2)}) collective-permute-start(bf16[192,3456]{1,0:T(8,128)(2,1)} %constant_dynamic-update-slice_fusion.34.refs_0_), channel_id=1, source_target_pairs={{0,2},{1,3},{2,0},{3,1},{4,6},{5,7},{6,4},{7,5},{8,10},{9,11},{10,... | collective-permute-start | bytes 3981320 | tf_op jit(solution)/shard_map/ppermute | solution.py:18
  375.8 46.5 %collective-permute-start.47 = (bf16[96,5760]{1,0:T(8,128)(2,1)}, bf16[96,5760]{1,0:T(8,128)(2,1)}, u32[]{:S(2)}, u32[]{:S(2)}) collective-permute-start(bf16[96,5760]{1,0:T(8,128)(2,1)} %pad_maximum_fusion.5), channel_id=1, source_target_pairs={{0,16},{16,0},{1,17},{17,1},{2,18},{18,2},{3,19},{19,3},{4,20},{20... | collective-permute-start | bytes 3317768 | tf_op jit(solution)/shard_map/ppermute | solution.py:18
  435.4 64.7 %collective-permute-start.58 = (bf16[192,5760]{1,0:T(8,128)(2,1)}, bf16[192,5760]{1,0:T(8,128)(2,1)}, u32[]{:S(2)}, u32[]{:S(2)}) collective-permute-start(bf16[192,5760]{1,0:T(8,128)(2,1)} %constant_dynamic-update-slice_fusion.44.refs_0_.refs_2_), channel_id=1, source_target_pairs={{0,2},{1,3},{2,0},{3,1},{4,6},{5,7},{6,4},{7,5},{8,10},{9,11},{10,... | collective-permute-start | bytes 6635528 | tf_op jit(solution)/shard_map/ppermute | solution.py:18
  436.8 76.1 %collective-permute-start.62 = (bf16[192,5760]{1,0:T(8,128)(2,1)}, bf16[192,5760]{1,0:T(8,128)(2,1)}, u32[]{:S(2)}, u32[]{:S(2)}) collective-permute-start(bf16[192,5760]{1,0:T(8,128)(2,1)} %constant_dynamic-update-slice_fusion.44.refs_0_.refs_2_), channel_id=1, source_target_pairs={{0,1},{1,0},{2,3},{3,2},{4,5},{5,4},{6,7},{7,6},{8,9},{9,8},{10,11... | collective-permute-start | bytes 6635528 | tf_op jit(solution)/shard_map/ppermute | solution.py:18
  437.5 62.5 %collective-permute-start.59 = (bf16[128,5760]{1,0:T(8,128)(2,1)}, bf16[128,5760]{1,0:T(8,128)(2,1)}, u32[]{:S(2)}, u32[]{:S(2)}) collective-permute-start(bf16[128,5760]{1,0:T(8,128)(2,1)} %constant_dynamic-update-slice_fusion.49.refs_1_.refs_3_), channel_id=1, source_target_pairs={{0,16},{16,0},{1,17},{17,1},{2,18},{18,2},{3,19},{19,3},{4,20},{20... | collective-permute-start | bytes 4423688 | tf_op jit(solution)/shard_map/ppermute | solution.py:18
  639.9 82.3 %collective-permute-start.80 = (bf16[640,5760]{1,0:T(8,128)(2,1)}, bf16[640,5760]{1,0:T(8,128)(2,1)}, u32[]{:S(2)}, u32[]{:S(2)}) collective-permute-start(bf16[640,5760]{1,0:T(8,128)(2,1)} %away_grad.4), channel_id=1, source_target_pairs={{0,1},{1,0},{2,3},{3,2},{4,5},{5,4},{6,7},{7,6},{8,9},{9,8},{10,11... | collective-permute-start | bytes 22118408 | tf_op jit(solution)/shard_map/ppermute | solution.py:18
  658.1 66.1 %collective-permute-start.78 = (f32[16,512]{1,0:T(8,128)}, f32[16,512]{1,0:T(8,128)}, u32[]{:S(2)}, u32[]{:S(2)}) collective-permute-start(f32[16,512]{1,0:T(8,128)} %slice_bitcast_fusion.3.totals_ref), channel_id=1, source_target_pairs={{0,16},{16,0},{1,17},{17,1},{2,18},{18,2},{3,19},{19,3},{4,20},{20... | collective-permute-start | bytes 98312 | tf_op jit(solution)/shard_map/ppermute | solution.py:18
  752.6 65.4 %collective-permute-start.85 = (bf16[640,3456]{1,0:T(8,128)(2,1)}, bf16[640,3456]{1,0:T(8,128)(2,1)}, u32[]{:S(2)}, u32[]{:S(2)}) collective-permute-start(bf16[640,3456]{1,0:T(8,128)(2,1)} %away_grad.5), channel_id=1, source_target_pairs={{0,1},{1,0},{2,3},{3,2},{4,5},{5,4},{6,7},{7,6},{8,9},{9,8},{10,11... | collective-permute-start | bytes 13271048 | tf_op jit(solution)/shard_map/ppermute | solution.py:18
  767.2 50.8 %collective-permute-start.83 = (bf16[192,5760]{1,0:T(8,128)(2,1)}, bf16[192,5760]{1,0:T(8,128)(2,1)}, u32[]{:S(2)}, u32[]{:S(2)}) collective-permute-start(bf16[192,5760]{1,0:T(8,128)(2,1)} %get-tuple-element.397), channel_id=1, source_target_pairs={{0,2},{1,3},{2,0},{3,1},{4,6},{5,7},{6,4},{7,5},{8,10},{9,11},{10,... | collective-permute-start | bytes 6635528 | tf_op jit(solution)/shard_map/ppermute | solution.py:18
  826.6 412.4 %all-gather.5.cloned.1.call-start = ((), (), s32[]{:S(2)}) async-start(), calls=%async_computation.1 | async-start | bytes 3649536 | tf_op jit(solution)/shard_map/all_gather | solution.py:1203
  844.5 60.4 %collective-permute-start.89 = (bf16[192,3456]{1,0:T(8,128)(2,1)}, bf16[192,3456]{1,0:T(8,128)(2,1)}, u32[]{:S(2)}, u32[]{:S(2)}) collective-permute-start(bf16[192,3456]{1,0:T(8,128)(2,1)} %get-tuple-element.415), channel_id=1, source_target_pairs={{0,2},{1,3},{2,0},{3,1},{4,6},{5,7},{6,4},{7,5},{8,10},{9,11},{10,... | collective-permute-start | bytes 3981320 | tf_op jit(solution)/shard_map/ppermute | solution.py:18
  845.8 59.1 %collective-permute-start.90 = (bf16[128,3456]{1,0:T(8,128)(2,1)}, bf16[128,3456]{1,0:T(8,128)(2,1)}, u32[]{:S(2)}, u32[]{:S(2)}) collective-permute-start(bf16[128,3456]{1,0:T(8,128)(2,1)} %get-tuple-element.416), channel_id=1, source_target_pairs={{0,16},{16,0},{1,17},{17,1},{2,18},{18,2},{3,19},{19,3},{4,20},{20... | collective-permute-start | bytes 2654216 | tf_op jit(solution)/shard_map/ppermute | solution.py:18
  948.7 65.3 %collective-permute-start.102 = (bf16[640,5760]{1,0:T(8,128)(2,1)}, bf16[640,5760]{1,0:T(8,128)(2,1)}, u32[]{:S(2)}, u32[]{:S(2)}) collective-permute-start(bf16[640,5760]{1,0:T(8,128)(2,1)} %away_grad.6), channel_id=1, source_target_pairs={{0,1},{1,0},{2,3},{3,2},{4,5},{5,4},{6,7},{7,6},{8,9},{9,8},{10,11... | collective-permute-start | bytes 22118408 | tf_op jit(solution)/shard_map/ppermute | solution.py:18
  956.6 81.5 %collective-permute-start.99 = (f32[16,512]{1,0:T(8,128)}, f32[16,512]{1,0:T(8,128)}, u32[]{:S(2)}, u32[]{:S(2)}) collective-permute-start(f32[16,512]{1,0:T(8,128)} %slice_bitcast_fusion.2.totals_ref), channel_id=1, source_target_pairs={{0,16},{16,0},{1,17},{17,1},{2,18},{18,2},{3,19},{19,3},{4,20},{20... | collective-permute-start | bytes 98312 | tf_op jit(solution)/shard_map/ppermute | solution.py:18
  958.7 53.2 %collective-permute-start.101 = (bf16[40,5760]{1,0:T(8,128)(2,1)}, bf16[40,5760]{1,0:T(8,128)(2,1)}, u32[]{:S(2)}, u32[]{:S(2)}) collective-permute-start(bf16[40,5760]{1,0:T(8,128)(2,1)} %pad_maximum_fusion.31), channel_id=1, source_target_pairs={{0,8},{1,9},{2,10},{3,11},{4,12},{5,13},{6,14},{7,15},{8,0},{9,1},... | collective-permute-start | bytes 1382408 | tf_op jit(solution)/shard_map/ppermute | solution.py:18
  1033.5 56.6 %collective-permute-start.106 = (bf16[192,5760]{1,0:T(8,128)(2,1)}, bf16[192,5760]{1,0:T(8,128)(2,1)}, u32[]{:S(2)}, u32[]{:S(2)}) collective-permute-start(bf16[192,5760]{1,0:T(8,128)(2,1)} %get-tuple-element.446), channel_id=1, source_target_pairs={{0,2},{1,3},{2,0},{3,1},{4,6},{5,7},{6,4},{7,5},{8,10},{9,11},{10,... | collective-permute-start | bytes 6635528 | tf_op jit(solution)/shard_map/ppermute | solution.py:18
  1038.1 52.1 %collective-permute-start.107 = (bf16[128,5760]{1,0:T(8,128)(2,1)}, bf16[128,5760]{1,0:T(8,128)(2,1)}, u32[]{:S(2)}, u32[]{:S(2)}) collective-permute-start(bf16[128,5760]{1,0:T(8,128)(2,1)} %get-tuple-element.447), channel_id=1, source_target_pairs={{0,16},{16,0},{1,17},{17,1},{2,18},{18,2},{3,19},{19,3},{4,20},{20... | collective-permute-start | bytes 4423688 | tf_op jit(solution)/shard_map/ppermute | solution.py:18
  1039.6 50.6 %collective-permute-start.108 = (bf16[40,3456]{1,0:T(8,128)(2,1)}, bf16[40,3456]{1,0:T(8,128)(2,1)}, u32[]{:S(2)}, u32[]{:S(2)}) collective-permute-start(bf16[40,3456]{1,0:T(8,128)(2,1)} %pad_maximum_fusion.38), channel_id=1, source_target_pairs={{0,8},{1,9},{2,10},{3,11},{4,12},{5,13},{6,14},{7,15},{8,0},{9,1},... | collective-permute-start | bytes 829448 | tf_op jit(solution)/shard_map/ppermute | solution.py:18
  1101.9 46.7 %collective-permute-start.110 = (bf16[96,5760]{1,0:T(8,128)(2,1)}, bf16[96,5760]{1,0:T(8,128)(2,1)}, u32[]{:S(2)}, u32[]{:S(2)}) collective-permute-start(bf16[96,5760]{1,0:T(8,128)(2,1)} %get-tuple-element.591), channel_id=1, source_target_pairs={{0,16},{16,0},{1,17},{17,1},{2,18},{18,2},{3,19},{19,3},{4,20},{20... | collective-permute-start | bytes 3317768 | tf_op jit(solution)/shard_map/ppermute | solution.py:18
  1107.2 47.4 %collective-permute-start.112 = (bf16[192,3456]{1,0:T(8,128)(2,1)}, bf16[192,3456]{1,0:T(8,128)(2,1)}, u32[]{:S(2)}, u32[]{:S(2)}) collective-permute-start(bf16[192,3456]{1,0:T(8,128)(2,1)} %get-tuple-element.460), channel_id=1, source_target_pairs={{0,2},{1,3},{2,0},{3,1},{4,6},{5,7},{6,4},{7,5},{8,10},{9,11},{10,... | collective-permute-start | bytes 3981320 | tf_op jit(solution)/shard_map/ppermute | solution.py:18
  (266 other events, 4314.8 us)
Sparse Core Ops, SparseCore 0:
  826.7 67.9 all-gather.2
  1164.6 74.2 all-gather.4

commit v5 on v4

--- a/solution.py
+++ b/solution.py
@@ -972,7 +972,7 @@
 
     def unit_ticks(unit):
         early = ((0, 1, 2, 4, 7, 8), (0, 2, 4, 9, 11, 12), (5, 9, 10, 13, 14, 15))
-        late = ((8, 9, 13, 14, 16, 17), (9, 10, 14, 16, 20, 21), (14, 16, 19, 20, 24, 25))
+        late = ((9, 10, 13, 14, 16, 17), (10, 13, 14, 16, 20, 21), (14, 16, 19, 20, 24, 25))
         if unit < 3:
             return early[unit]
         return tuple(tick + 10 * (unit // 3 - 1) for tick in late[unit % 3])

time: 1270 us -> 1270 us (level)
    unnamed x433 -> x419, local copies, waits for them, and re-layouts: 95.7 us -> 86.5 us
  transfers between devices with their start and end apart: 122 -> 122, of which waited for: 37 -> 38; matrix products, arithmetic and copies ran while one was open for 25% -> 24% of each run, Pallas kernels for 36% -> 36%
where the time goes in v5:
time: 1270 us; the launch traced here: 1260 us
  Pallas kernels  490 us (39%)
  waiting for transfers between devices  280 us (22%)
  local copies, waits for them, and re-layouts  155 us (12%)
  other arithmetic  139 us (11%)
  starting transfers between devices  103 us (8%)
  matrix products  78.2 us (6%)
  between operations  16.9 us (1%)
    ppermute x120, waiting for transfers between devices, swap_bit(): lax.ppermute(block, axis, [(low, low ^ 1 << bit) for low in range(count)])  264 us
    ppermute x120, starting transfers between devices, swap_bit(): lax.ppermute(block, axis, [(low, low ^ 1 << bit) for low in range(count)])  103 us
    unnamed x419, local copies, waits for them, and re-layouts  86.5 us
    pallas_call x4, Pallas kernels, project_norm_back(): pl.pallas_call(kernel, out_shape=outs, grid=(tiles.count,), in_specs=[pl....  75.7 us
    pallas_call x8, Pallas kernels, call(): pl.pallas_call(kernel, out_shape=outs, grid=(sum(self.counts),), in_specs...  73.9 us
    dot_general x14, matrix products, contract(): lax.dot_general(left, right, (((left_dim,), (right_dim,)), ((), ())), pre...  72.8 us
    pallas_call x2, Pallas kernels, attend_back(): pl.pallas_call(kernel, out_shape=outs, grid=(head_count,), in_specs=in_sp...  66.3 us
    pallas_call x2, Pallas kernels, attend(): pl.pallas_call(kernel, out_shape=[mixed, wide, totals], grid=(head_count,...  54.5 us
  transfers between devices with their start and end apart: 122, of which 38 were waited for; matrix products, arithmetic and copies ran while one was open for 24% of the time, Pallas kernels for 36%

profile of v5, /device:TPU:0, one launch (start us, length us, event | category | flops | bytes accessed | tf_op | source)
XLA Modules:
  0.0 1262.6 jit_solution(4590465089026321031)
XLA Ops:
  54.7 10.7 collective-permute-done.7
  111.4 19.2 %collective-permute-done.9 = f32[16,13824]{1,0:T(8,128)S(1)} collective-permute-done((f32[16,13824]{1,0:T(8,128)S(1)}, f32[16,13824]{1,0:T(8,128)S(1)}, u32[]{:S(2)}, u32[]{:S(2)}) %collective-permute-start.9) | collective-permute-done | bytes 884768 | tf_op jit(solution)/shard_map/ppermute | solution.py:18
  183.9 10.2 project_qkv.2.qkv_ref.key_ref.value_ref
  238.7 27.1 %attend.2 = (bf16[512,1152]{1,0:T(8,128)(2,1)}, f32[512,1152]{1,0:T(8,128)}, f32[512,128]{1,0:T(8,128)}) custom-call(bf16[512,3456]{1,0:T(8,128)(2,1)} %project_qkv.2.qkv_ref.key_ref.value_ref, bf16[512,3456]{1,0:T(8,128)(2,1)} %project_other.2.key_ref.value_ref.other_ref, bf16[512,3456]{1,0:T(8,128)(2,1)} %project_other.2.key_ref.value_ref.other_ref, ...), custom_call_target="tpu_custom_call" | custom-call | flops 8589934592 | bytes 8257536 | tf_op jit(solution)/shard_map/attend/pallas_call | solution.py:704
  304.3 10.7 collective-permute-done.37
  330.7 14.5 %project_up.2 = (f32[512,4608]{1,0:T(8,128)}, bf16[4608,512]{1,0:T(8,128)(2,1)}) custom-call(bf16[512,1280]{1,0:T(8,128)(2,1)} %fusion.12.left_ref.refs_0_, f32[1,4608]{1,0:T(1,128)} %reshape.577.bias_ref, f32[2,4608]{1,0:T(2,128)} %get-tuple-element.575.channel_ref, bf16[192,5760]{1,0:T(8,128)(2,1)} %copy-done.10, ...), custom_call_target="tpu_custom_call" | custom-call | flops 6039797760 | bytes 30212096 | tf_op jit(solution)/shard_map/project_up/pallas_call | solution.py:452
  345.2 11.0 collective-permute-done.41
  389.2 13.1 %fusion.90 = (f32[512]{0:T(512)S(1)}, f32[512,1152]{1,0:T(8,128)S(1)}, f32[512,1152]{1,0:T(8,128)}) fusion(f32[512,1152]{1,0:T(8,128)} %copy-done.3, f32[2,1152]{1,0:T(2,128)S(1)} %get-tuple-element.770, f32[512]{0:T(512)S(1)} %bitcast.318, f32[1152]{0:T(1024)} %reshape_squeeze.36, bf16[4608,512]{1,0:T(8,128)(2,1)} %get-tuple-element.317, ...), kind=kOutput, calls=%fused_computation.443 | convolution fusion | flops 5438766592 | bytes 22431232 | tf_op jit(solution)/shard_map/dot_general | solution.py:27
  469.0 27.4 %attend.3 = (bf16[512,1152]{1,0:T(8,128)(2,1)}, f32[512,1152]{1,0:T(8,128)}, f32[512,128]{1,0:T(8,128)}) custom-call(bf16[512,3456]{1,0:T(8,128)(2,1)} %project_qkv.3.qkv_ref.key_ref.value_ref, bf16[512,3456]{1,0:T(8,128)(2,1)} %project_other.3.key_ref.value_ref.other_ref, bf16[512,3456]{1,0:T(8,128)(2,1)} %project_other.3.key_ref.value_ref.other_ref, ...), custom_call_target="tpu_custom_call" | custom-call | flops 8589934592 | bytes 8257536 | tf_op jit(solution)/shard_map/attend/pallas_call | solution.py:704
  523.9 14.6 %project_up.3 = (f32[512,4608]{1,0:T(8,128)}, bf16[4608,512]{1,0:T(8,128)(2,1)}) custom-call(bf16[512,1280]{1,0:T(8,128)(2,1)} %fusion.16.left_ref.refs_0_, f32[1,4608]{1,0:T(1,128)} %reshape.589.bias_ref, f32[2,4608]{1,0:T(2,128)} %get-tuple-element.574.channel_ref, bf16[192,5760]{1,0:T(8,128)(2,1)} %constant_dynamic-update-slice_fusion.44.refs_0_.refs_2_, ...), custom_call_target="tpu_custom_call" | custom-call | flops 6039797760 | bytes 30212096 | tf_op jit(solution)/shard_map/project_up/pallas_call | solution.py:452
  569.6 16.3 %hidden_back.2 = (bf16[512,4608]{1,0:T(8,128)(2,1)}, f32[1,4608]{1,0:T(1,128)}) custom-call(bf16[512,1152]{1,0:T(8,128)(2,1)} %copy-done.15, bf16[4608,1152]{1,0:T(8,128)(2,1)} %bitcast.284, f32[512,4608]{1,0:T(8,128)} %get-tuple-element.367.pre_ref, f32[2,4608]{1,0:T(2,128)} %get-tuple-element.574.channel_ref), custom_call_target="tpu_custom_call" | custom-call | flops 5435817984 | bytes 25952256 | tf_op jit(solution)/shard_map/hidden_back/pallas_call | solution.py:622
  600.2 20.5 %back_up.2 = (f32[512,1152]{1,0:T(8,128)}, bf16[512,1152]{1,0:T(8,128)(2,1)}, f32[8,1152]{1,0:T(8,128)}) custom-call(bf16[512,4608]{1,0:T(8,128)(2,1)} %get-tuple-element.376.right_ref.refs_2_, bf16[1280,1152]{1,0:T(8,128)(2,1)} %fusion.order_ref, f32[512,1152]{1,0:T(8,128)} %copy-done.1, f32[512,1152]{1,0:T(8,128)} %residual_ref.1, ...), custom_call_target="tpu_custom_call" | custom-call | flops 9059696640 | bytes 33085440 | tf_op jit(solution)/shard_map/back_up/pallas_call | solution.py:579
  656.5 12.7 %multiply_reduce_fusion.1 = (f32[2,1152]{1,0:T(2,128)}, f32[512,1152]{1,0:T(8,128)S(1)}) fusion(f32[2,256]{1,0:T(2,128)S(1)} %convert_element_type.971, f32[512,1152]{1,0:T(8,128)} %residual_ref.1, f32[1152]{0:T(1024)S(1)} %copy-done.137, bf16[4608,512]{1,0:T(8,128)(2,1)} %get-tuple-element.361, bf16[4608,1152]{1,0:T(8,128)(2,1)} %bitcast.285), kind=kOutput, calls=%fused_computation.63 | convolution fusion | flops 5438175232 | bytes 20069888 | tf_op jit(solution)/shard_map/dot_general | solution.py:27
  687.4 33.1 %attend_back.2 = (bf16[512,1152]{1,0:T(8,128)(2,1)}, f32[512,2304]{1,0:T(8,128)}) custom-call(bf16[512,3456]{1,0:T(8,128)(2,1)} %project_qkv.3.qkv_ref.key_ref.value_ref, bf16[512,3456]{1,0:T(8,128)(2,1)} %project_other.3.key_ref.value_ref.other_ref, bf16[512,3456]{1,0:T(8,128)(2,1)} %project_other.3.key_ref.value_ref.other_ref, ...), custom_call_target="tpu_custom_call" | custom-call | flops 17179869184 | bytes 12976128 | tf_op jit(solution)/shard_map/attend_back/pallas_call | solution.py:776
  722.9 21.7 %attend_back_other.2.right_ref.refs_1_ = bf16[512,3456]{1,0:T(8,128)(2,1)} custom-call(bf16[512,3456]{1,0:T(8,128)(2,1)} %project_qkv.3.qkv_ref.key_ref.value_ref, bf16[512,3456]{1,0:T(8,128)(2,1)} %project_qkv.3.qkv_ref.key_ref.value_ref, bf16[512,3456]{1,0:T(8,128)(2,1)} %project_other.3.key_ref.value_ref.other_ref, ...), custom_call_target="tpu_custom_call" | custom-call | flops 8589934592 | bytes 11796480 | tf_op jit(solution)/shard_map/attend_back_other/pallas_call | solution.py:845
  753.6 12.5 stay_grad.4
  776.8 17.0 %back_qkv.2 = (f32[512,1152]{1,0:T(8,128)}, f32[8,1152]{1,0:T(8,128)}) custom-call(bf16[512,3456]{1,0:T(8,128)(2,1)} %attend_back_other.2.right_ref.refs_1_, bf16[1280,1152]{1,0:T(8,128)(2,1)} %fusion.order_ref, f32[512,1152]{1,0:T(8,128)} %copy-done, f32[512,1152]{1,0:T(8,128)} %get-tuple-element.394.residual_ref, f32[2,1152]{1,0:T(2,128)} %get-tuple-element.774.scale_ref, ...), custom_call_target="tpu_custom_call" | custom-call | flops 7549747200 | bytes 22459392 | tf_op jit(solution)/shard_map/back_qkv/pallas_call | solution.py:579
  802.2 14.7 %collective-permute-done.83 = bf16[192,5760]{1,0:T(8,128)(2,1)} collective-permute-done((bf16[192,5760]{1,0:T(8,128)(2,1)}, bf16[192,5760]{1,0:T(8,128)(2,1)}, u32[]{:S(2)}, u32[]{:S(2)}) %collective-permute-start.83) | collective-permute-done | bytes 2211872 | tf_op jit(solution)/shard_map/ppermute | solution.py:18
  845.9 16.4 %hidden_back.3 = (bf16[512,4608]{1,0:T(8,128)(2,1)}, f32[1,4608]{1,0:T(1,128)}) custom-call(bf16[512,1152]{1,0:T(8,128)(2,1)} %bitcast.290, bf16[4608,1152]{1,0:T(8,128)(2,1)} %bitcast.283, f32[512,4608]{1,0:T(8,128)} %get-tuple-element.400.pre_ref, f32[2,4608]{1,0:T(2,128)} %get-tuple-element.575.channel_ref), custom_call_target="tpu_custom_call" | custom-call | flops 5435817984 | bytes 25952256 | tf_op jit(solution)/shard_map/hidden_back/pallas_call | solution.py:622
  883.0 20.9 %back_up.3 = (f32[512,1152]{1,0:T(8,128)}, bf16[512,1152]{1,0:T(8,128)(2,1)}, f32[8,1152]{1,0:T(8,128)}) custom-call(bf16[512,4608]{1,0:T(8,128)(2,1)} %get-tuple-element.412.right_ref.refs_2_, bf16[1280,1152]{1,0:T(8,128)(2,1)} %fusion.order_ref, f32[512,1152]{1,0:T(8,128)} %copy-done.3, f32[512,1152]{1,0:T(8,128)} %get-tuple-element.399, ...), custom_call_target="tpu_custom_call" | custom-call | flops 9059696640 | bytes 33085440 | tf_op jit(solution)/shard_map/back_up/pallas_call | solution.py:579
  907.7 11.2 collective-permute-done.92
  927.1 9.9 away_grad.6
  958.9 12.2 collective-permute-done.96
  978.3 33.2 %attend_back.3 = (bf16[512,1152]{1,0:T(8,128)(2,1)}, f32[512,2304]{1,0:T(8,128)}) custom-call(bf16[512,3456]{1,0:T(8,128)(2,1)} %project_qkv.2.qkv_ref.key_ref.value_ref, bf16[512,3456]{1,0:T(8,128)(2,1)} %project_other.2.key_ref.value_ref.other_ref, bf16[512,3456]{1,0:T(8,128)(2,1)} %project_other.2.key_ref.value_ref.other_ref, ...), custom_call_target="tpu_custom_call" | custom-call | flops 17179869184 | bytes 12976128 | tf_op jit(solution)/shard_map/attend_back/pallas_call | solution.py:776
  1020.8 12.1 stay_grad.6
  1041.5 21.6 %attend_back_other.3.refs_1_.right_ref = bf16[512,3456]{1,0:T(8,128)(2,1)} custom-call(bf16[512,3456]{1,0:T(8,128)(2,1)} %project_qkv.2.qkv_ref.key_ref.value_ref, bf16[512,3456]{1,0:T(8,128)(2,1)} %project_qkv.2.qkv_ref.key_ref.value_ref, bf16[512,3456]{1,0:T(8,128)(2,1)} %project_other.2.key_ref.value_ref.other_ref, ...), custom_call_target="tpu_custom_call" | custom-call | flops 8589934592 | bytes 11796480 | tf_op jit(solution)/shard_map/attend_back_other/pallas_call | solution.py:845
  1107.8 17.3 %back_qkv.3 = (f32[512,1152]{1,0:T(8,128)}, f32[8,1152]{1,0:T(8,128)}) custom-call(bf16[512,3456]{1,0:T(8,128)(2,1)} %attend_back_other.3.refs_1_.right_ref, bf16[1280,1152]{1,0:T(8,128)(2,1)} %fusion.order_ref, f32[512,1152]{1,0:T(8,128)} %convert_element_type.876.inputs_ref, f32[512,1152]{1,0:T(8,128)} %get-tuple-element.455.residual_ref, ...), custom_call_target="tpu_custom_call" | custom-call | flops 7549747200 | bytes 22459392 | tf_op jit(solution)/shard_map/back_qkv/pallas_call | solution.py:579
  1129.0 17.8 %collective-permute-done.113 = bf16[128,3456]{1,0:T(8,128)(2,1)} collective-permute-done((bf16[128,3456]{1,0:T(8,128)(2,1)}, bf16[128,3456]{1,0:T(8,128)(2,1)}, u32[]{:S(2)}, u32[]{:S(2)}) %collective-permute-start.113) | collective-permute-done | bytes 884768 | tf_op jit(solution)/shard_map/ppermute | solution.py:18
  1162.8 10.3 collective-permute-done.116
  1184.2 21.7 %collective-permute-done.117 = bf16[80,3456]{1,0:T(8,128)(2,1)S(1)} collective-permute-done((bf16[80,3456]{1,0:T(8,128)(2,1)S(1)}, bf16[80,3456]{1,0:T(8,128)(2,1)S(1)}, u32[]{:S(2)}, u32[]{:S(2)}) %collective-permute-start.117) | collective-permute-done | bytes 552992 | tf_op jit(solution)/shard_map/ppermute | solution.py:18
  1207.6 10.0 collective-permute-done.118
  1221.9 15.2 %all-gather.5.cloned.1.call-done = bf16[256,6912]{1,0:T(8,128)(2,1)} async-done(((bf16[8,6912]{1,0:T(8,128)(2,1)}), bf16[256,6912]{1,0:T(8,128)(2,1)}) %all-gather.5.cloned.1.call-update) | async-done | bytes 3538960 | tf_op jit(solution)/shard_map/all_gather | solution.py:1203
  (946 shorter events, 709.1 us)
Async XLA Ops:
  7.2 1006.4 %all-gather.3.cloned.1.call-start = ((), (), s32[]{:S(2)}) async-start(), calls=%async_computation | async-start | bytes 3649536 | tf_op jit(solution)/shard_map/all_gather | solution.py:1203
  76.9 53.8 %collective-permute-start.10 = (bf16[80,5760]{1,0:T(8,128)(2,1)}, bf16[80,5760]{1,0:T(8,128)(2,1)}, u32[]{:S(2)}, u32[]{:S(2)}) collective-permute-start(bf16[80,5760]{1,0:T(8,128)(2,1)} %pad_maximum_fusion.7), channel_id=1, source_target_pairs={{0,4},{1,5},{2,6},{3,7},{4,0},{5,1},{6,2},{7,3},{8,12},{9,13},{10,... | collective-permute-start | bytes 2764808 | tf_op jit(solution)/shard_map/ppermute | solution.py:18
  79.2 51.5 %collective-permute-start.11 = (bf16[96,3456]{1,0:T(8,128)(2,1)}, bf16[96,3456]{1,0:T(8,128)(2,1)}, u32[]{:S(2)}, u32[]{:S(2)}) collective-permute-start(bf16[96,3456]{1,0:T(8,128)(2,1)} %pad_maximum_fusion.15), channel_id=1, source_target_pairs={{0,16},{16,0},{1,17},{17,1},{2,18},{18,2},{3,19},{19,3},{4,20},{20... | collective-permute-start | bytes 1990664 | tf_op jit(solution)/shard_map/ppermute | solution.py:18
  82.8 47.9 %collective-permute-start.12 = (bf16[64,3456]{1,0:T(8,128)(2,1)}, bf16[64,3456]{1,0:T(8,128)(2,1)}, u32[]{:S(2)}, u32[]{:S(2)}) collective-permute-start(bf16[64,3456]{1,0:T(8,128)(2,1)} %pad_maximum_fusion.33), channel_id=1, source_target_pairs={{0,2},{1,3},{2,0},{3,1},{4,6},{5,7},{6,4},{7,5},{8,10},{9,11},{10,... | collective-permute-start | bytes 1327112 | tf_op jit(solution)/shard_map/ppermute | solution.py:18
  132.5 48.9 %collective-permute-start.18 = (bf16[192,3456]{1,0:T(8,128)(2,1)S(1)}, bf16[192,3456]{1,0:T(8,128)(2,1)S(1)}, u32[]{:S(2)}, u32[]{:S(2)}) collective-permute-start(bf16[192,3456]{1,0:T(8,128)(2,1)S(1)} %constant_dynamic-update-slice_fusion.2.refs_0_), channel_id=1, source_target_pairs={{0,1},{1,0},{2,3},{3,2},{4,5},{5,4},{6,7},{7,6},{8,9},{9,8},{10,11... | collective-permute-start | bytes 3981320 | tf_op jit(solution)/shard_map/ppermute | solution.py:18
  134.1 46.6 %collective-permute-start.20 = (bf16[128,3456]{1,0:T(8,128)(2,1)S(1)}, bf16[128,3456]{1,0:T(8,128)(2,1)S(1)}, u32[]{:S(2)}, u32[]{:S(2)}) collective-permute-start(bf16[128,3456]{1,0:T(8,128)(2,1)S(1)} %constant_dynamic-update-slice_fusion.7.refs_1_), channel_id=1, source_target_pairs={{0,1},{1,0},{2,3},{3,2},{4,5},{5,4},{6,7},{7,6},{8,9},{9,8},{10,11... | collective-permute-start | bytes 2654216 | tf_op jit(solution)/shard_map/ppermute | solution.py:18
  180.8 45.7 %collective-permute-start.23 = (bf16[96,5760]{1,0:T(8,128)(2,1)}, bf16[96,5760]{1,0:T(8,128)(2,1)}, u32[]{:S(2)}, u32[]{:S(2)}) collective-permute-start(bf16[96,5760]{1,0:T(8,128)(2,1)} %pad_maximum_fusion.4), channel_id=1, source_target_pairs={{0,16},{16,0},{1,17},{17,1},{2,18},{18,2},{3,19},{19,3},{4,20},{20... | collective-permute-start | bytes 3317768 | tf_op jit(solution)/shard_map/ppermute | solution.py:18
  227.9 56.6 %collective-permute-start.28 = (bf16[192,5760]{1,0:T(8,128)(2,1)S(1)}, bf16[192,5760]{1,0:T(8,128)(2,1)}, u32[]{:S(2)}, u32[]{:S(2)}) collective-permute-start(bf16[192,5760]{1,0:T(8,128)(2,1)S(1)} %constant_dynamic-update-slice_fusion.12.refs_0_.refs_2_), channel_id=1, source_target_pairs={{0,2},{1,3},{2,0},{3,1},{4,6},{5,7},{6,4},{7,5},{8,10},{9,11},{10,... | collective-permute-start | bytes 6635528 | tf_op jit(solution)/shard_map/ppermute | solution.py:18
  229.5 59.5 %collective-permute-start.30 = (bf16[192,5760]{1,0:T(8,128)(2,1)S(1)}, bf16[192,5760]{1,0:T(8,128)(2,1)}, u32[]{:S(2)}, u32[]{:S(2)}) collective-permute-start(bf16[192,5760]{1,0:T(8,128)(2,1)S(1)} %constant_dynamic-update-slice_fusion.12.refs_0_.refs_2_), channel_id=1, source_target_pairs={{0,1},{1,0},{2,3},{3,2},{4,5},{5,4},{6,7},{7,6},{8,9},{9,8},{10,11... | collective-permute-start | bytes 6635528 | tf_op jit(solution)/shard_map/ppermute | solution.py:18
  237.2 47.3 %collective-permute-start.29 = (bf16[128,5760]{1,0:T(8,128)(2,1)}, bf16[128,5760]{1,0:T(8,128)(2,1)}, u32[]{:S(2)}, u32[]{:S(2)}) collective-permute-start(bf16[128,5760]{1,0:T(8,128)(2,1)} %constant_dynamic-update-slice_fusion.17.refs_1_.refs_3_), channel_id=1, source_target_pairs={{0,16},{16,0},{1,17},{17,1},{2,18},{18,2},{3,19},{19,3},{4,20},{20... | collective-permute-start | bytes 4423688 | tf_op jit(solution)/shard_map/ppermute | solution.py:18
  317.1 46.0 %collective-permute-start.38 = (bf16[576,1152]{1,0:T(8,128)(2,1)}, bf16[576,1152]{1,0:T(8,128)(2,1)}, u32[]{:S(2)}, u32[]{:S(2)}) collective-permute-start(bf16[576,1152]{1,0:T(8,128)(2,1)} %constant_dynamic-update-slice_fusion.24), channel_id=1, source_target_pairs={{0,2},{1,3},{2,0},{3,1},{4,6},{5,7},{6,4},{7,5},{8,10},{9,11},{10,... | collective-permute-start | bytes 3981320 | tf_op jit(solution)/shard_map/ppermute | solution.py:18
  365.8 54.9 %collective-permute-start.47 = (bf16[192,3456]{1,0:T(8,128)(2,1)}, bf16[192,3456]{1,0:T(8,128)(2,1)}, u32[]{:S(2)}, u32[]{:S(2)}) collective-permute-start(bf16[192,3456]{1,0:T(8,128)(2,1)} %constant_dynamic-update-slice_fusion.34.refs_0_), channel_id=1, source_target_pairs={{0,2},{1,3},{2,0},{3,1},{4,6},{5,7},{6,4},{7,5},{8,10},{9,11},{10,... | collective-permute-start | bytes 3981320 | tf_op jit(solution)/shard_map/ppermute | solution.py:18
  375.6 45.0 %collective-permute-start.49 = (bf16[96,5760]{1,0:T(8,128)(2,1)}, bf16[96,5760]{1,0:T(8,128)(2,1)}, u32[]{:S(2)}, u32[]{:S(2)}) collective-permute-start(bf16[96,5760]{1,0:T(8,128)(2,1)} %pad_maximum_fusion.5), channel_id=1, source_target_pairs={{0,16},{16,0},{1,17},{17,1},{2,18},{18,2},{3,19},{19,3},{4,20},{20... | collective-permute-start | bytes 3317768 | tf_op jit(solution)/shard_map/ppermute | solution.py:18
  433.7 64.5 %collective-permute-start.58 = (bf16[192,5760]{1,0:T(8,128)(2,1)}, bf16[192,5760]{1,0:T(8,128)(2,1)}, u32[]{:S(2)}, u32[]{:S(2)}) collective-permute-start(bf16[192,5760]{1,0:T(8,128)(2,1)} %constant_dynamic-update-slice_fusion.44.refs_0_.refs_2_), channel_id=1, source_target_pairs={{0,2},{1,3},{2,0},{3,1},{4,6},{5,7},{6,4},{7,5},{8,10},{9,11},{10,... | collective-permute-start | bytes 6635528 | tf_op jit(solution)/shard_map/ppermute | solution.py:18
  434.2 76.0 %collective-permute-start.62 = (bf16[192,5760]{1,0:T(8,128)(2,1)}, bf16[192,5760]{1,0:T(8,128)(2,1)}, u32[]{:S(2)}, u32[]{:S(2)}) collective-permute-start(bf16[192,5760]{1,0:T(8,128)(2,1)} %constant_dynamic-update-slice_fusion.44.refs_0_.refs_2_), channel_id=1, source_target_pairs={{0,1},{1,0},{2,3},{3,2},{4,5},{5,4},{6,7},{7,6},{8,9},{9,8},{10,11... | collective-permute-start | bytes 6635528 | tf_op jit(solution)/shard_map/ppermute | solution.py:18
  435.9 60.5 %collective-permute-start.59 = (bf16[128,5760]{1,0:T(8,128)(2,1)}, bf16[128,5760]{1,0:T(8,128)(2,1)}, u32[]{:S(2)}, u32[]{:S(2)}) collective-permute-start(bf16[128,5760]{1,0:T(8,128)(2,1)} %constant_dynamic-update-slice_fusion.49.refs_1_.refs_3_), channel_id=1, source_target_pairs={{0,16},{16,0},{1,17},{17,1},{2,18},{18,2},{3,19},{19,3},{4,20},{20... | collective-permute-start | bytes 4423688 | tf_op jit(solution)/shard_map/ppermute | solution.py:18
  637.8 82.8 %collective-permute-start.80 = (bf16[640,5760]{1,0:T(8,128)(2,1)}, bf16[640,5760]{1,0:T(8,128)(2,1)}, u32[]{:S(2)}, u32[]{:S(2)}) collective-permute-start(bf16[640,5760]{1,0:T(8,128)(2,1)} %away_grad.4), channel_id=1, source_target_pairs={{0,1},{1,0},{2,3},{3,2},{4,5},{5,4},{6,7},{7,6},{8,9},{9,8},{10,11... | collective-permute-start | bytes 22118408 | tf_op jit(solution)/shard_map/ppermute | solution.py:18
  656.0 66.9 %collective-permute-start.78 = (f32[16,512]{1,0:T(8,128)}, f32[16,512]{1,0:T(8,128)}, u32[]{:S(2)}, u32[]{:S(2)}) collective-permute-start(f32[16,512]{1,0:T(8,128)} %slice_bitcast_fusion.3.totals_ref), channel_id=1, source_target_pairs={{0,16},{16,0},{1,17},{17,1},{2,18},{18,2},{3,19},{19,3},{4,20},{20... | collective-permute-start | bytes 98312 | tf_op jit(solution)/shard_map/ppermute | solution.py:18
  751.6 65.3 %collective-permute-start.85 = (bf16[640,3456]{1,0:T(8,128)(2,1)}, bf16[640,3456]{1,0:T(8,128)(2,1)}, u32[]{:S(2)}, u32[]{:S(2)}) collective-permute-start(bf16[640,3456]{1,0:T(8,128)(2,1)} %away_grad.5), channel_id=1, source_target_pairs={{0,1},{1,0},{2,3},{3,2},{4,5},{5,4},{6,7},{7,6},{8,9},{9,8},{10,11... | collective-permute-start | bytes 13271048 | tf_op jit(solution)/shard_map/ppermute | solution.py:18
  766.1 50.8 %collective-permute-start.83 = (bf16[192,5760]{1,0:T(8,128)(2,1)}, bf16[192,5760]{1,0:T(8,128)(2,1)}, u32[]{:S(2)}, u32[]{:S(2)}) collective-permute-start(bf16[192,5760]{1,0:T(8,128)(2,1)} %get-tuple-element.397), channel_id=1, source_target_pairs={{0,2},{1,3},{2,0},{3,1},{4,6},{5,7},{6,4},{7,5},{8,10},{9,11},{10,... | collective-permute-start | bytes 6635528 | tf_op jit(solution)/shard_map/ppermute | solution.py:18
  825.5 411.6 %all-gather.5.cloned.1.call-start = ((), (), s32[]{:S(2)}) async-start(), calls=%async_computation.1 | async-start | bytes 3649536 | tf_op jit(solution)/shard_map/all_gather | solution.py:1203
  844.7 60.0 %collective-permute-start.89 = (bf16[192,3456]{1,0:T(8,128)(2,1)}, bf16[192,3456]{1,0:T(8,128)(2,1)}, u32[]{:S(2)}, u32[]{:S(2)}) collective-permute-start(bf16[192,3456]{1,0:T(8,128)(2,1)} %get-tuple-element.415), channel_id=1, source_target_pairs={{0,2},{1,3},{2,0},{3,1},{4,6},{5,7},{6,4},{7,5},{8,10},{9,11},{10,... | collective-permute-start | bytes 3981320 | tf_op jit(solution)/shard_map/ppermute | solution.py:18
  845.3 59.4 %collective-permute-start.90 = (bf16[128,3456]{1,0:T(8,128)(2,1)}, bf16[128,3456]{1,0:T(8,128)(2,1)}, u32[]{:S(2)}, u32[]{:S(2)}) collective-permute-start(bf16[128,3456]{1,0:T(8,128)(2,1)} %get-tuple-element.416), channel_id=1, source_target_pairs={{0,16},{16,0},{1,17},{17,1},{2,18},{18,2},{3,19},{19,3},{4,20},{20... | collective-permute-start | bytes 2654216 | tf_op jit(solution)/shard_map/ppermute | solution.py:18
  948.3 65.3 %collective-permute-start.102 = (bf16[640,5760]{1,0:T(8,128)(2,1)}, bf16[640,5760]{1,0:T(8,128)(2,1)}, u32[]{:S(2)}, u32[]{:S(2)}) collective-permute-start(bf16[640,5760]{1,0:T(8,128)(2,1)} %away_grad.6), channel_id=1, source_target_pairs={{0,1},{1,0},{2,3},{3,2},{4,5},{5,4},{6,7},{7,6},{8,9},{9,8},{10,11... | collective-permute-start | bytes 22118408 | tf_op jit(solution)/shard_map/ppermute | solution.py:18
  955.7 81.7 %collective-permute-start.99 = (f32[16,512]{1,0:T(8,128)}, f32[16,512]{1,0:T(8,128)}, u32[]{:S(2)}, u32[]{:S(2)}) collective-permute-start(f32[16,512]{1,0:T(8,128)} %slice_bitcast_fusion.2.totals_ref), channel_id=1, source_target_pairs={{0,16},{16,0},{1,17},{17,1},{2,18},{18,2},{3,19},{19,3},{4,20},{20... | collective-permute-start | bytes 98312 | tf_op jit(solution)/shard_map/ppermute | solution.py:18
  958.2 53.2 %collective-permute-start.101 = (bf16[40,5760]{1,0:T(8,128)(2,1)}, bf16[40,5760]{1,0:T(8,128)(2,1)}, u32[]{:S(2)}, u32[]{:S(2)}) collective-permute-start(bf16[40,5760]{1,0:T(8,128)(2,1)} %pad_maximum_fusion.31), channel_id=1, source_target_pairs={{0,8},{1,9},{2,10},{3,11},{4,12},{5,13},{6,14},{7,15},{8,0},{9,1},... | collective-permute-start | bytes 1382408 | tf_op jit(solution)/shard_map/ppermute | solution.py:18
  1019.3 45.6 %collective-permute-start.105 = (bf16[144,1152]{1,0:T(8,128)(2,1)}, bf16[144,1152]{1,0:T(8,128)(2,1)}, u32[]{:S(2)}, u32[]{:S(2)}) collective-permute-start(bf16[144,1152]{1,0:T(8,128)(2,1)} %pad_maximum_fusion.37), channel_id=1, source_target_pairs={{0,8},{1,9},{2,10},{3,11},{4,12},{5,13},{6,14},{7,15},{8,0},{9,1},... | collective-permute-start | bytes 995336 | tf_op jit(solution)/shard_map/ppermute | solution.py:18
  1032.8 56.2 %collective-permute-start.106 = (bf16[192,5760]{1,0:T(8,128)(2,1)}, bf16[192,5760]{1,0:T(8,128)(2,1)}, u32[]{:S(2)}, u32[]{:S(2)}) collective-permute-start(bf16[192,5760]{1,0:T(8,128)(2,1)} %get-tuple-element.446), channel_id=1, source_target_pairs={{0,2},{1,3},{2,0},{3,1},{4,6},{5,7},{6,4},{7,5},{8,10},{9,11},{10,... | collective-permute-start | bytes 6635528 | tf_op jit(solution)/shard_map/ppermute | solution.py:18
  1037.3 51.7 %collective-permute-start.107 = (bf16[128,5760]{1,0:T(8,128)(2,1)}, bf16[128,5760]{1,0:T(8,128)(2,1)}, u32[]{:S(2)}, u32[]{:S(2)}) collective-permute-start(bf16[128,5760]{1,0:T(8,128)(2,1)} %get-tuple-element.447), channel_id=1, source_target_pairs={{0,16},{16,0},{1,17},{17,1},{2,18},{18,2},{3,19},{19,3},{4,20},{20... | collective-permute-start | bytes 4423688 | tf_op jit(solution)/shard_map/ppermute | solution.py:18
  1038.5 50.5 %collective-permute-start.108 = (bf16[40,3456]{1,0:T(8,128)(2,1)}, bf16[40,3456]{1,0:T(8,128)(2,1)}, u32[]{:S(2)}, u32[]{:S(2)}) collective-permute-start(bf16[40,3456]{1,0:T(8,128)(2,1)} %pad_maximum_fusion.38), channel_id=1, source_target_pairs={{0,8},{1,9},{2,10},{3,11},{4,12},{5,13},{6,14},{7,15},{8,0},{9,1},... | collective-permute-start | bytes 829448 | tf_op jit(solution)/shard_map/ppermute | solution.py:18
  1100.7 46.1 %collective-permute-start.110 = (bf16[96,5760]{1,0:T(8,128)(2,1)}, bf16[96,5760]{1,0:T(8,128)(2,1)}, u32[]{:S(2)}, u32[]{:S(2)}) collective-permute-start(bf16[96,5760]{1,0:T(8,128)(2,1)} %get-tuple-element.591), channel_id=1, source_target_pairs={{0,16},{16,0},{1,17},{17,1},{2,18},{18,2},{3,19},{19,3},{4,20},{20... | collective-permute-start | bytes 3317768 | tf_op jit(solution)/shard_map/ppermute | solution.py:18
  1105.2 46.3 %collective-permute-start.112 = (bf16[192,3456]{1,0:T(8,128)(2,1)}, bf16[192,3456]{1,0:T(8,128)(2,1)}, u32[]{:S(2)}, u32[]{:S(2)}) collective-permute-start(bf16[192,3456]{1,0:T(8,128)(2,1)} %get-tuple-element.460), channel_id=1, source_target_pairs={{0,2},{1,3},{2,0},{3,1},{4,6},{5,7},{6,4},{7,5},{8,10},{9,11},{10,... | collective-permute-start | bytes 3981320 | tf_op jit(solution)/shard_map/ppermute | solution.py:18
  (259 other events, 4350.5 us)
Sparse Core Ops, SparseCore 0:
  825.6 67.7 all-gather.2
  1163.0 74.0 all-gather.4
